TPU v7x, 32 devices: a whole 2x2x4 slice. The times are simulated.
32 devices in a mesh: dp: 4 (over z), mp: 8 (over y, x, core).
Axes of the slice: x: 2, y: 2, z: 4, core: 2. Of those that a mesh axis runs over, the one named last changes fastest.
Arguments:
- tokens: bfloat16 [8192, 2048], P(('dp', 'mp')), may hold values from -6 to 6
- segment: int32 [8192], P('dp'), may hold values from 0 to 2, as said below
- valid: int32 [8192], replicated, may hold values from 0 to 1
- gain_attn: float32 [2048], replicated, may hold values from 0.5 to 1.5
- w_query: bfloat16 [2048, 2048], P(None, 'mp'), may hold values from -0.125 to 0.125
- w_key: bfloat16 [2048, 2048], P(None, 'mp'), may hold values from -0.125 to 0.125
- w_value: bfloat16 [2048, 2048], P(None, 'mp'), may hold values from -0.125 to 0.125
- w_out: bfloat16 [2048, 2048], P('mp'), may hold values from -3 to 3
- gain_mlp: float32 [2048], replicated, may hold values from 0.5 to 1.5
- w_up: bfloat16 [2048, 8192], P(None, 'mp'), may hold values from -0.125 to 0.125
- w_down: bfloat16 [8192, 2048], P('mp'), may hold values from -0.0625 to 0.0625
- grad_out: bfloat16 [8192, 2048], P(('dp', 'mp')), may hold values from -6 to 6
Outputs:
- out_tokens: bfloat16 [8192, 2048], P(('dp', 'mp'))
- grad_tokens: bfloat16 [8192, 2048], P(('dp', 'mp'))
- grad_gain_attn: float32 [2048], P(('dp', 'mp'))
- grad_query: float32 [2048, 2048], P('dp', 'mp')
- grad_key: float32 [2048, 2048], P('dp', 'mp')
- grad_value: float32 [2048, 2048], P('dp', 'mp')
- grad_out_proj: float32 [2048, 2048], P('mp', 'dp')
- grad_gain_mlp: float32 [2048], P(('dp', 'mp'))
- grad_up: float32 [2048, 8192], P('dp', 'mp')
- grad_down: float32 [8192, 2048], P('mp', 'dp')
- rms_stream: float32 [], replicated
- rms_attn: float32 [], replicated
- rms_mlp: float32 [], replicated
Inputs may be any that keep to these rules, and one draw needn't show every extreme that they name: `segment`: within each slot the clip numbers never fall; clip 1 starts before position 128 of the slot and clip 2 starts at or after position 1921.
All inputs are finite; a program needn't handle non-finite values.
Results may differ from a plain program's by a relative error of at most 0.022.
Values may be sent and summed in bfloat16 or wider, within the bound.
A program may use at most 512 MiB of HBM per device.

v0:
```python
import jax
import jax.numpy as jnp
from jax import lax
from jax.sharding import PartitionSpec as P

D = 2048
HD = 128


EPSILON = 1e-05
NEGATIVE = -1e30


def norm_rows(values, norm_gain):
    scale = lax.rsqrt(jnp.mean(values * values, axis=-1, keepdims=True) + EPSILON)
    return values * scale * norm_gain


def norm_back(values, norm_gain, grad_norm):
    scale = lax.rsqrt(jnp.mean(values * values, axis=-1, keepdims=True) + EPSILON)
    normal = values * scale
    grad_hat = grad_norm * norm_gain
    inner = jnp.mean(grad_hat * normal, axis=-1, keepdims=True)
    return (scale * (grad_hat - normal * inner), normal)


def gelu_fn(values):
    return jax.nn.gelu(values, approximate=True)


def contract_rows(left_side, right_side):
    return lax.dot_general(
        left_side, right_side, (((0,), (0,)), ((), ())), preferred_element_type=jnp.float32
    )


def contract_cols(left_side, right_side):
    return lax.dot_general(
        left_side, right_side, (((1,), (1,)), ((), ())), preferred_element_type=jnp.float32
    )


def block_mask(first_row, row_count, segment_rows, valid_rows):
    rows_here = first_row + jnp.arange(row_count, dtype=jnp.int32)
    columns = jnp.arange(segment_rows.shape[0], dtype=jnp.int32)
    segment_here = lax.dynamic_slice_in_dim(segment_rows, first_row, row_count)
    same_clip = segment_here[:, None] == segment_rows[None, :]
    earlier = (columns[None, :] < rows_here[:, None]) & (valid_rows[None, :] > 0)
    itself = columns[None, :] == rows_here[:, None]
    return same_clip & (earlier | itself)


def attend_forward(queries, keys_all, values_all, segment_rows, valid_rows, head_count):
    seq_rows = queries.shape[0]
    block_rows = min(512, seq_rows)
    key_heads = keys_all.reshape(seq_rows, head_count, HD)
    value_heads = values_all.reshape(seq_rows, head_count, HD)

    def one_block(first_row):
        query_block = lax.dynamic_slice_in_dim(queries, first_row, block_rows, 0).reshape(
            block_rows, head_count, HD
        )
        scores = jnp.einsum(
            "qhd,khd->hqk", query_block, key_heads, preferred_element_type=jnp.float32
        ) * HD ** (-0.5)
        allowed = block_mask(first_row, block_rows, segment_rows, valid_rows)
        scores = jnp.where(allowed[None], scores, NEGATIVE)
        largest = jnp.max(scores, axis=-1, keepdims=True)
        powers = jnp.exp(scores - largest)
        row_total = jnp.sum(powers, axis=-1, keepdims=True)
        attention = (powers / row_total).astype(jnp.bfloat16)
        blended = jnp.einsum(
            "hqk,khd->qhd", attention, value_heads, preferred_element_type=jnp.float32
        )
        return (
            blended.astype(jnp.bfloat16).reshape(block_rows, head_count * HD),
            (largest + jnp.log(row_total))[:, :, 0],
        )

    starts = jnp.arange(seq_rows // block_rows, dtype=jnp.int32) * block_rows
    blended, logsum = lax.map(one_block, starts)
    return (blended.reshape(seq_rows, head_count * HD), logsum)


def attend_backward(
    queries, keys_all, values_all, logsum, grad_mixed, segment_rows, valid_rows, head_count
):
    seq_rows = queries.shape[0]
    block_rows = min(512, seq_rows)
    scale = HD ** (-0.5)
    key_heads = keys_all.reshape(seq_rows, head_count, HD)
    value_heads = values_all.reshape(seq_rows, head_count, HD)

    def one_block(running, block_item):
        grad_keys, grad_values = running
        first_row, block_logsum = block_item
        query_block = lax.dynamic_slice_in_dim(queries, first_row, block_rows, 0).reshape(
            block_rows, head_count, HD
        )
        grad_block = lax.dynamic_slice_in_dim(grad_mixed, first_row, block_rows, 0).reshape(
            block_rows, head_count, HD
        )
        scores = (
            jnp.einsum("qhd,khd->hqk", query_block, key_heads, preferred_element_type=jnp.float32)
            * scale
        )
        allowed = block_mask(first_row, block_rows, segment_rows, valid_rows)
        scores = jnp.where(allowed[None], scores, NEGATIVE)
        attention = jnp.exp(scores - block_logsum[:, :, None])
        grad_attention = jnp.einsum(
            "qhd,khd->hqk", grad_block, value_heads, preferred_element_type=jnp.float32
        )
        inner = jnp.sum(grad_attention * attention, axis=-1, keepdims=True)
        grad_scores = (attention * (grad_attention - inner)).astype(jnp.bfloat16)
        grad_query_block = (
            jnp.einsum("hqk,khd->qhd", grad_scores, key_heads, preferred_element_type=jnp.float32)
            * scale
        )
        grad_keys = (
            grad_keys
            + jnp.einsum(
                "hqk,qhd->khd", grad_scores, query_block, preferred_element_type=jnp.float32
            )
            * scale
        )
        grad_values = grad_values + jnp.einsum(
            "hqk,qhd->khd",
            attention.astype(jnp.bfloat16),
            grad_block,
            preferred_element_type=jnp.float32,
        )
        return ((grad_keys, grad_values), grad_query_block.reshape(block_rows, head_count * HD))

    starts = jnp.arange(seq_rows // block_rows, dtype=jnp.int32) * block_rows
    zeros_heads = jnp.zeros((seq_rows, head_count, HD), jnp.float32)
    (grad_keys, grad_values), grad_queries = lax.scan(
        one_block, (zeros_heads, zeros_heads), (starts, logsum)
    )
    width = head_count * HD
    return (
        grad_queries.reshape(seq_rows, width).astype(jnp.bfloat16),
        grad_keys.reshape(seq_rows, width).astype(jnp.bfloat16),
        grad_values.reshape(seq_rows, width).astype(jnp.bfloat16),
    )


def on_device(
    tokens,
    segment,
    valid,
    gain_attn,
    w_query,
    w_key,
    w_value,
    w_out,
    gain_mlp,
    w_up,
    w_down,
    grad_out,
):
    own_rows = tokens.shape[0]
    seq_rows = segment.shape[0]
    head_count = w_query.shape[1] // HD
    dp_index = lax.axis_index("dp")
    mp_index = lax.axis_index("mp")
    own_first = mp_index * own_rows
    valid_group = lax.dynamic_slice_in_dim(valid, dp_index * seq_rows, seq_rows)
    valid_own = lax.dynamic_slice_in_dim(valid_group, own_first, own_rows)
    token_values = tokens.astype(jnp.float32)
    gathered = lax.all_gather(tokens, "mp", axis=0, tiled=True)
    normed_attn = norm_rows(gathered.astype(jnp.float32), gain_attn).astype(jnp.bfloat16)
    queries = jnp.dot(normed_attn, w_query, preferred_element_type=jnp.float32).astype(jnp.bfloat16)
    keys_all = jnp.dot(normed_attn, w_key, preferred_element_type=jnp.float32).astype(jnp.bfloat16)
    values_all = jnp.dot(normed_attn, w_value, preferred_element_type=jnp.float32).astype(
        jnp.bfloat16
    )
    mixed, logsum = attend_forward(queries, keys_all, values_all, segment, valid_group, head_count)
    attn_rows = lax.psum(
        jnp.dot(mixed, w_out, preferred_element_type=jnp.float32).astype(jnp.bfloat16), "mp"
    ).astype(jnp.float32)
    residual_rows = gathered.astype(jnp.float32) + attn_rows
    attn_own = lax.dynamic_slice_in_dim(attn_rows, own_first, own_rows, 0)
    residual_own = lax.dynamic_slice_in_dim(residual_rows, own_first, own_rows, 0)
    normed_mlp = norm_rows(residual_rows, gain_mlp).astype(jnp.bfloat16)
    hidden_pre = jnp.dot(normed_mlp, w_up, preferred_element_type=jnp.float32)
    hidden = gelu_fn(hidden_pre).astype(jnp.bfloat16)
    mlp_own = lax.psum_scatter(
        jnp.dot(hidden, w_down, preferred_element_type=jnp.float32).astype(jnp.bfloat16),
        "mp",
        scatter_dimension=0,
        tiled=True,
    ).astype(jnp.float32)
    stream_own = residual_own + mlp_own
    out_tokens = stream_own.astype(jnp.bfloat16)
    mask_own = valid_own.astype(jnp.float32)[:, None]
    squares = lax.psum(
        (
            jnp.sum(mask_own * stream_own * stream_own),
            jnp.sum(mask_own * attn_own * attn_own),
            jnp.sum(mask_own * mlp_own * mlp_own),
        ),
        ("dp", "mp"),
    )
    counted = jnp.maximum(jnp.sum(valid).astype(jnp.float32) * D, 1.0)
    grad_rows = lax.all_gather(grad_out, "mp", axis=0, tiled=True)
    grad_hidden = contract_cols(grad_rows, w_down)
    grad_down = contract_rows(hidden, grad_rows)
    grad_pre = jax.vjp(gelu_fn, hidden_pre)[1](grad_hidden)[0].astype(jnp.bfloat16)
    grad_up = contract_rows(normed_mlp, grad_pre)
    grad_normed = lax.psum(contract_cols(grad_pre, w_up).astype(jnp.bfloat16), "mp").astype(
        jnp.float32
    )
    grad_input_rows, normal_rows = norm_back(residual_rows, gain_mlp, grad_normed)
    grad_resid_rows = grad_rows.astype(jnp.float32) + grad_input_rows
    grad_resid_own = lax.dynamic_slice_in_dim(grad_resid_rows, own_first, own_rows, 0)
    gain_mlp_part = jnp.sum(
        lax.dynamic_slice_in_dim(grad_normed * normal_rows, own_first, own_rows, 0), axis=0
    )
    grad_branch = grad_resid_rows.astype(jnp.bfloat16)
    grad_out_proj = contract_rows(mixed, grad_branch)
    grad_mixed = contract_cols(grad_branch, w_out).astype(jnp.bfloat16)
    grad_queries, grad_keys, grad_values = attend_backward(
        queries, keys_all, values_all, logsum, grad_mixed, segment, valid_group, head_count
    )
    grad_query = contract_rows(normed_attn, grad_queries)
    grad_key = contract_rows(normed_attn, grad_keys)
    grad_value = contract_rows(normed_attn, grad_values)
    total_term = contract_cols(grad_queries, w_query)
    total_term = total_term + contract_cols(grad_keys, w_key)
    grad_normed_attn = lax.psum_scatter(
        (total_term + contract_cols(grad_values, w_value)).astype(jnp.bfloat16),
        "mp",
        scatter_dimension=0,
        tiled=True,
    ).astype(jnp.float32)
    grad_input_attn, normal_attn = norm_back(token_values, gain_attn, grad_normed_attn)
    grad_tokens = (grad_resid_own + grad_input_attn).astype(jnp.bfloat16)
    gain_attn_part = jnp.sum(grad_normed_attn * normal_attn, axis=0)
    gain_grads = (
        lax.psum_scatter(gain_attn_part, ("dp", "mp"), scatter_dimension=0, tiled=True),
        lax.psum_scatter(gain_mlp_part, ("dp", "mp"), scatter_dimension=0, tiled=True),
    )
    inner_grads = (
        lax.psum_scatter(
            grad_query.astype(jnp.bfloat16), "dp", scatter_dimension=0, tiled=True
        ).astype(jnp.float32),
        lax.psum_scatter(
            grad_key.astype(jnp.bfloat16), "dp", scatter_dimension=0, tiled=True
        ).astype(jnp.float32),
        lax.psum_scatter(
            grad_value.astype(jnp.bfloat16), "dp", scatter_dimension=0, tiled=True
        ).astype(jnp.float32),
        lax.psum_scatter(
            grad_up.astype(jnp.bfloat16), "dp", scatter_dimension=0, tiled=True
        ).astype(jnp.float32),
    )
    outer_grads = (
        lax.psum_scatter(
            grad_out_proj.astype(jnp.bfloat16), "dp", scatter_dimension=1, tiled=True
        ).astype(jnp.float32),
        lax.psum_scatter(
            grad_down.astype(jnp.bfloat16), "dp", scatter_dimension=1, tiled=True
        ).astype(jnp.float32),
    )
    return (
        out_tokens,
        grad_tokens,
        gain_grads[0],
        inner_grads[0],
        inner_grads[1],
        inner_grads[2],
        outer_grads[0],
        gain_grads[1],
        inner_grads[3],
        outer_grads[1],
        jnp.sqrt(squares[0] / counted),
        jnp.sqrt(squares[1] / counted),
        jnp.sqrt(squares[2] / counted),
    )


def solution(mesh):
    placed = (
        P(("dp", "mp"), None),
        P("dp"),
        P(),
        P(),
        P(None, "mp"),
        P(None, "mp"),
        P(None, "mp"),
        P("mp", None),
        P(),
        P(None, "mp"),
        P("mp", None),
        P(("dp", "mp"), None),
    )
    return jax.shard_map(
        on_device,
        mesh=mesh,
        in_specs=placed,
        out_specs=(
            P(("dp", "mp"), None),
            P(("dp", "mp"), None),
            P(("dp", "mp")),
            P("dp", "mp"),
            P("dp", "mp"),
            P("dp", "mp"),
            P("mp", "dp"),
            P(("dp", "mp")),
            P("dp", "mp"),
            P("mp", "dp"),
            P(),
            P(),
            P(),
        ),
        check_vma=False,
    )
```

profile of v0, /device:TPU:0, one launch (start us, length us, event | category | flops | bytes accessed | tf_op | source)
XLA Modules:
  0.0 1086.3 jit_solution(5463557942506468040)
XLA Ops:
  8.8 58.3 %all-gather.3.cloned.1.call-done = bf16[2048,2048]{1,0:T(8,128)(2,1)} async-done(((bf16[256,2048]{1,0:T(8,128)(2,1)}), bf16[2048,2048]{1,0:T(8,128)(2,1)}) %all-gather.3.cloned.1.call-update) | async-done | bytes 8388624 | tf_op jit(solution)/shard_map/all_gather | solution.py:170
  67.1 5.1 fusion.26
  72.2 8.7 fusion.28
  80.9 6.9 convolution_convert_fusion.8
  92.0 6.7 convolution_convert_fusion.10
  100.2 67.6 %while.27 = (s32[]{:T(128)}, bf16[4,512,256]{2,1,0:T(8,128)(2,1)}, f32[4,2,512]{2,1,0:T(2,128)S(1)}, s32[4]{0:T(128)S(1)}, s32[2048]{0:T(1024)S(1)}, /*index=5*/...) while((s32[]{:T(128)}, bf16[4,512,256]{2,1,0:T(8,128)(2,1)}, ...), condition=%wide.region_4.5_spmd, body=%wide.region_1.4_spmd.sunk | while | flops 1105331712 | bytes 37812440 | solution.py:81
  103.6 3.7 fusion.131
  120.5 3.7 fusion.131
  137.4 3.7 fusion.131
  154.3 3.7 fusion.131
  167.8 7.2 convolution_convert_fusion.2
  175.1 14.7 %fusion.62 = f32[2048,1024]{1,0:T(8,128)} fusion(bf16[2048,2048]{1,0:T(8,128)(2,1)} %all-gather.5.cloned.1.call-done, bf16[1024,2048]{1,0:T(8,128)(2,1)} %param.26), kind=kOutput, calls=%fused_computation.115 | convolution fusion | flops 8589934592 | bytes 20971520 | tf_op jit(solution)/shard_map/dot_general | solution.py:38
  189.8 112.3 %all-reduce.6.cloned.1.call-done = bf16[2048,2048]{1,0:T(8,128)(2,1)} async-done(((bf16[2048,2048]{1,0:T(8,128)(2,1)}), bf16[2048,2048]{1,0:T(8,128)(2,1)}) %all-reduce.6.cloned.1.call-update) | async-done | bytes 8388624 | tf_op jit(solution)/shard_map/psum | solution.py:178
  302.0 13.7 %convert_add_fusion = (f32[2048,2048]{1,0:T(8,128)}, f32[2048]{0:T(1024)S(1)}) fusion(bf16[2048,2048]{1,0:T(8,128)(2,1)} %all-gather.3.cloned.1.call-done, bf16[2048,2048]{1,0:T(8,128)(2,1)} %all-reduce.6.cloned.1.call-done), kind=kLoop, calls=%fused_computation.44 | loop fusion | flops 20969472 | bytes 33562624 | tf_op jit(solution)/shard_map/add | solution.py:181
  315.7 10.7 broadcast_multiply_fusion
  326.4 20.0 %fusion.35 = (bf16[2048,1024]{1,0:T(8,128)(2,1)S(1)}, f32[2048,1024]{1,0:T(8,128)}) fusion(f32[2048,1024]{1,0:T(8,128)} %fusion.62, bf16[2048,1024]{1,0:T(8,128)(2,1)S(1)} %copy-done.27, f32[2048,2048]{1,0:T(8,128)} %broadcast_multiply_fusion, f32[2048]{0:T(1024)S(1)} %copy-done.25), kind=kOutput, calls=%fused_computation.63 | convolution fusion | flops 8640266240 | bytes 41951232 | tf_op jit(solution)/shard_map/dot_general | solution.py:185
  348.4 11.1 %convolution_convert_fusion = bf16[2048,2048]{1,0:T(8,128)(2,1)} fusion(bf16[2048,1024]{1,0:T(8,128)(2,1)S(1)} %get-tuple-element.291, bf16[2048,1024]{1,0:T(8,128)(2,1)S(1)} %copy-done.27), kind=kOutput, calls=%fused_computation.66 | convolution fusion | flops 8594128896 | bytes 16777216 | tf_op jit(solution)/shard_map/dot_general | solution.py:38
  361.8 124.6 %all-reduce.8.cloned.1.call-done = bf16[2048,2048]{1,0:T(8,128)(2,1)} async-done(((bf16[2048,2048]{1,0:T(8,128)(2,1)}), bf16[2048,2048]{1,0:T(8,128)(2,1)}) %all-reduce.8.cloned.1.call-update) | async-done | bytes 8388624 | tf_op jit(solution)/shard_map/psum | solution.py:210
  486.4 9.2 multiply_reduce_fusion.1
  495.7 12.6 %multiply_add_fusion = f32[2048,2048]{1,0:T(8,128)S(1)} fusion(f32[2048,2048]{1,0:T(8,128)} %broadcast_multiply_fusion, bf16[2048,2048]{1,0:T(8,128)(2,1)} %all-gather.5.cloned.1.call-done, f32[2048]{0:T(1024)S(1)} %broadcast_multiply_fusion.1, bf16[2048,2048]{1,0:T(8,128)(2,1)} %all-reduce.8.cloned.1.call-done, f32[2048]{0:T(1024)S(1)} %copy-done.25, ...), kind=kLoop, calls=%fused_computation.51 | loop fusion | flops 29360128 | bytes 50356224 | tf_op jit(solution)/shard_map/add | solution.py:214
  508.3 5.7 copy-done.2
  517.3 9.1 fusion.43
  526.5 100.6 %while.28 = (s32[]{:T(128)}, f32[2048,2,128]{0,2,1:T(8,128)S(1)}, f32[2048,2,128]{0,2,1:T(8,128)}, bf16[4,512,256]{2,1,0:T(8,128)(2,1)}, s32[4]{0:T(128)S(1)}, /...) while((s32[]{:T(128)}, f32[2048,2,128]{0,2,1:T(8,128)S(1)}, ...), condition=%wide.region_13.14_spmd.clone, body=%wide.region_11.13_spmd.clone.sunk | while | flops 2724988416 | bytes 107800928 | solution.py:136
  532.6 3.7 fusion.146
  541.8 3.9 multiply_reduce_fusion.4
  557.7 3.7 fusion.146
  566.8 3.9 multiply_reduce_fusion.4
  582.7 3.7 fusion.146
  591.9 3.9 multiply_reduce_fusion.4
  607.7 3.7 fusion.146
  616.9 3.9 multiply_reduce_fusion.4
  627.1 7.1 convolution_convert_fusion.7
  634.4 6.9 convolution_convert_fusion.6
  643.2 6.9 convolution_convert_fusion.5
  650.1 15.4 %convolution_convert_fusion.4 = bf16[2048,1024]{1,0:T(8,128)(2,1)} fusion(bf16[2048,1024]{1,0:T(8,128)(2,1)} %copy-done.28, f32[2048,2048]{1,0:T(8,128)} %broadcast_multiply_fusion, f32[2048]{0:T(1024)S(1)} %copy-done.26), kind=kOutput, calls=%fused_computation.74 | convolution fusion | flops 8600420352 | bytes 25174016 | tf_op jit(solution)/shard_map/dot_general | solution.py:32
  665.6 16.3 %convolution_convert_fusion.3 = bf16[1024,2048]{1,0:T(8,128)(2,1)} fusion(bf16[2048,2048]{1,0:T(8,128)(2,1)} %all-gather.5.cloned.1.call-done, f32[2048,1024]{1,0:T(8,128)} %get-tuple-element.292), kind=kOutput, calls=%fused_computation.73 | convolution fusion | flops 8610906112 | bytes 20971520 | tf_op jit(solution)/shard_map/dot_general | solution.py:32
  681.9 15.5 %convolution_convert_fusion.1 = bf16[2048,2048]{1,0:T(8,128)(2,1)} fusion(bf16[1024,2048]{1,0:T(8,128)(2,1)} %param.26, f32[2048,1024]{1,0:T(8,128)} %get-tuple-element.292), kind=kOutput, calls=%fused_computation.67 | convolution fusion | flops 8613003264 | bytes 20971520 | tf_op jit(solution)/shard_map/dot_general | solution.py:188
  698.7 8.2 fusion.64
  706.9 8.1 fusion.63
  715.0 16.6 %add_convert_fusion = bf16[2048,2048]{1,0:T(8,128)(2,1)} fusion(f32[2048,2048]{1,0:T(8,128)} %fusion.63, f32[2048,2048]{1,0:T(8,128)} %fusion.64, bf16[2048,256]{0,1:T(8,128)(2,1)S(1)} %bitcast.131, bf16[2048,256]{1,0:T(8,128)(2,1)S(1)} %copy-done.19), kind=kOutput, calls=%fused_computation.50 | convolution fusion | flops 2160066560 | bytes 44040192 | tf_op jit(solution)/shard_map/dot_general | solution.py:38
  734.0 11.3 %convert_element_type.148 = f32[2048,2048]{1,0:T(8,128)} convert(bf16[2048,2048]{1,0:T(8,128)(2,1)} %all-reduce.6.cloned.1.call-done) | non-fusion elementwise | flops 4194304 | bytes 25165824 | tf_op jit(solution)/shard_map/convert_element_type | solution.py:180
  745.3 11.4 %convert_element_type.157 = f32[2048,2048]{1,0:T(8,128)} convert(bf16[2048,2048]{1,0:T(8,128)(2,1)} %all-reduce.8.cloned.1.call-done) | non-fusion elementwise | flops 4194304 | bytes 25165824 | tf_op jit(solution)/shard_map/convert_element_type | solution.py:210
  766.3 30.6 %reduce-scatter.21.cloned.1.call-done = bf16[512,1024]{1,0:T(8,128)(2,1)} async-done(((bf16[2048,1024]{1,0:T(8,128)(2,1)}), bf16[512,1024]{1,0:T(8,128)(2,1)}) %reduce-scatter.21.cloned.1.call-update) | async-done | bytes 1048592 | tf_op jit(solution)/shard_map/reduce_scatter | solution.py:253
  799.9 76.7 %reduce-scatter.23.cloned.1.call-done = bf16[1024,512]{1,0:T(8,128)(2,1)} async-done(((bf16[1024,2048]{1,0:T(8,128)(2,1)}), bf16[1024,512]{1,0:T(8,128)(2,1)}) %reduce-scatter.23.cloned.1.call-update) | async-done | bytes 1048592 | tf_op jit(solution)/shard_map/reduce_scatter | solution.py:261
  879.3 72.4 %reduce-scatter.9.cloned.1.call-done = bf16[256,2048]{1,0:T(8,128)(2,1)} async-done(((bf16[2048,2048]{1,0:T(8,128)(2,1)}), bf16[256,2048]{1,0:T(8,128)(2,1)}) %reduce-scatter.9.cloned.1.call-update) | async-done | bytes 1048592 | tf_op jit(solution)/shard_map/reduce_scatter | solution.py:187
  951.8 5.0 fusion.58
  956.7 70.1 %reduce-scatter.11.cloned.1.call-done = bf16[256,2048]{1,0:T(8,128)(2,1)} async-done(((bf16[2048,2048]{1,0:T(8,128)(2,1)}), bf16[256,2048]{1,0:T(8,128)(2,1)}) %reduce-scatter.11.cloned.1.call-update) | async-done | bytes 1048592 | tf_op jit(solution)/shard_map/reduce_scatter | solution.py:230
  1028.9 39.9 %all-reduce.2 = (f32[2048]{0:T(1024)S(1)}, f32[2048]{0:T(1024)S(1)}, f32[]{:T(128)}, f32[]{:T(128)}, f32[]{:T(128)}) all-reduce(f32[2048]{0:T(1024)S(1)} %get-tuple-element.232, f32[2048]{0:T(1024)S(1)} %fusion.59, f32[]{:T(128)} %get-tuple-element.235, f32[]{:T(128)} %get-tuple-element.236, ...), channel_id=4, replica_groups=mesh['dp'=4,'mp'=8] {'dp','mp'}, use_global_device_ids=true, to_apply=%region_17.18.clone | all-reduce | flops 4099 | bytes 32792
  (254 shorter events, 147.9 us)
Async XLA Ops:
  7.2 160.6 %copy-start = (bf16[256,2048]{1,0:T(8,128)(2,1)S(1)}, bf16[256,2048]{1,0:T(8,128)(2,1)}, u32[]{:S(2)}) copy-start(bf16[256,2048]{1,0:T(8,128)(2,1)} %param.23) | copy-start | bytes 3145732
  7.2 65.0 %copy-start.23 = (f32[2048]{0:T(1024)S(1)}, f32[2048]{0:T(1024)}, u32[]{:S(2)}) copy-start(f32[2048]{0:T(1024)} %param.19) | copy-start | bytes 24580
  7.2 59.8 %all-gather.3.cloned.1.call-start = ((), (), s32[]{:S(2)}) async-start(), calls=%async_computation.8 | async-start | bytes 9437184 | tf_op jit(solution)/shard_map/all_gather | solution.py:170
  7.9 167.2 %all-gather.5.cloned.1.call-start = ((), (), s32[]{:S(2)}) async-start(), calls=%async_computation.11 | async-start | bytes 9437184 | tf_op jit(solution)/shard_map/all_gather | solution.py:205
  8.7 293.3 %all-reduce.6.cloned.1.call-start = ((), (), s32[]{:S(2)}) async-start(), calls=%async_computation.9 | async-start | bytes 16777216 | tf_op jit(solution)/shard_map/psum | solution.py:178
  72.2 8.7 copy-start.18
  80.9 6.9 copy-start.9
  80.9 6.9 copy-start.14
  87.8 4.2 copy-start.16
  90.2 8.5 copy-start.4
  92.0 8.2 copy-start.13
  92.0 8.2 dynamic-slice-start
  107.4 6.1 copy-start.21
  124.3 6.1 copy-start.21
  141.2 6.1 copy-start.21
  158.0 6.1 copy-start.21
  167.8 7.3 copy-start.8
  175.0 311.4 %all-reduce.8.cloned.1.call-start = ((), (), s32[]{:S(2)}) async-start(), calls=%async_computation.12 | async-start | bytes 16777216 | tf_op jit(solution)/shard_map/psum | solution.py:210
  302.0 13.7 %copy-start.3 = (bf16[2048,2048]{1,0:T(8,128)(2,1)S(1)}, bf16[2048,2048]{1,0:T(8,128)(2,1)}, u32[]{:S(2)}) copy-start(bf16[2048,2048]{1,0:T(8,128)(2,1)} %all-reduce.6.cloned.1.call-done) | copy-start | bytes 25165828
  315.7 10.7 copy-start.25
  315.7 10.7 copy-start.27
  359.5 399.7 %reduce-scatter.19.cloned.1.call-start = ((), (), s32[]{:S(2)}) async-start(), calls=%async_computation.17 | async-start | bytes 1310720 | tf_op jit(solution)/shard_map/reduce_scatter | solution.py:258
  495.7 18.3 %copy-start.10 = (bf16[4,512,256]{2,1,0:T(8,128)(2,1)S(1)}, bf16[4,512,256]{2,1,0:T(8,128)(2,1)}, u32[]{:S(2)}) copy-start(bf16[4,512,256]{2,1,0:T(8,128)(2,1)} %get-tuple-element.125) | copy-start | bytes 3145732
  508.3 5.7 copy-start.2
  526.4 234.6 %reduce-scatter.13.cloned.1.call-start = ((), (), s32[]{:S(2)}) async-start(), calls=%async_computation.14 | async-start | bytes 1310720 | tf_op jit(solution)/shard_map/reduce_scatter | solution.py:244
  531.4 7.5 copy-start.11
  538.9 2.9 copy-start.6
  541.8 3.9 copy-start.12
  556.4 7.5 copy-start.11
  563.9 2.9 copy-start.6
  566.8 3.9 copy-start.12
  581.4 7.5 copy-start.11
  588.9 2.9 copy-start.6
  591.9 3.9 copy-start.12
  606.4 7.5 copy-start.11
  616.8 3.9 copy-start.12
  634.2 128.6 %reduce-scatter.15.cloned.1.call-start = ((), (), s32[]{:S(2)}) async-start(), calls=%async_computation.15 | async-start | bytes 1310720 | tf_op jit(solution)/shard_map/reduce_scatter | solution.py:247
  641.4 123.2 %reduce-scatter.17.cloned.1.call-start = ((), (), s32[]{:S(2)}) async-start(), calls=%async_computation.16 | async-start | bytes 1310720 | tf_op jit(solution)/shard_map/reduce_scatter | solution.py:250
  643.1 7.0 copy-start.26
  650.1 146.9 %reduce-scatter.21.cloned.1.call-start = ((), (), s32[]{:S(2)}) async-start(), calls=%async_computation.18 | async-start | bytes 5242880 | tf_op jit(solution)/shard_map/reduce_scatter | solution.py:253
  665.5 211.0 %reduce-scatter.23.cloned.1.call-start = ((), (), s32[]{:S(2)}) async-start(), calls=%async_computation.19 | async-start | bytes 5242880 | tf_op jit(solution)/shard_map/reduce_scatter | solution.py:261
  681.9 269.9 %reduce-scatter.9.cloned.1.call-start = ((), (), s32[]{:S(2)}) async-start(), calls=%async_computation.10 | async-start | bytes 9437184 | tf_op jit(solution)/shard_map/reduce_scatter | solution.py:187
  697.4 329.4 %reduce-scatter.11.cloned.1.call-start = ((), (), s32[]{:S(2)}) async-start(), calls=%async_computation.13 | async-start | bytes 9437184 | tf_op jit(solution)/shard_map/reduce_scatter | solution.py:230
  698.7 8.2 copy-start.17
  698.7 8.2 copy-start.20
  706.9 8.1 copy-start.19
  759.2 267.6 %copy-start.24 = (f32[2048]{0:T(1024)S(1)}, f32[2048]{0:T(1024)}, u32[]{:S(2)}) copy-start(f32[2048]{0:T(1024)} %param.19) | copy-start | bytes 24580
  797.0 278.6 %copy-start.1 = (bf16[256,2048]{1,0:T(8,128)(2,1)S(1)}, bf16[256,2048]{1,0:T(8,128)(2,1)}, u32[]{:S(2)}) copy-start(bf16[256,2048]{1,0:T(8,128)(2,1)} %param.23) | copy-start | bytes 3145732
  (9 other events, 19.5 us)
Sparse Core Ops, SparseCore 0:
  9.9 57.0 all-gather.2
  68.9 54.3 all-gather.4
  175.1 126.8 all-reduce.5
  359.6 126.7 all-reduce.7
  526.6 27.3 reduce-scatter.18
  634.4 27.3 reduce-scatter.12
  664.6 25.7 reduce-scatter.14
  693.4 25.7 reduce-scatter.16
  721.5 75.4 reduce-scatter.20
  799.2 77.2 reduce-scatter.22
  880.0 71.7 reduce-scatter.8
  955.5 71.2 reduce-scatter.10
where the time goes:
time: 1090 us
  waiting for transfers between devices  547 us (50%)
  matrix products  255 us (23%)
  other arithmetic  167 us (15%)
  blocking collectives  39.9 us (4%)
  local copies, waits for them, and re-layouts  39 us (4%)
  between operations  21.2 us (2%)
  loops' own time  17 us (2%)
    psum x1, waiting for transfers between devices, on_device(): lax.psum(contract_cols(grad_pre, w_up).astype(jnp.bfloat16), 'mp')  125 us
    psum x1, waiting for transfers between devices, on_device(): lax.psum(jnp.dot(mixed, w_out, preferred_element_type=jnp.float32).astype...  112 us
    reduce_scatter x1, waiting for transfers between devices, on_device(): lax.psum_scatter(grad_down.astype(jnp.bfloat16), 'dp', scatter_dimension=...  76.7 us
    reduce_scatter x1, waiting for transfers between devices, on_device(): lax.psum_scatter(jnp.dot(hidden, w_down, preferred_element_type=jnp.float...  72.4 us
    reduce_scatter x1, waiting for transfers between devices, on_device(): lax.psum_scatter((total_term + contract_cols(grad_values, w_value)).astyp...  70.1 us
    dot_general x6, matrix products, contract_cols(): lax.dot_general(left_side, right_side, (((1,), (1,)), ((), ())), preferre...  67.7 us
    all_gather x1, waiting for transfers between devices, on_device(): gathered = lax.all_gather(tokens, 'mp', axis=0, tiled=True)  58.3 us
    dot_general x6, matrix products, contract_rows(): lax.dot_general(left_side, right_side, (((0,), (0,)), ((), ())), preferre...  55.9 us
  transfers between devices with their start and end apart: 12, of which 7 were waited for; matrix products, arithmetic and copies ran while one was open for 33% of the time, Pallas kernels for 0%

commit v1 on v0

v1 whole, which is shorter than its diff:
```python
import functools
import jax, jax.numpy as jnp
from jax import lax
from jax.experimental import pallas as pl
from jax.experimental.pallas import tpu as pltpu
HD=128
NEGATIVE=-1e30
LOG2E=1.4426950408889634

def attn_fwd_body(blk, nb, order_ref, q_ref, k_ref, v_ref, rk_ref, ck_ref, mix_ref, lse_ref, ks, vs):
    c = HD ** -0.5 * LOG2E
    for a in range(nb):
        pos = pl.multiple_of(order_ref[a] * blk, blk)
        ks[a*blk:(a+1)*blk, :] = k_ref[pl.ds(pos, blk), :]
        vs[a*blk:(a+1)*blk, :] = v_ref[pl.ds(pos, blk), :]
    tri_r = lax.broadcasted_iota(jnp.int32, (blk, blk), 0)
    tri_c = lax.broadcasted_iota(jnp.int32, (blk, blk), 1)
    for a in range(nb):
        L = (a+1)*blk
        pos = pl.multiple_of(order_ref[a] * blk, blk)
        q = q_ref[pl.ds(pos, blk), :]
        s = lax.dot_general(q, ks[:L, :], (((1,), (1,)), ((), ())), preferred_element_type=jnp.float32)
        rk = rk_ref[a*blk:(a+1)*blk, :]
        ck = ck_ref[:, :L]
        ok = rk == ck
        sd = s[:, L-blk:]
        okd = ok[:, L-blk:]
        okd = (okd & (tri_c < tri_r)) | (tri_c == tri_r)
        sd = jnp.where(okd, sd, NEGATIVE)
        if a:
            so = jnp.where(ok[:, :L-blk], s[:, :L-blk], NEGATIVE)
            m = jnp.maximum(jnp.max(so, axis=1, keepdims=True), jnp.max(sd, axis=1, keepdims=True))
            po = jnp.exp2((so - m) * c)
            pd = jnp.exp2((sd - m) * c)
            l = jnp.sum(po, axis=1, keepdims=True) + jnp.sum(pd, axis=1, keepdims=True)
            o = jnp.dot(po.astype(jnp.bfloat16), vs[:L-blk, :], preferred_element_type=jnp.float32) + jnp.dot(pd.astype(jnp.bfloat16), vs[L-blk:L, :], preferred_element_type=jnp.float32)
        else:
            m = jnp.max(sd, axis=1, keepdims=True)
            pd = jnp.exp2((sd - m) * c)
            l = jnp.sum(pd, axis=1, keepdims=True)
            o = jnp.dot(pd.astype(jnp.bfloat16), vs[L-blk:L, :], preferred_element_type=jnp.float32)
        o = o / l
        mix_ref[pl.ds(pos, blk), :] = o.astype(jnp.bfloat16)
        lse_ref[0, a*blk:(a+1)*blk, :] = m * c + jnp.log2(l)

def attn_fwd(qkv, order, rowkey, colkey, heads, blk=256):
    S = qkv.shape[0]; nb = S // blk
    return pl.pallas_call(
        functools.partial(attn_fwd_body, blk, nb), name="attn_fwd",
        grid_spec=pltpu.PrefetchScalarGridSpec(num_scalar_prefetch=1, grid=(heads,),
            in_specs=[pl.BlockSpec((S, HD), lambda h, o: (0, h)),
                      pl.BlockSpec((S, HD), lambda h, o: (0, heads + h)),
                      pl.BlockSpec((S, HD), lambda h, o: (0, 2*heads + h)),
                      pl.BlockSpec((S, 1), lambda h, o: (0, 0)),
                      pl.BlockSpec((1, S), lambda h, o: (0, 0))],
            out_specs=[pl.BlockSpec((S, HD), lambda h, o: (0, h)),
                       pl.BlockSpec((1, S, 1), lambda h, o: (h, 0, 0))],
            scratch_shapes=[pltpu.VMEM((S, HD), jnp.bfloat16)]*2),
        out_shape=[jax.ShapeDtypeStruct((S, heads*HD), jnp.bfloat16), jax.ShapeDtypeStruct((heads, S, 1), jnp.float32)],
        compiler_params=pltpu.CompilerParams(vmem_limit_bytes=40*2**20),
        cost_estimate=pl.CostEstimate(flops=4*S*S*HD*heads//2, bytes_accessed=8*S*HD*heads, transcendentals=S*S*heads//2),
    )(order, qkv, qkv, qkv, rowkey, colkey)

def attn_bwd_body(blk, nb, order_ref, q_ref, k_ref, v_ref, do_ref, mix_ref, lse_ref, rk_ref, ck_ref, dq_ref, dk_ref, dv_ref, ks, vs, dks, dvs):
    scale = HD ** -0.5
    c = scale * LOG2E
    for a in range(nb):
        pos = pl.multiple_of(order_ref[a] * blk, blk)
        ks[a*blk:(a+1)*blk, :] = k_ref[pl.ds(pos, blk), :]
        vs[a*blk:(a+1)*blk, :] = v_ref[pl.ds(pos, blk), :]
    tri_r = lax.broadcasted_iota(jnp.int32, (blk, blk), 0)
    tri_c = lax.broadcasted_iota(jnp.int32, (blk, blk), 1)
    nt = (((1,), (1,)), ((), ()))
    tn = (((0,), (0,)), ((), ()))
    f32 = jnp.float32
    for a in reversed(range(nb)):
        L = (a+1)*blk; Lo = L - blk
        pos = pl.multiple_of(order_ref[a] * blk, blk)
        q = q_ref[pl.ds(pos, blk), :]
        do = do_ref[pl.ds(pos, blk), :]
        delta = jnp.sum(do.astype(f32) * mix_ref[pl.ds(pos, blk), :].astype(f32), axis=1, keepdims=True)
        s = lax.dot_general(q, ks[:L, :], nt, preferred_element_type=f32)
        dp = lax.dot_general(do, vs[:L, :], nt, preferred_element_type=f32)
        rk = rk_ref[a*blk:(a+1)*blk, :]
        ck = ck_ref[:, :L]
        ok = rk == ck
        lse = lse_ref[0, a*blk:(a+1)*blk, :]
        okd = (ok[:, Lo:] & (tri_c < tri_r)) | (tri_c == tri_r)
        p = jnp.exp2(s * c - lse)
        pd = jnp.where(okd, p[:, Lo:], 0.0)
        dsd = (pd * (dp[:, Lo:] - delta)).astype(jnp.bfloat16)
        pd = pd.astype(jnp.bfloat16)
        dq = jnp.dot(dsd, ks[Lo:L, :], preferred_element_type=f32)
        dkd = lax.dot_general(dsd, q, tn, preferred_element_type=f32)
        dvd = lax.dot_general(pd, do, tn, preferred_element_type=f32)
        if a == nb - 1:
            dks[Lo:L, :] = dkd
            dvs[Lo:L, :] = dvd
        else:
            dks[Lo:L, :] += dkd
            dvs[Lo:L, :] += dvd
        if a:
            po = jnp.where(ok[:, :Lo], p[:, :Lo], 0.0)
            dso = (po * (dp[:, :Lo] - delta)).astype(jnp.bfloat16)
            po = po.astype(jnp.bfloat16)
            dq += jnp.dot(dso, ks[:Lo, :], preferred_element_type=f32)
            dko = lax.dot_general(dso, q, tn, preferred_element_type=f32)
            dvo = lax.dot_general(po, do, tn, preferred_element_type=f32)
            if a == nb - 1:
                dks[:Lo, :] = dko
                dvs[:Lo, :] = dvo
            else:
                dks[:Lo, :] += dko
                dvs[:Lo, :] += dvo
        dq_ref[pl.ds(pos, blk), :] = (dq * scale).astype(jnp.bfloat16)
    for a in range(nb):
        pos = pl.multiple_of(order_ref[a] * blk, blk)
        dk_ref[pl.ds(pos, blk), :] = (dks[a*blk:(a+1)*blk, :] * scale).astype(jnp.bfloat16)
        dv_ref[pl.ds(pos, blk), :] = dvs[a*blk:(a+1)*blk, :].astype(jnp.bfloat16)

def attn_bwd(qkv, do, mixed, lse, order, rowkey, colkey, heads, blk=256):
    S = qkv.shape[0]; nb = S // blk
    bs = lambda off: pl.BlockSpec((S, HD), lambda h, o: (0, off*heads + h))
    return pl.pallas_call(
        functools.partial(attn_bwd_body, blk, nb), name="attn_bwd",
        grid_spec=pltpu.PrefetchScalarGridSpec(num_scalar_prefetch=1, grid=(heads,),
            in_specs=[bs(0), bs(1), bs(2), bs(0), bs(0),
                      pl.BlockSpec((1, S, 1), lambda h, o: (h, 0, 0)),
                      pl.BlockSpec((S, 1), lambda h, o: (0, 0)),
                      pl.BlockSpec((1, S), lambda h, o: (0, 0))],
            out_specs=[bs(0), bs(0), bs(0)],
            scratch_shapes=[pltpu.VMEM((S, HD), jnp.bfloat16)]*2 + [pltpu.VMEM((S, HD), jnp.float32)]*2),
        out_shape=[jax.ShapeDtypeStruct((S, heads*HD), jnp.bfloat16)]*3,
        compiler_params=pltpu.CompilerParams(vmem_limit_bytes=48*2**20),
        cost_estimate=pl.CostEstimate(flops=10*S*S*HD*heads//2, bytes_accessed=16*S*HD*heads, transcendentals=S*S*heads//2),
    )(order, qkv, qkv, qkv, do, mixed, lse, rowkey, colkey)

from jax.sharding import PartitionSpec as P

EPSILON = 1e-05
BF = jnp.bfloat16
F32 = jnp.float32


def row_scale(values):
    return lax.rsqrt(jnp.mean(values * values, axis=-1, keepdims=True) + EPSILON)


def norm_rows(values, norm_gain):
    return values * row_scale(values) * norm_gain


def norm_back(values, norm_gain, grad_norm):
    scale = row_scale(values)
    normal = values * scale
    grad_hat = grad_norm * norm_gain
    inner = jnp.mean(grad_hat * normal, axis=-1, keepdims=True)
    return scale * (grad_hat - normal * inner)


def gelu_fn(values):
    return jax.nn.gelu(values, approximate=True)


def dot_nn(a, b):
    return jnp.dot(a, b, preferred_element_type=F32)


def dot_tn(a, b):
    return lax.dot_general(a, b, (((0,), (0,)), ((), ())), preferred_element_type=F32)


def dot_nt(a, b):
    return lax.dot_general(a, b, (((1,), (1,)), ((), ())), preferred_element_type=F32)


def after(value, *others):
    return lax.optimization_barrier((value,) + others)[0]


def swap_bits(r):
    return (r & 1) | ((r & 2) << 1) | ((r & 4) >> 1)


class Cube:
    def __init__(self, me):
        self.me = me
        self.core = me % 2
        self.sib = [(i, i ^ 1) for i in range(8)]
        self.first = [(i, i ^ (2 if i % 2 else 4)) for i in range(8)]
        self.second = [(i, i ^ (4 if i % 2 else 2)) for i in range(8)]
        mask = jnp.bitwise_xor(jnp.arange(8, dtype=jnp.int32), me)
        swapped = (mask & 1) | ((mask & 2) << 1) | ((mask & 4) >> 1)
        self.order = jnp.where(self.core == 0, mask, swapped).astype(jnp.int32)

    def gather(self, own):
        half = own.shape[0] // 2
        send = lambda v, p: lax.ppermute(v, "mp", p)
        p4, p2, p1 = send(own, self.first), send(own, self.second), send(own, self.sib)
        p6 = jnp.concatenate([send(p2[:half], self.first), send(p4[half:], self.second)])
        p5, p3 = send(p2, self.sib), send(p4, self.sib)
        p7 = send(p6, self.sib)
        return [[own, p1], [p2, p3], [p4, p5], [p6, p7]]

    def scatter(self, product, width, chunks):
        half = width // 2
        step = half // chunks
        core = self.core
        send = lambda v, p: lax.ppermute(v, "mp", p)
        mine, other = [], []
        for j in range(chunks):
            away = product((1 - core) * half + j * step, step).astype(BF)
            came = send(away, self.sib)
            keep = product(core * half + j * step, step)
            rows = keep.shape[0] // 8
            cut = lambda v, a, b: v[a * rows:b * rows].astype(F32)
            came = jnp.concatenate([came[k * rows:(k + 1) * rows] for k in (1, 0, 5, 4, 3, 2, 7, 6)])
            one = send((cut(keep, 4, 8) + cut(came, 4, 8)).astype(BF), self.first)
            two = send((cut(keep, 2, 4) + cut(came, 2, 4) + cut(one, 2, 4)).astype(BF), self.second)
            total = cut(keep, 0, 2) + cut(came, 0, 2) + cut(one, 0, 2) + cut(two, 0, 2)
            mine.append(total[:rows])
            other.append(send(total[rows:].astype(BF), self.sib).astype(F32))
        mine, other = jnp.concatenate(mine, 1), jnp.concatenate(other, 1)
        low = jnp.where(core == 0, mine, other)
        high = jnp.where(core == 0, other, mine)
        return jnp.concatenate([low, high], 1)

    def total(self, vector):
        send = lambda v, axis, n, bit: lax.ppermute(v, axis, [(i, i ^ bit) for i in range(n)])
        for bit in (1, 2, 4):
            vector = vector + send(vector, "mp", 8, bit)
        n_dp = lax.axis_size("dp")
        bit = 1
        while bit < n_dp:
            vector = vector + send(vector, "dp", n_dp, bit)
            bit *= 2
        return vector


class Plain:
    def __init__(self, me, count):
        self.order = jnp.arange(count, dtype=jnp.int32)

    def gather(self, own):
        return [[lax.all_gather(own, "mp", axis=0, tiled=True)]]

    def scatter(self, product, width, chunks):
        return lax.psum_scatter(product(0, width).astype(BF), "mp", scatter_dimension=0, tiled=True).astype(F32)

    def total(self, vector):
        return lax.psum(vector, ("dp", "mp"))


def take(array, start, size, axis):
    if size == array.shape[axis]:
        return array
    return lax.dynamic_slice_in_dim(array, start, size, axis)


def stack(groups):
    flat = [block for group in groups for block in group]
    return jnp.concatenate(flat) if len(flat) > 1 else flat[0]


def joined(group):
    return jnp.concatenate(group) if len(group) > 1 else group[0]


def on_device(tokens, segment, valid, gain_attn, w_query, w_key, w_value, w_out, gain_mlp, w_up, w_down, grad_out):
    own_rows, width = tokens.shape
    seq_rows = segment.shape[0]
    heads = w_query.shape[1] // HD
    n_dp, n_mp = lax.axis_size("dp"), lax.axis_size("mp")
    dp, me = lax.axis_index("dp"), lax.axis_index("mp")
    net = Cube(me) if n_mp == 8 and n_dp & (n_dp - 1) == 0 else Plain(me, seq_rows // own_rows)
    chunks = 2
    valid_group = lax.dynamic_slice_in_dim(valid, dp * seq_rows, seq_rows)
    valid_own = lax.dynamic_slice_in_dim(valid_group, me * own_rows, own_rows)
    row_key = segment[:, None]
    col_key = jnp.where(valid_group > 0, segment, -1)[None, :]
    tokens32 = tokens.astype(F32)
    w_qkv = jnp.concatenate([w_query, w_key, w_value], 1)

    normed_groups = net.gather(norm_rows(tokens32, gain_attn).astype(BF))
    qkv = joined([dot_nn(joined(g), w_qkv).astype(BF) for g in normed_groups])
    normed = stack(normed_groups)

    mixed, lse = attn_fwd(qkv, net.order, row_key, col_key, heads, own_rows)
    grad_groups = net.gather(after(grad_out, qkv))
    attn_own = net.scatter(lambda a, n: dot_nn(mixed, take(w_out, a, n, 1)), width, chunks)
    residual = tokens32 + attn_own
    mlp_groups = net.gather(norm_rows(residual, gain_mlp).astype(BF))

    hidden, grad_pre = [], []
    for group, grads in zip(mlp_groups, grad_groups):
        pre = dot_nn(joined(group), w_up)
        grad_hidden = dot_nt(joined(grads), w_down)
        value, back = jax.vjp(gelu_fn, pre)
        hidden.append(value.astype(BF))
        grad_pre.append(back(grad_hidden)[0].astype(BF))
    hidden, grad_pre = joined(hidden), joined(grad_pre)
    normed_mlp, grad_rows = stack(mlp_groups), stack(grad_groups)

    grad_down = lax.psum_scatter(dot_tn(hidden, grad_rows).astype(BF), "dp", scatter_dimension=1, tiled=True).astype(F32)
    grad_normed = net.scatter(lambda a, n: dot_nt(grad_pre, take(w_up, a, n, 0)), width, chunks)
    part_up = dot_tn(normed_mlp, grad_pre)
    grad_up = lax.psum_scatter(part_up.astype(BF), "dp", scatter_dimension=0, tiled=True).astype(F32)
    gain_mlp_part = jnp.sum(part_up * w_up.astype(F32), axis=1) / gain_mlp

    grad_residual = grad_out.astype(F32) + norm_back(residual, gain_mlp, grad_normed)
    branch_groups = net.gather(grad_residual.astype(BF))
    grad_mixed = joined([dot_nt(joined(g), w_out).astype(BF) for g in branch_groups])
    grad_branch = stack(branch_groups)
    grad_out_proj = lax.psum_scatter(
        dot_tn(mixed, grad_branch).astype(BF), "dp", scatter_dimension=1, tiled=True
    ).astype(F32)
    late_hidden = after(hidden, grad_mixed)
    mlp_own = net.scatter(lambda a, n: dot_nn(late_hidden, take(w_down, a, n, 1)), width, chunks)
    stream = residual + mlp_own
    mask_own = valid_own.astype(F32)[:, None]

    grads_qkv = jnp.concatenate(
        attn_bwd(qkv, grad_mixed, mixed, lse, net.order, row_key, col_key, heads, own_rows), 1
    )
    part_qkv = dot_tn(normed, grads_qkv)
    grad_qkv = lax.psum_scatter(part_qkv.astype(BF), "dp", scatter_dimension=0, tiled=True).astype(F32)
    gain_attn_part = jnp.sum(part_qkv * w_qkv.astype(F32), axis=1) / gain_attn
    grad_normed_attn = net.scatter(lambda a, n: dot_nt(grads_qkv, take(w_qkv, a, n, 0)), width, chunks)
    grad_tokens = (grad_residual + norm_back(tokens32, gain_attn, grad_normed_attn)).astype(BF)

    squares = jnp.stack([jnp.sum(mask_own * part * part) for part in (stream, attn_own, mlp_own)])
    summed = net.total(jnp.concatenate([gain_attn_part, gain_mlp_part, squares]))
    counted = jnp.maximum(jnp.sum(valid).astype(F32) * width, 1.0)
    gain_rows = width // (n_dp * n_mp)
    place = (dp * n_mp + me) * gain_rows
    rms = jnp.sqrt(summed[2 * width:] / counted)
    shard = heads * HD
    return (
        stream.astype(BF),
        grad_tokens,
        lax.dynamic_slice_in_dim(summed[:width], place, gain_rows),
        grad_qkv[:, :shard],
        grad_qkv[:, shard:2 * shard],
        grad_qkv[:, 2 * shard:],
        grad_out_proj,
        lax.dynamic_slice_in_dim(summed[width:2 * width], place, gain_rows),
        grad_up,
        grad_down,
        rms[0],
        rms[1],
        rms[2],
    )


def solution(mesh):
    tokens_spec = P(("dp", "mp"), None)
    cols, rows = P(None, "mp"), P("mp", None)
    return jax.shard_map(
        on_device,
        mesh=mesh,
        in_specs=(tokens_spec, P("dp"), P(), P(), cols, cols, cols, rows, P(), cols, rows, tokens_spec),
        out_specs=(
            tokens_spec,
            tokens_spec,
            P(("dp", "mp")),
            P("dp", "mp"),
            P("dp", "mp"),
            P("dp", "mp"),
            P("mp", "dp"),
            P(("dp", "mp")),
            P("dp", "mp"),
            P("mp", "dp"),
            P(),
            P(),
            P(),
        ),
        check_vma=False,
    )
```

time: 1090 us -> 574 us (0.53)
  waiting for transfers between devices: 547 us -> 177 us
  other arithmetic: 167 us -> 45.6 us
  matrix products: 255 us -> 151 us
  starting transfers between devices: 0.49 us -> 53.5 us
  local copies, waits for them, and re-layouts: 39 us -> 87.9 us
  blocking collectives: 39.9 us -> 0 us
  Pallas kernels: 0 us -> 33 us
  loops' own time: 17 us -> 0 us
    reduce_scatter x8 -> x4, waiting for transfers between devices: 250 us -> 0.03 us  [the longest x1 0.02 us: on_device(): lax.psum_scatter(dot_tn(hidden, grad_rows).astype(BF), 'dp', scatter_dime...]
    psum x2 -> x0, waiting for transfers between devices: 237 us -> none  [the longest x1 125 us: on_device(): lax.psum(contract_cols(grad_pre, w_up).astype(jnp.bfloat16), 'mp')]
    ppermute x0 -> x69, waiting for transfers between devices: none -> 176 us  [the longest x32 102 us: scatter(): send = lambda v, p: lax.ppermute(v, 'mp', p)]
    dot_general x46 -> x36, matrix products: 255 us -> 151 us  [the longest x16 57.5 us: dot_nt(): lax.dot_general(a, b, (((1,), (1,)), ((), ())), preferred_element_type=F32)]
    all_gather x2 -> x0, waiting for transfers between devices: 58.3 us -> none  [the longest x1 58.3 us: on_device(): gathered = lax.all_gather(tokens, 'mp', axis=0, tiled=True)]
    unnamed x51 -> x197, local copies, waits for them, and re-layouts: 13.1 us -> 67.1 us
    ppermute x0 -> x69, starting transfers between devices: none -> 53 us  [the longest x32 25.4 us: gather(): send = lambda v, p: lax.ppermute(v, 'mp', p)]
    convert_element_type x17 -> x20, other arithmetic: 60.1 us -> 18.2 us  [the longest x8 4.78 us: scatter(): one = send((cut(keep, 4, 8) + cut(came, 4, 8)).astype(BF), self.first)]
  transfers between devices with their start and end apart: 12 -> 73, of which waited for: 7 -> 23; matrix products, arithmetic and copies ran while one was open for 33% -> 45% of each run, Pallas kernels for 0% -> 4%
where the time goes in v1:
time: 574 us; the launch traced here: 564 us
  waiting for transfers between devices  177 us (31%)
  matrix products  151 us (26%)
  local copies, waits for them, and re-layouts  87.9 us (15%)
  starting transfers between devices  53.5 us (9%)
  other arithmetic  45.6 us (8%)
  Pallas kernels  33 us (6%)
  between operations  16.4 us (3%)
    ppermute x32, waiting for transfers between devices, scatter(): send = lambda v, p: lax.ppermute(v, 'mp', p)  102 us
    ppermute x32, waiting for transfers between devices, gather(): send = lambda v, p: lax.ppermute(v, 'mp', p)  71.4 us
    unnamed x197, local copies, waits for them, and re-layouts  67.1 us
    dot_general x16, matrix products, dot_nt(): lax.dot_general(a, b, (((1,), (1,)), ((), ())), preferred_element_type=F32)  57.5 us
    dot_general x16, matrix products, dot_nn(): return jnp.dot(a, b, preferred_element_type=F32)  47.5 us
    dot_general x4, matrix products, dot_tn(): lax.dot_general(a, b, (((0,), (0,)), ((), ())), preferred_element_type=F32)  45.9 us
    ppermute x32, starting transfers between devices, gather(): send = lambda v, p: lax.ppermute(v, 'mp', p)  25.4 us
    pallas_call x1, Pallas kernels, attn_bwd(): pl.pallas_call(functools.partial(attn_bwd_body, blk, nb), name='attn_bwd'...  20.3 us
  transfers between devices with their start and end apart: 73, of which 23 were waited for; matrix products, arithmetic and copies ran while one was open for 45% of the time, Pallas kernels for 4%

profile of v1, /device:TPU:0, one launch (start us, length us, event | category | flops | bytes accessed | tf_op | source)
XLA Modules:
  0.0 563.8 jit_solution(9440752543353186455)
XLA Ops:
  10.9 3.0 collective-permute-start.2
  21.8 3.1 pad_maximum_fusion.2
  24.9 12.8 %collective-permute-done.2 = bf16[256,2048]{0,1:T(8,128)(2,1)} collective-permute-done((bf16[256,2048]{0,1:T(8,128)(2,1)}, bf16[256,2048]{0,1:T(8,128)(2,1)}, u32[]{:S(2)}, u32[]{:S(2)}) %collective-permute-start.2) | collective-permute-done | bytes 1048608 | tf_op jit(solution)/shard_map/ppermute | solution.py:198
  41.5 6.5 %copy.60 = bf16[2048,1024]{0,1:T(8,128)(2,1)} copy(bf16[2048,1024]{1,0:T(8,128)(2,1)} %param.21) | data formatting | bytes 8388608 | tf_op args[9]
  53.5 4.5 fusion.139
  58.0 2.9 collective-permute-done.6
  61.0 3.2 collective-permute-done.5
  65.8 3.4 fusion.136
  69.2 3.1 fusion.133
  74.7 12.7 %attn_fwd.1 = (bf16[2048,256]{1,0:T(8,128)(2,1)S(1)}, f32[2,2048,1]{2,1,0:T(8,128)S(1)}) custom-call(s32[8]{0:T(128)S(1)} %broadcast_select_fusion.order_ref, bf16[2048,768]{1,0:T(8,128)(2,1)S(1)} %pad_maximum_fusion.3.q_ref.k_ref.v_ref, bf16[2048,768]{1,0:T(8,128)(2,1)S(1)} %pad_maximum_fusion.3.q_ref.k_ref.v_ref, ...), custom_call_target="tpu_custom_call" | custom-call | flops 2147483648 | bytes 4194304 | tf_op jit(solution)/shard_map/attn_fwd/pallas_call | solution.py:48
  103.0 17.2 %collective-permute-done.26 = bf16[256,2048]{1,0:T(8,128)(2,1)S(1)} collective-permute-done((bf16[256,2048]{1,0:T(8,128)(2,1)S(1)}, bf16[256,2048]{1,0:T(8,128)(2,1)S(1)}, u32[]{:S(2)}, u32[]{:S(2)}) %collective-permute-start.26) | collective-permute-done | bytes 1048608 | tf_op jit(solution)/shard_map/ppermute | solution.py:198
  123.9 13.1 %collective-permute-done.12 = bf16[1024,512]{0,1:T(8,128)(2,1)S(1)} collective-permute-done((bf16[1024,512]{0,1:T(8,128)(2,1)S(1)}, bf16[1024,512]{0,1:T(8,128)(2,1)S(1)}, u32[]{:S(2)}, u32[]{:S(2)}) %collective-permute-start.12) | collective-permute-done | bytes 1048608 | tf_op jit(solution)/shard_map/ppermute | solution.py:209
  138.3 15.6 %collective-permute-done.9 = bf16[1024,512]{0,1:T(8,128)(2,1)S(1)} collective-permute-done((bf16[1024,512]{0,1:T(8,128)(2,1)S(1)}, bf16[1024,512]{0,1:T(8,128)(2,1)S(1)}, u32[]{:S(2)}, u32[]{:S(2)}) %collective-permute-start.9) | collective-permute-done | bytes 1048608 | tf_op jit(solution)/shard_map/ppermute | solution.py:209
  156.7 7.9 %collective-permute-done.10 = bf16[512,512]{0,1:T(8,128)(2,1)S(1)} collective-permute-done((bf16[512,512]{0,1:T(8,128)(2,1)S(1)}, bf16[512,512]{0,1:T(8,128)(2,1)S(1)}, u32[]{:S(2)}, u32[]{:S(2)}) %collective-permute-start.10) | collective-permute-done | bytes 524320 | tf_op jit(solution)/shard_map/ppermute | solution.py:209
  177.6 18.0 %collective-permute-done.18 = bf16[256,2048]{0,1:T(8,128)(2,1)S(1)} collective-permute-done((bf16[256,2048]{0,1:T(8,128)(2,1)S(1)}, bf16[256,2048]{0,1:T(8,128)(2,1)S(1)}, u32[]{:S(2)}, u32[]{:S(2)}) %collective-permute-start.18) | collective-permute-done | bytes 1048608 | tf_op jit(solution)/shard_map/ppermute | solution.py:198
  202.1 4.6 fusion.15
  206.7 3.0 collective-permute-done.22
  212.7 4.4 fusion.29
  220.0 4.6 fusion.22
  227.5 5.3 fusion.36
  232.8 7.0 %convolution_convert_fusion.3 = bf16[2048,512]{0,1:T(8,128)(2,1)S(1)} fusion(bf16[2048,1024]{1,0:T(8,128)(2,1)S(1)} %copy-done.28, s32[]{:T(128)S(6)} %select_n.102, bf16[512,1024]{1,0:T(8,128)(2,1)S(1)} %fusion.36, bf16[512,1024]{1,0:T(8,128)(2,1)S(1)} %fusion.29, bf16[512,1024]{1,0:T(8,128)(2,1)S(1)} %fusion.22, bf16[512,1024]{1,0:T(8,128)(2,1)S(1)} %fusion.15), kind=kOutput, calls=%fused_computation.23 | convolution fusion | flops 2165309440 | bytes 7340036 | tf_op jit(solution)/shard_map/dot_general | solution.py:174
  240.4 3.6 convolution_convert_fusion.4
  258.1 13.1 %convolution_convert_fusion = bf16[1024,2048]{1,0:T(8,128)(2,1)} fusion(bf16[2048,2048]{1,0:T(8,128)(2,1)} %constant_dynamic-update-slice_fusion.30, bf16[512,1024]{1,0:T(8,128)(2,1)S(1)} %get-tuple-element.149, bf16[512,1024]{1,0:T(8,128)(2,1)S(1)} %get-tuple-element.151, bf16[512,1024]{1,0:T(8,128)(2,1)S(1)} %get-tuple-element.153, ...), kind=kOutput, calls=%fused_computation.4 | convolution fusion | flops 8608808960 | bytes 16777216 | tf_op jit(solution)/shard_map/dot_general | solution.py:170
  287.8 4.1 collective-permute-done.34
  303.0 15.5 %fusion.249 = (bf16[2048,1024]{0,1:T(8,128)(2,1)}, f32[2048]{0:T(1024)S(1)}) fusion(bf16[2048,1024]{0,1:T(8,128)(2,1)} %copy.60, bf16[2048,2048]{0,1:T(8,128)(2,1)} %constant_dynamic-update-slice_fusion.12, bf16[512,1024]{1,0:T(8,128)(2,1)} %copy-done.72, bf16[512,1024]{1,0:T(8,128)(2,1)} %copy-done.68, bf16[512,1024]{1,0:T(8,128)(2,1)} %copy-done.70, ...), kind=kOutput, calls=%fused_computation.365 | convolution fusion | flops 8615098368 | bytes 20979712 | tf_op jit(solution)/shard_map/dot_general | solution.py:170
  318.5 7.6 %collective-permute-done.42 = bf16[256,2048]{0,1:T(8,128)(2,1)S(1)} collective-permute-done((bf16[256,2048]{0,1:T(8,128)(2,1)}, bf16[256,2048]{0,1:T(8,128)(2,1)S(1)}, u32[]{:S(2)}, u32[]{:S(2)}) %collective-permute-start.42) | collective-permute-done | bytes 1048608 | tf_op jit(solution)/shard_map/ppermute | solution.py:198
  326.1 3.7 pad_maximum_fusion
  339.0 5.2 collective-permute-done.46
  355.7 20.3 %attn_bwd.1 = (bf16[2048,256]{1,0:T(8,128)(2,1)S(1)}, bf16[2048,256]{1,0:T(8,128)(2,1)S(1)}, bf16[2048,256]{1,0:T(8,128)(2,1)S(1)}) custom-call(s32[8]{0:T(128)S(1)} %copy-done.6, bf16[2048,768]{1,0:T(8,128)(2,1)} %copy-done.1, bf16[2048,768]{1,0:T(8,128)(2,1)} %copy-done.1, bf16[2048,768]{1,0:T(8,128)(2,1)} %copy-done.1, ...), custom_call_target="tpu_custom_call" | custom-call | flops 5368709120 | bytes 8388608 | tf_op jit(solution)/shard_map/attn_bwd/pallas_call | solution.py:124
  376.2 5.3 convolution_convert_fusion.7
  382.9 5.1 convolution_convert_fusion.1
  388.0 3.4 convolution_convert_fusion.9
  391.4 13.9 %fusion.250 = (bf16[2048,768]{0,1:T(8,128)(2,1)}, f32[2048]{0:T(1024)S(1)}) fusion(bf16[2048,256]{0,1:T(8,128)(2,1)} %copy.48, bf16[2048,256]{0,1:T(8,128)(2,1)S(1)} %copy-done.36, bf16[2048,256]{0,1:T(8,128)(2,1)S(1)} %copy-done.34, bf16[2048,2048]{0,1:T(8,128)(2,1)} %copy-done.58, bf16[2048,768]{1,0:T(8,128)(2,1)} %copy-done.54), kind=kOutput, calls=%fused_computation.366 | convolution fusion | flops 6456604672 | bytes 17833984 | tf_op jit(solution)/shard_map/dot_general | solution.py:170
  405.5 6.3 %convolution_convert_fusion.2 = bf16[2048,512]{0,1:T(8,128)(2,1)} fusion(bf16[2048,1024]{1,0:T(8,128)(2,1)} %pad_maximum_fusion, bf16[1024,2048]{1,0:T(8,128)(2,1)} %param.22, s32[]{:T(128)S(6)} %select_n.100), kind=kOutput, calls=%fused_computation.22 | convolution fusion | flops 2148532224 | bytes 7340036 | tf_op jit(solution)/shard_map/dot_general | solution.py:166
  411.9 4.6 convolution_convert_fusion.8
  416.5 4.6 fusion.190
  421.5 4.5 fusion.187
  426.1 4.1 fusion.199
  430.3 3.3 fusion.202
  445.6 4.9 collective-permute-done.60
  451.6 15.7 %collective-permute-done.57 = bf16[1024,512]{0,1:T(8,128)(2,1)S(1)} collective-permute-done((bf16[1024,512]{0,1:T(8,128)(2,1)S(1)}, bf16[1024,512]{0,1:T(8,128)(2,1)S(1)}, u32[]{:S(2)}, u32[]{:S(2)}) %collective-permute-start.57) | collective-permute-done | bytes 1048608 | tf_op jit(solution)/shard_map/ppermute | solution.py:209
  468.4 15.7 %collective-permute-done.49 = bf16[1024,512]{0,1:T(8,128)(2,1)S(1)} collective-permute-done((bf16[1024,512]{0,1:T(8,128)(2,1)S(1)}, bf16[1024,512]{0,1:T(8,128)(2,1)S(1)}, u32[]{:S(2)}, u32[]{:S(2)}) %collective-permute-start.49) | collective-permute-done | bytes 1048608 | tf_op jit(solution)/shard_map/ppermute | solution.py:209
  485.3 15.7 %collective-permute-done.52 = bf16[1024,512]{0,1:T(8,128)(2,1)S(1)} collective-permute-done((bf16[1024,512]{0,1:T(8,128)(2,1)S(1)}, bf16[1024,512]{0,1:T(8,128)(2,1)S(1)}, u32[]{:S(2)}, u32[]{:S(2)}) %collective-permute-start.52) | collective-permute-done | bytes 1048608 | tf_op jit(solution)/shard_map/ppermute | solution.py:209
  505.1 5.4 collective-permute-done.53
  513.8 2.8 convert_select_fusion.1
  524.2 2.8 convert_element_type.442
  539.5 3.0 collective-permute-start.68
  542.5 3.9 fusion.8
  (448 shorter events, 193.1 us)
Async XLA Ops:
  7.2 517.0 %reduce-scatter.11.cloned.1.call-start = ((), (), s32[]{:S(2)}) async-start(), calls=%async_computation.7 | async-start | bytes 5242880 | tf_op jit(solution)/shard_map/reduce_scatter | solution.py:304
  10.9 26.8 %collective-permute-start.2 = (bf16[256,2048]{0,1:T(8,128)(2,1)}, bf16[256,2048]{0,1:T(8,128)(2,1)}, u32[]{:S(2)}, u32[]{:S(2)}) collective-permute-start(bf16[256,2048]{0,1:T(8,128)(2,1)} %get-tuple-element.61), channel_id=1, source_target_pairs={{0,4},{1,3},{2,6},{3,1},{4,0},{5,7},{6,2},{7,5},{8,12},{9,11},{10,... | collective-permute-start | bytes 3145736 | tf_op jit(solution)/shard_map/ppermute | solution.py:198
  13.9 36.6 %collective-permute-start.1 = (bf16[256,2048]{0,1:T(8,128)(2,1)}, bf16[256,2048]{0,1:T(8,128)(2,1)}, u32[]{:S(2)}, u32[]{:S(2)}) collective-permute-start(bf16[256,2048]{0,1:T(8,128)(2,1)} %get-tuple-element.61), channel_id=1, source_target_pairs={{0,2},{1,5},{2,0},{3,7},{4,6},{5,1},{6,4},{7,3},{8,10},{9,13},{10,... | collective-permute-start | bytes 3145736 | tf_op jit(solution)/shard_map/ppermute | solution.py:198
  15.4 38.1 %collective-permute-start = (bf16[256,2048]{0,1:T(8,128)(2,1)}, bf16[256,2048]{0,1:T(8,128)(2,1)}, u32[]{:S(2)}, u32[]{:S(2)}) collective-permute-start(bf16[256,2048]{0,1:T(8,128)(2,1)} %get-tuple-element.61), channel_id=1, source_target_pairs={{0,1},{1,0},{2,3},{3,2},{4,5},{5,4},{6,7},{7,6},{8,9},{9,8},{10,11... | collective-permute-start | bytes 3145736 | tf_op jit(solution)/shard_map/ppermute | solution.py:198
  37.7 28.0 %collective-permute-start.3 = (bf16[256,2048]{0,1:T(8,128)(2,1)}, bf16[256,2048]{0,1:T(8,128)(2,1)}, u32[]{:S(2)}, u32[]{:S(2)}) collective-permute-start(bf16[256,2048]{0,1:T(8,128)(2,1)} %collective-permute-done.2), channel_id=1, source_target_pairs={{0,1},{1,0},{2,3},{3,2},{4,5},{5,4},{6,7},{7,6},{8,9},{9,8},{10,11... | collective-permute-start | bytes 3145736 | tf_op jit(solution)/shard_map/ppermute | solution.py:198
  49.0 11.9 %collective-permute-start.6 = (bf16[128,2048]{0,1:T(8,128)(2,1)S(1)}, bf16[128,2048]{0,1:T(8,128)(2,1)S(1)}, u32[]{:S(2)}, u32[]{:S(2)}) collective-permute-start(bf16[128,2048]{0,1:T(8,128)(2,1)S(1)} %slice.605), channel_id=1, source_target_pairs={{0,2},{1,5},{2,0},{3,7},{4,6},{5,1},{6,4},{7,3},{8,10},{9,13},{10,... | collective-permute-start | bytes 1572872 | tf_op jit(solution)/shard_map/ppermute | solution.py:198
  51.6 12.5 %collective-permute-start.5 = (bf16[128,2048]{0,1:T(8,128)(2,1)S(1)}, bf16[128,2048]{0,1:T(8,128)(2,1)S(1)}, u32[]{:S(2)}, u32[]{:S(2)}) collective-permute-start(bf16[128,2048]{0,1:T(8,128)(2,1)S(1)} %slice.604), channel_id=1, source_target_pairs={{0,4},{1,3},{2,6},{3,1},{4,0},{5,7},{6,2},{7,5},{8,12},{9,11},{10,... | collective-permute-start | bytes 1572872 | tf_op jit(solution)/shard_map/ppermute | solution.py:198
  53.4 15.8 %collective-permute-start.4 = (bf16[256,2048]{0,1:T(8,128)(2,1)}, bf16[256,2048]{0,1:T(8,128)(2,1)S(1)}, u32[]{:S(2)}, u32[]{:S(2)}) collective-permute-start(bf16[256,2048]{0,1:T(8,128)(2,1)} %collective-permute-done.1), channel_id=1, source_target_pairs={{0,1},{1,0},{2,3},{3,2},{4,5},{5,4},{6,7},{7,6},{8,9},{9,8},{10,11... | collective-permute-start | bytes 3145736 | tf_op jit(solution)/shard_map/ppermute | solution.py:198
  94.3 25.9 %collective-permute-start.26 = (bf16[256,2048]{1,0:T(8,128)(2,1)S(1)}, bf16[256,2048]{1,0:T(8,128)(2,1)S(1)}, u32[]{:S(2)}, u32[]{:S(2)}) collective-permute-start(bf16[256,2048]{1,0:T(8,128)(2,1)S(1)} %copy-done.31), channel_id=1, source_target_pairs={{0,4},{1,3},{2,6},{3,1},{4,0},{5,7},{6,2},{7,5},{8,12},{9,11},{10,... | collective-permute-start | bytes 3145736 | tf_op jit(solution)/shard_map/ppermute | solution.py:198
  96.2 26.1 %collective-permute-start.25 = (bf16[256,2048]{1,0:T(8,128)(2,1)S(1)}, bf16[256,2048]{1,0:T(8,128)(2,1)S(1)}, u32[]{:S(2)}, u32[]{:S(2)}) collective-permute-start(bf16[256,2048]{1,0:T(8,128)(2,1)S(1)} %copy-done.31), channel_id=1, source_target_pairs={{0,2},{1,5},{2,0},{3,7},{4,6},{5,1},{6,4},{7,3},{8,10},{9,13},{10,... | collective-permute-start | bytes 3145736 | tf_op jit(solution)/shard_map/ppermute | solution.py:198
  96.9 26.0 %collective-permute-start.24 = (bf16[256,2048]{1,0:T(8,128)(2,1)S(1)}, bf16[256,2048]{1,0:T(8,128)(2,1)S(1)}, u32[]{:S(2)}, u32[]{:S(2)}) collective-permute-start(bf16[256,2048]{1,0:T(8,128)(2,1)S(1)} %copy-done.31), channel_id=1, source_target_pairs={{0,1},{1,0},{2,3},{3,2},{4,5},{5,4},{6,7},{7,6},{8,9},{9,8},{10,11... | collective-permute-start | bytes 3145736 | tf_op jit(solution)/shard_map/ppermute | solution.py:198
  98.9 38.1 %collective-permute-start.12 = (bf16[1024,512]{0,1:T(8,128)(2,1)S(1)}, bf16[1024,512]{0,1:T(8,128)(2,1)S(1)}, u32[]{:S(2)}, u32[]{:S(2)}) collective-permute-start(bf16[1024,512]{0,1:T(8,128)(2,1)S(1)} %fusion.47), channel_id=1, source_target_pairs={{0,4},{1,3},{2,6},{3,1},{4,0},{5,7},{6,2},{7,5},{8,12},{9,11},{10,... | collective-permute-start | bytes 3145736 | tf_op jit(solution)/shard_map/ppermute | solution.py:209
  99.8 54.1 %collective-permute-start.9 = (bf16[1024,512]{0,1:T(8,128)(2,1)S(1)}, bf16[1024,512]{0,1:T(8,128)(2,1)S(1)}, u32[]{:S(2)}, u32[]{:S(2)}) collective-permute-start(bf16[1024,512]{0,1:T(8,128)(2,1)S(1)} %fusion.48), channel_id=1, source_target_pairs={{0,4},{1,3},{2,6},{3,1},{4,0},{5,7},{6,2},{7,5},{8,12},{9,11},{10,... | collective-permute-start | bytes 3145736 | tf_op jit(solution)/shard_map/ppermute | solution.py:209
  120.2 45.1 %collective-permute-start.30 = (bf16[128,2048]{1,0:T(8,128)(2,1)S(1)}, bf16[128,2048]{1,0:T(8,128)(2,1)S(1)}, u32[]{:S(2)}, u32[]{:S(2)}) collective-permute-start(bf16[128,2048]{1,0:T(8,128)(2,1)S(1)} %slice.639), channel_id=1, source_target_pairs={{0,2},{1,5},{2,0},{3,7},{4,6},{5,1},{6,4},{7,3},{8,10},{9,13},{10,... | collective-permute-start | bytes 1572872 | tf_op jit(solution)/shard_map/ppermute | solution.py:198
  122.3 43.3 %collective-permute-start.29 = (bf16[128,2048]{1,0:T(8,128)(2,1)S(1)}, bf16[128,2048]{1,0:T(8,128)(2,1)S(1)}, u32[]{:S(2)}, u32[]{:S(2)}) collective-permute-start(bf16[128,2048]{1,0:T(8,128)(2,1)S(1)} %slice.638), channel_id=1, source_target_pairs={{0,4},{1,3},{2,6},{3,1},{4,0},{5,7},{6,2},{7,5},{8,12},{9,11},{10,... | collective-permute-start | bytes 1572872 | tf_op jit(solution)/shard_map/ppermute | solution.py:198
  122.8 43.2 %collective-permute-start.27 = (bf16[256,2048]{1,0:T(8,128)(2,1)S(1)}, bf16[256,2048]{1,0:T(8,128)(2,1)S(1)}, u32[]{:S(2)}, u32[]{:S(2)}) collective-permute-start(bf16[256,2048]{1,0:T(8,128)(2,1)S(1)} %collective-permute-done.26), channel_id=1, source_target_pairs={{0,1},{1,0},{2,3},{3,2},{4,5},{5,4},{6,7},{7,6},{8,9},{9,8},{10,11... | collective-permute-start | bytes 3145736 | tf_op jit(solution)/shard_map/ppermute | solution.py:198
  137.2 19.0 %collective-permute-start.13 = (bf16[512,512]{0,1:T(8,128)(2,1)S(1)}, bf16[512,512]{0,1:T(8,128)(2,1)S(1)}, u32[]{:S(2)}, u32[]{:S(2)}) collective-permute-start(bf16[512,512]{0,1:T(8,128)(2,1)S(1)} %fusion.179), channel_id=1, source_target_pairs={{0,2},{1,5},{2,0},{3,7},{4,6},{5,1},{6,4},{7,3},{8,10},{9,13},{10,... | collective-permute-start | bytes 1572872 | tf_op jit(solution)/shard_map/ppermute | solution.py:209
  156.2 17.4 %collective-permute-start.28 = (bf16[256,2048]{1,0:T(8,128)(2,1)S(1)}, bf16[256,2048]{1,0:T(8,128)(2,1)S(1)}, u32[]{:S(2)}, u32[]{:S(2)}) collective-permute-start(bf16[256,2048]{1,0:T(8,128)(2,1)S(1)} %collective-permute-done.25), channel_id=1, source_target_pairs={{0,1},{1,0},{2,3},{3,2},{4,5},{5,4},{6,7},{7,6},{8,9},{9,8},{10,11... | collective-permute-start | bytes 3145736 | tf_op jit(solution)/shard_map/ppermute | solution.py:198
  169.8 25.8 %collective-permute-start.18 = (bf16[256,2048]{0,1:T(8,128)(2,1)S(1)}, bf16[256,2048]{0,1:T(8,128)(2,1)S(1)}, u32[]{:S(2)}, u32[]{:S(2)}) collective-permute-start(bf16[256,2048]{0,1:T(8,128)(2,1)S(1)} %get-tuple-element.59), channel_id=1, source_target_pairs={{0,4},{1,3},{2,6},{3,1},{4,0},{5,7},{6,2},{7,5},{8,12},{9,11},{10,... | collective-permute-start | bytes 3145736 | tf_op jit(solution)/shard_map/ppermute | solution.py:198
  171.5 25.4 %collective-permute-start.17 = (bf16[256,2048]{0,1:T(8,128)(2,1)S(1)}, bf16[256,2048]{0,1:T(8,128)(2,1)S(1)}, u32[]{:S(2)}, u32[]{:S(2)}) collective-permute-start(bf16[256,2048]{0,1:T(8,128)(2,1)S(1)} %get-tuple-element.59), channel_id=1, source_target_pairs={{0,2},{1,5},{2,0},{3,7},{4,6},{5,1},{6,4},{7,3},{8,10},{9,13},{10,... | collective-permute-start | bytes 3145736 | tf_op jit(solution)/shard_map/ppermute | solution.py:198
  172.6 26.8 %collective-permute-start.16 = (bf16[256,2048]{0,1:T(8,128)(2,1)S(1)}, bf16[256,2048]{0,1:T(8,128)(2,1)S(1)}, u32[]{:S(2)}, u32[]{:S(2)}) collective-permute-start(bf16[256,2048]{0,1:T(8,128)(2,1)S(1)} %get-tuple-element.59), channel_id=1, source_target_pairs={{0,1},{1,0},{2,3},{3,2},{4,5},{5,4},{6,7},{7,6},{8,9},{9,8},{10,11... | collective-permute-start | bytes 3145736 | tf_op jit(solution)/shard_map/ppermute | solution.py:198
  195.7 14.1 %collective-permute-start.22 = (bf16[128,2048]{0,1:T(8,128)(2,1)S(1)}, bf16[128,2048]{0,1:T(8,128)(2,1)S(1)}, u32[]{:S(2)}, u32[]{:S(2)}) collective-permute-start(bf16[128,2048]{0,1:T(8,128)(2,1)S(1)} %slice.637), channel_id=1, source_target_pairs={{0,2},{1,5},{2,0},{3,7},{4,6},{5,1},{6,4},{7,3},{8,10},{9,13},{10,... | collective-permute-start | bytes 1572872 | tf_op jit(solution)/shard_map/ppermute | solution.py:198
  197.0 12.7 %collective-permute-start.21 = (bf16[128,2048]{0,1:T(8,128)(2,1)S(1)}, bf16[128,2048]{0,1:T(8,128)(2,1)S(1)}, u32[]{:S(2)}, u32[]{:S(2)}) collective-permute-start(bf16[128,2048]{0,1:T(8,128)(2,1)S(1)} %slice.636), channel_id=1, source_target_pairs={{0,4},{1,3},{2,6},{3,1},{4,0},{5,7},{6,2},{7,5},{8,12},{9,11},{10,... | collective-permute-start | bytes 1572872 | tf_op jit(solution)/shard_map/ppermute | solution.py:198
  198.8 18.4 %collective-permute-start.19 = (bf16[256,2048]{0,1:T(8,128)(2,1)S(1)}, bf16[256,2048]{0,1:T(8,128)(2,1)S(1)}, u32[]{:S(2)}, u32[]{:S(2)}) collective-permute-start(bf16[256,2048]{0,1:T(8,128)(2,1)S(1)} %collective-permute-done.18), channel_id=1, source_target_pairs={{0,1},{1,0},{2,3},{3,2},{4,5},{5,4},{6,7},{7,6},{8,9},{9,8},{10,11... | collective-permute-start | bytes 3145736 | tf_op jit(solution)/shard_map/ppermute | solution.py:198
  209.9 14.8 %collective-permute-start.23 = (bf16[256,2048]{0,1:T(8,128)(2,1)S(1)}, bf16[256,2048]{0,1:T(8,128)(2,1)S(1)}, u32[]{:S(2)}, u32[]{:S(2)}) collective-permute-start(bf16[256,2048]{0,1:T(8,128)(2,1)S(1)} %pad_maximum_fusion.8), channel_id=1, source_target_pairs={{0,1},{1,0},{2,3},{3,2},{4,5},{5,4},{6,7},{7,6},{8,9},{9,8},{10,11... | collective-permute-start | bytes 3145736 | tf_op jit(solution)/shard_map/ppermute | solution.py:198
  253.6 21.4 %collective-permute-start.36 = (bf16[1024,512]{0,1:T(8,128)(2,1)}, bf16[1024,512]{0,1:T(8,128)(2,1)}, u32[]{:S(2)}, u32[]{:S(2)}) collective-permute-start(bf16[1024,512]{0,1:T(8,128)(2,1)} %fusion.45), channel_id=1, source_target_pairs={{0,4},{1,3},{2,6},{3,1},{4,0},{5,7},{6,2},{7,5},{8,12},{9,11},{10,... | collective-permute-start | bytes 3145736 | tf_op jit(solution)/shard_map/ppermute | solution.py:209
  257.5 23.4 %collective-permute-start.33 = (bf16[1024,512]{0,1:T(8,128)(2,1)}, bf16[1024,512]{0,1:T(8,128)(2,1)}, u32[]{:S(2)}, u32[]{:S(2)}) collective-permute-start(bf16[1024,512]{0,1:T(8,128)(2,1)} %fusion.46), channel_id=1, source_target_pairs={{0,4},{1,3},{2,6},{3,1},{4,0},{5,7},{6,2},{7,5},{8,12},{9,11},{10,... | collective-permute-start | bytes 3145736 | tf_op jit(solution)/shard_map/ppermute | solution.py:209
  271.2 255.9 %reduce-scatter.9.cloned.1.call-start = ((), (), s32[]{:S(2)}) async-start(), calls=%async_computation.6 | async-start | bytes 5242880 | tf_op jit(solution)/shard_map/reduce_scatter | solution.py:307
  300.1 26.0 %collective-permute-start.42 = (bf16[256,2048]{0,1:T(8,128)(2,1)}, bf16[256,2048]{0,1:T(8,128)(2,1)S(1)}, u32[]{:S(2)}, u32[]{:S(2)}) collective-permute-start(bf16[256,2048]{0,1:T(8,128)(2,1)} %get-tuple-element.57), channel_id=1, source_target_pairs={{0,4},{1,3},{2,6},{3,1},{4,0},{5,7},{6,2},{7,5},{8,12},{9,11},{10,... | collective-permute-start | bytes 3145736 | tf_op jit(solution)/shard_map/ppermute | solution.py:198
  301.6 29.7 %collective-permute-start.41 = (bf16[256,2048]{0,1:T(8,128)(2,1)}, bf16[256,2048]{0,1:T(8,128)(2,1)S(1)}, u32[]{:S(2)}, u32[]{:S(2)}) collective-permute-start(bf16[256,2048]{0,1:T(8,128)(2,1)} %get-tuple-element.57), channel_id=1, source_target_pairs={{0,2},{1,5},{2,0},{3,7},{4,6},{5,1},{6,4},{7,3},{8,10},{9,13},{10,... | collective-permute-start | bytes 3145736 | tf_op jit(solution)/shard_map/ppermute | solution.py:198
  303.0 30.1 %collective-permute-start.40 = (bf16[256,2048]{0,1:T(8,128)(2,1)}, bf16[256,2048]{0,1:T(8,128)(2,1)}, u32[]{:S(2)}, u32[]{:S(2)}) collective-permute-start(bf16[256,2048]{0,1:T(8,128)(2,1)} %get-tuple-element.57), channel_id=1, source_target_pairs={{0,1},{1,0},{2,3},{3,2},{4,5},{5,4},{6,7},{7,6},{8,9},{9,8},{10,11... | collective-permute-start | bytes 3145736 | tf_op jit(solution)/shard_map/ppermute | solution.py:198
  326.1 19.1 %collective-permute-start.43 = (bf16[256,2048]{0,1:T(8,128)(2,1)S(1)}, bf16[256,2048]{0,1:T(8,128)(2,1)}, u32[]{:S(2)}, u32[]{:S(2)}) collective-permute-start(bf16[256,2048]{0,1:T(8,128)(2,1)S(1)} %collective-permute-done.42), channel_id=1, source_target_pairs={{0,1},{1,0},{2,3},{3,2},{4,5},{5,4},{6,7},{7,6},{8,9},{9,8},{10,11... | collective-permute-start | bytes 3145736 | tf_op jit(solution)/shard_map/ppermute | solution.py:198
  329.8 199.8 %reduce-scatter.7.cloned.1.call-start = ((), (), s32[]{:S(2)}) async-start(), calls=%async_computation.5 | async-start | bytes 1310720 | tf_op jit(solution)/shard_map/reduce_scatter | solution.py:314
  329.9 14.3 %collective-permute-start.46 = (bf16[128,2048]{0,1:T(8,128)(2,1)S(1)}, bf16[128,2048]{0,1:T(8,128)(2,1)S(1)}, u32[]{:S(2)}, u32[]{:S(2)}) collective-permute-start(bf16[128,2048]{0,1:T(8,128)(2,1)S(1)} %slice.671), channel_id=1, source_target_pairs={{0,2},{1,5},{2,0},{3,7},{4,6},{5,1},{6,4},{7,3},{8,10},{9,13},{10,... | collective-permute-start | bytes 1572872 | tf_op jit(solution)/shard_map/ppermute | solution.py:198
  331.3 13.0 %collective-permute-start.45 = (bf16[128,2048]{0,1:T(8,128)(2,1)S(1)}, bf16[128,2048]{0,1:T(8,128)(2,1)S(1)}, u32[]{:S(2)}, u32[]{:S(2)}) collective-permute-start(bf16[128,2048]{0,1:T(8,128)(2,1)S(1)} %slice.670), channel_id=1, source_target_pairs={{0,4},{1,3},{2,6},{3,1},{4,0},{5,7},{6,2},{7,5},{8,12},{9,11},{10,... | collective-permute-start | bytes 1572872 | tf_op jit(solution)/shard_map/ppermute | solution.py:198
  333.1 15.6 %collective-permute-start.44 = (bf16[256,2048]{0,1:T(8,128)(2,1)S(1)}, bf16[256,2048]{0,1:T(8,128)(2,1)S(1)}, u32[]{:S(2)}, u32[]{:S(2)}) collective-permute-start(bf16[256,2048]{0,1:T(8,128)(2,1)S(1)} %collective-permute-done.41), channel_id=1, source_target_pairs={{0,1},{1,0},{2,3},{3,2},{4,5},{5,4},{6,7},{7,6},{8,9},{9,8},{10,11... | collective-permute-start | bytes 3145736 | tf_op jit(solution)/shard_map/ppermute | solution.py:198
  381.6 52.0 %collective-permute-start.59 = (bf16[2048,512]{0,1:T(8,128)(2,1)}, bf16[2048,512]{0,1:T(8,128)(2,1)}, u32[]{:S(2)}, u32[]{:S(2)}) collective-permute-start(bf16[2048,512]{0,1:T(8,128)(2,1)} %convolution_convert_fusion.7), channel_id=1, source_target_pairs={{0,1},{1,0},{2,3},{3,2},{4,5},{5,4},{6,7},{7,6},{8,9},{9,8},{10,11... | collective-permute-start | bytes 6291464 | tf_op jit(solution)/shard_map/ppermute | solution.py:209
  405.3 147.4 %reduce-scatter.5.cloned.1.call-start = ((), (), s32[]{:S(2)}) async-start(), calls=%async_computation.4 | async-start | bytes 3932160 | tf_op jit(solution)/shard_map/reduce_scatter | solution.py:326
  416.5 20.0 %collective-permute-start.56 = (bf16[2048,512]{0,1:T(8,128)(2,1)}, bf16[2048,512]{0,1:T(8,128)(2,1)}, u32[]{:S(2)}, u32[]{:S(2)}) collective-permute-start(bf16[2048,512]{0,1:T(8,128)(2,1)} %convolution_convert_fusion.8), channel_id=1, source_target_pairs={{0,1},{1,0},{2,3},{3,2},{4,5},{5,4},{6,7},{7,6},{8,9},{9,8},{10,11... | collective-permute-start | bytes 6291464 | tf_op jit(solution)/shard_map/ppermute | solution.py:209
  421.0 18.7 %collective-permute-start.48 = (bf16[2048,512]{0,1:T(8,128)(2,1)}, bf16[2048,512]{0,1:T(8,128)(2,1)}, u32[]{:S(2)}, u32[]{:S(2)}) collective-permute-start(bf16[2048,512]{0,1:T(8,128)(2,1)} %convolution_convert_fusion.2), channel_id=1, source_target_pairs={{0,1},{1,0},{2,3},{3,2},{4,5},{5,4},{6,7},{7,6},{8,9},{9,8},{10,11... | collective-permute-start | bytes 6291464 | tf_op jit(solution)/shard_map/ppermute | solution.py:209
  426.1 17.0 %collective-permute-start.51 = (bf16[2048,512]{0,1:T(8,128)(2,1)}, bf16[2048,512]{0,1:T(8,128)(2,1)S(1)}, u32[]{:S(2)}, u32[]{:S(2)}) collective-permute-start(bf16[2048,512]{0,1:T(8,128)(2,1)} %convolution_convert_fusion.1), channel_id=1, source_target_pairs={{0,1},{1,0},{2,3},{3,2},{4,5},{5,4},{6,7},{7,6},{8,9},{9,8},{10,11... | collective-permute-start | bytes 6291464 | tf_op jit(solution)/shard_map/ppermute | solution.py:209
  435.6 14.9 %collective-permute-start.60 = (bf16[1024,512]{0,1:T(8,128)(2,1)S(1)}, bf16[1024,512]{0,1:T(8,128)(2,1)S(1)}, u32[]{:S(2)}, u32[]{:S(2)}) collective-permute-start(bf16[1024,512]{0,1:T(8,128)(2,1)S(1)} %fusion.41), channel_id=1, source_target_pairs={{0,4},{1,3},{2,6},{3,1},{4,0},{5,7},{6,2},{7,5},{8,12},{9,11},{10,... | collective-permute-start | bytes 3145736 | tf_op jit(solution)/shard_map/ppermute | solution.py:209
  438.6 28.7 %collective-permute-start.57 = (bf16[1024,512]{0,1:T(8,128)(2,1)S(1)}, bf16[1024,512]{0,1:T(8,128)(2,1)S(1)}, u32[]{:S(2)}, u32[]{:S(2)}) collective-permute-start(bf16[1024,512]{0,1:T(8,128)(2,1)S(1)} %fusion.42), channel_id=1, source_target_pairs={{0,4},{1,3},{2,6},{3,1},{4,0},{5,7},{6,2},{7,5},{8,12},{9,11},{10,... | collective-permute-start | bytes 3145736 | tf_op jit(solution)/shard_map/ppermute | solution.py:209
  441.9 42.3 %collective-permute-start.49 = (bf16[1024,512]{0,1:T(8,128)(2,1)S(1)}, bf16[1024,512]{0,1:T(8,128)(2,1)S(1)}, u32[]{:S(2)}, u32[]{:S(2)}) collective-permute-start(bf16[1024,512]{0,1:T(8,128)(2,1)S(1)} %fusion.44), channel_id=1, source_target_pairs={{0,4},{1,3},{2,6},{3,1},{4,0},{5,7},{6,2},{7,5},{8,12},{9,11},{10,... | collective-permute-start | bytes 3145736 | tf_op jit(solution)/shard_map/ppermute | solution.py:209
  444.4 56.6 %collective-permute-start.52 = (bf16[1024,512]{0,1:T(8,128)(2,1)S(1)}, bf16[1024,512]{0,1:T(8,128)(2,1)S(1)}, u32[]{:S(2)}, u32[]{:S(2)}) collective-permute-start(bf16[1024,512]{0,1:T(8,128)(2,1)S(1)} %fusion.43), channel_id=1, source_target_pairs={{0,4},{1,3},{2,6},{3,1},{4,0},{5,7},{6,2},{7,5},{8,12},{9,11},{10,... | collective-permute-start | bytes 3145736 | tf_op jit(solution)/shard_map/ppermute | solution.py:209
  450.7 51.5 %collective-permute-start.61 = (bf16[512,512]{0,1:T(8,128)(2,1)S(1)}, bf16[512,512]{0,1:T(8,128)(2,1)S(1)}, u32[]{:S(2)}, u32[]{:S(2)}) collective-permute-start(bf16[512,512]{0,1:T(8,128)(2,1)S(1)} %fusion.155), channel_id=1, source_target_pairs={{0,2},{1,5},{2,0},{3,7},{4,6},{5,1},{6,4},{7,3},{8,10},{9,13},{10,... | collective-permute-start | bytes 1572872 | tf_op jit(solution)/shard_map/ppermute | solution.py:209
  467.5 35.0 %collective-permute-start.58 = (bf16[512,512]{0,1:T(8,128)(2,1)S(1)}, bf16[512,512]{0,1:T(8,128)(2,1)S(1)}, u32[]{:S(2)}, u32[]{:S(2)}) collective-permute-start(bf16[512,512]{0,1:T(8,128)(2,1)S(1)} %fusion.159), channel_id=1, source_target_pairs={{0,2},{1,5},{2,0},{3,7},{4,6},{5,1},{6,4},{7,3},{8,10},{9,13},{10,... | collective-permute-start | bytes 1572872 | tf_op jit(solution)/shard_map/ppermute | solution.py:209
  484.4 19.7 %collective-permute-start.50 = (bf16[512,512]{0,1:T(8,128)(2,1)S(1)}, bf16[512,512]{0,1:T(8,128)(2,1)S(1)}, u32[]{:S(2)}, u32[]{:S(2)}) collective-permute-start(bf16[512,512]{0,1:T(8,128)(2,1)S(1)} %fusion.167), channel_id=1, source_target_pairs={{0,2},{1,5},{2,0},{3,7},{4,6},{5,1},{6,4},{7,3},{8,10},{9,13},{10,... | collective-permute-start | bytes 1572872 | tf_op jit(solution)/shard_map/ppermute | solution.py:209
  (105 other events, 1202.2 us)
Sparse Core Ops, SparseCore 0:
  271.3 77.8 reduce-scatter.10
  351.6 77.2 reduce-scatter.8
  431.2 27.6 reduce-scatter.6
  461.2 58.8 reduce-scatter.4

commit v2 on v1

--- a/solution.py
+++ b/solution.py
@@ -182,6 +182,157 @@
     return (r & 1) | ((r & 2) << 1) | ((r & 4) >> 1)
 
 
+MESH = pl.DeviceIdType.MESH
+HBM_SPACE = pl.ANY
+VMEM_SPACE = pltpu.VMEM
+
+
+def neighbours():
+    dp, me = lax.axis_index("dp"), lax.axis_index("mp")
+    core, along_x, along_y = me % 2, (me // 2) % 2, me // 4
+    by_x, by_y = me + 2 - 4 * along_x, me + 4 - 8 * along_y
+    first = (1 - core) * by_y + core * by_x
+    second = (1 - core) * by_x + core * by_y
+    return core, (dp, me + 1 - 2 * core), (dp, first), (dp, second)
+
+
+def greet(*others):
+    barrier = pltpu.get_barrier_semaphore()
+    for other in others:
+        pl.semaphore_signal(barrier, inc=1, device_id=other, device_id_type=MESH)
+    pl.semaphore_wait(barrier, len(others))
+
+
+class Gather:
+    COPIES = 11
+
+    def __init__(self, buf, sends, recvs, sib, first, second):
+        rows = buf.shape[1]
+        low, high, whole = pl.ds(0, rows // 2), pl.ds(rows // 2, rows // 2), pl.ds(0, rows)
+
+        def copy(i, source, target, part, device):
+            return pltpu.make_async_remote_copy(
+                src_ref=buf.at[source, part], dst_ref=buf.at[target, part],
+                send_sem=sends.at[i], recv_sem=recvs.at[i], device_id=device, device_id_type=MESH,
+            )
+
+        self.copies = [
+            copy(0, 0, 4, high, first), copy(1, 0, 4, low, first),
+            copy(2, 0, 2, low, second), copy(3, 0, 2, high, second),
+            copy(4, 0, 1, whole, sib),
+            copy(5, 2, 6, low, first), copy(6, 4, 6, high, second),
+            copy(7, 4, 3, whole, sib), copy(8, 2, 5, whole, sib),
+            copy(9, 6, 7, low, sib), copy(10, 6, 7, high, sib),
+        ]
+
+    def start(self):
+        for i in (0, 2, 1, 3, 4):
+            self.copies[i].start()
+
+    def pair(self):
+        self.copies[4].wait_recv()
+
+    def forward(self):
+        for arrived, onward in ((2, 5), (0, 6)):
+            self.copies[arrived].wait_recv()
+            self.copies[onward].start()
+        for arrived, onward in ((1, 7), (3, 8)):
+            self.copies[arrived].wait_recv()
+            self.copies[onward].start()
+
+    def middle(self):
+        self.copies[7].wait_recv()
+        self.copies[8].wait_recv()
+
+    def finish(self):
+        for arrived, onward in ((5, 9), (6, 10)):
+            self.copies[arrived].wait_recv()
+            self.copies[onward].start()
+        self.copies[9].wait_recv()
+        self.copies[10].wait_recv()
+
+    def drain(self):
+        for one in self.copies:
+            one.wait_send()
+
+
+def norm_store(rows_ref, gain_ref, store, step=32):
+    def some(i, carry):
+        part = pl.ds(pl.multiple_of(i * step, step), step)
+        store(part, norm_rows(rows_ref[part, :].astype(F32), gain_ref[...]).astype(BF))
+        return carry
+
+    lax.fori_loop(0, rows_ref.shape[0] // step, some, 0)
+
+
+def project_body(tok_hbm, gain_ref, wq_hbm, wk_hbm, wv_hbm, qkv_hbm, normed_hbm, tok_ref, w_ref, qkv_ref, buf, sends, recvs, locals_):
+    core, sib, first, second = neighbours()
+    rows = tok_ref.shape[0]
+    width = wq_hbm.shape[1]
+    fetch = [pltpu.make_async_copy(tok_hbm, tok_ref, locals_.at[16])]
+    for k, w_hbm in enumerate((wq_hbm, wk_hbm, wv_hbm)):
+        fetch.append(pltpu.make_async_copy(w_hbm, w_ref.at[:, pl.ds(k * width, width)], locals_.at[17 + k]))
+    for one in fetch:
+        one.start()
+    greet(sib, first, second)
+    fetch[0].wait()
+
+    def keep(part, value):
+        buf[0, part, :] = value
+
+    norm_store(tok_ref, gain_ref, keep)
+    ring = Gather(buf, sends, recvs, sib, first, second)
+    ring.start()
+    for one in fetch[1:]:
+        one.wait()
+
+    def moved(s):
+        at = pl.ds(pl.multiple_of(s * rows, rows), rows)
+        return (
+            pltpu.make_async_copy(buf.at[s], normed_hbm.at[at], locals_.at[s]),
+            pltpu.make_async_copy(qkv_ref.at[at], qkv_hbm.at[at], locals_.at[8 + s]),
+        )
+
+    def slot(s, carry):
+        at = pl.ds(pl.multiple_of(s * rows, rows), rows)
+        normed_out, qkv_out = moved(s)
+        normed_out.start()
+        qkv_ref[at, :] = dot_nn(buf[s], w_ref[...]).astype(BF)
+        qkv_out.start()
+        return carry
+
+    ring.pair()
+    lax.fori_loop(0, 2, slot, 0)
+    ring.forward()
+    ring.middle()
+    lax.fori_loop(2, 6, slot, 0)
+    ring.finish()
+    lax.fori_loop(6, 8, slot, 0)
+    for s in range(8):
+        for one in moved(s):
+            one.wait()
+    ring.drain()
+
+
+def project(tokens, gain, w_query, w_key, w_value):
+    rows, width = tokens.shape
+    cols = w_query.shape[1]
+    hbm = pl.BlockSpec(memory_space=HBM_SPACE)
+    return pl.pallas_call(
+        project_body, name="gather_project",
+        in_specs=[hbm, pl.BlockSpec(memory_space=VMEM_SPACE), hbm, hbm, hbm],
+        out_specs=[hbm, hbm],
+        out_shape=[jax.ShapeDtypeStruct((8 * rows, 3 * cols), BF), jax.ShapeDtypeStruct((8 * rows, width), BF)],
+        scratch_shapes=[
+            pltpu.VMEM((rows, width), BF), pltpu.VMEM((width, 3 * cols), BF), pltpu.VMEM((8 * rows, 3 * cols), BF),
+            pltpu.VMEM((8, rows, width), BF), pltpu.SemaphoreType.DMA((11,)), pltpu.SemaphoreType.DMA((11,)),
+            pltpu.SemaphoreType.DMA((20,)),
+        ],
+        compiler_params=pltpu.CompilerParams(collective_id=1, has_side_effects=True, vmem_limit_bytes=58 * 2**20),
+        cost_estimate=pl.CostEstimate(flops=2 * 8 * rows * width * 3 * cols, bytes_accessed=60 * 2**20, transcendentals=0),
+    )(tokens, gain[None, :], w_query, w_key, w_value)
+
+
 class Cube:
     def __init__(self, me):
         self.me = me
@@ -281,9 +432,12 @@
     tokens32 = tokens.astype(F32)
     w_qkv = jnp.concatenate([w_query, w_key, w_value], 1)
 
-    normed_groups = net.gather(norm_rows(tokens32, gain_attn).astype(BF))
-    qkv = joined([dot_nn(joined(g), w_qkv).astype(BF) for g in normed_groups])
-    normed = stack(normed_groups)
+    if isinstance(net, Cube):
+        qkv, normed = project(tokens, gain_attn, w_query, w_key, w_value)
+    else:
+        normed_groups = net.gather(norm_rows(tokens32, gain_attn).astype(BF))
+        qkv = joined([dot_nn(joined(g), w_qkv).astype(BF) for g in normed_groups])
+        normed = stack(normed_groups)
 
     mixed, lse = attn_fwd(qkv, net.order, row_key, col_key, heads, own_rows)
     grad_groups = net.gather(after(grad_out, qkv))

time: 574 us -> 573 us (level)
  waiting for transfers between devices: 177 us -> 132 us
  Pallas kernels: 33 us -> 76.5 us
  local copies, waits for them, and re-layouts: 87.9 us -> 105 us
  starting transfers between devices: 53.5 us -> 43.9 us
    pallas_call x0 -> x1, Pallas kernels: none -> 44.6 us  [project(): pl.pallas_call(project_body, name='gather_project', in_specs=[hbm, pl.Blo...]
    ppermute x32 -> x24, waiting for transfers between devices: 71.4 us -> 30.7 us  [gather(): send = lambda v, p: lax.ppermute(v, 'mp', p)]
    dot_general x16, matrix products: 57.5 us -> 72.4 us  [dot_nt(): lax.dot_general(a, b, (((1,), (1,)), ((), ())), preferred_element_type=F32)]
    unnamed x197 -> x190, local copies, waits for them, and re-layouts: 67.1 us -> 79.2 us
    ppermute x32 -> x24, starting transfers between devices: 25.4 us -> 14.4 us  [gather(): send = lambda v, p: lax.ppermute(v, 'mp', p)]
    dot_general x16 -> x12, matrix products: 47.5 us -> 38.4 us  [dot_nn(): return jnp.dot(a, b, preferred_element_type=F32)]
  transfers between devices with their start and end apart: 73 -> 65, of which waited for: 23 -> 19; matrix products, arithmetic and copies ran while one was open for 45% -> 46% of each run, Pallas kernels for 4% -> 3%
where the time goes in v2:
time: 573 us; the launch traced here: 568 us
  matrix products  153 us (27%)
  waiting for transfers between devices  132 us (23%)
  local copies, waits for them, and re-layouts  105 us (18%)
  Pallas kernels  76.5 us (13%)
  starting transfers between devices  43.9 us (8%)
  other arithmetic  41.9 us (7%)
  between operations  16.1 us (3%)
    ppermute x32, waiting for transfers between devices, scatter(): send = lambda v, p: lax.ppermute(v, 'mp', p)  98.8 us
    unnamed x190, local copies, waits for them, and re-layouts  79.2 us
    dot_general x16, matrix products, dot_nt(): lax.dot_general(a, b, (((1,), (1,)), ((), ())), preferred_element_type=F32)  72.4 us
    pallas_call x1, Pallas kernels, project(): pl.pallas_call(project_body, name='gather_project', in_specs=[hbm, pl.Blo...  44.6 us
    dot_general x4, matrix products, dot_tn(): lax.dot_general(a, b, (((0,), (0,)), ((), ())), preferred_element_type=F32)  42.5 us
    dot_general x12, matrix products, dot_nn(): return jnp.dot(a, b, preferred_element_type=F32)  38.4 us
    ppermute x24, waiting for transfers between devices, gather(): send = lambda v, p: lax.ppermute(v, 'mp', p)  30.7 us
    ppermute x32, starting transfers between devices, scatter(): send = lambda v, p: lax.ppermute(v, 'mp', p)  21.6 us
  transfers between devices with their start and end apart: 65, of which 19 were waited for; matrix products, arithmetic and copies ran while one was open for 46% of the time, Pallas kernels for 3%

profile of v2, /device:TPU:0, one launch (start us, length us, event | category | flops | bytes accessed | tf_op | source)
XLA Modules:
  0.0 568.3 jit_solution(18332127250997310967)
XLA Ops:
  9.2 44.6 %gather_project.1 = (bf16[2048,768]{1,0:T(8,128)(2,1)}, bf16[2048,2048]{1,0:T(8,128)(2,1)}) custom-call(bf16[256,2048]{1,0:T(8,128)(2,1)} %tok_hbm.1, f32[1,2048]{1,0:T(1,128)} %bitcast.45, bf16[2048,256]{1,0:T(8,128)(2,1)} %wq_hbm.1, bf16[2048,256]{1,0:T(8,128)(2,1)} %wk_hbm.1, bf16[2048,256]{1,0:T(8,128)(2,1)} %wv_hbm.1), custom_call_target="tpu_custom_call" | custom-call | flops 6442450944 | bytes 62914560 | tf_op jit(solution)/shard_map/gather_project/pallas_call | solution.py:321
  55.7 12.3 %attn_fwd.1 = (bf16[2048,256]{1,0:T(8,128)(2,1)S(1)}, f32[2,2048,1]{2,1,0:T(8,128)S(1)}) custom-call(s32[8]{0:T(128)S(1)} %broadcast_select_fusion.order_ref, bf16[2048,768]{1,0:T(8,128)(2,1)S(1)} %copy-done.1, bf16[2048,768]{1,0:T(8,128)(2,1)S(1)} %copy-done.1, bf16[2048,768]{1,0:T(8,128)(2,1)S(1)} %copy-done.1, s32[2048,1]{1,0:T(8,128)S(1)} %copy.46.rk_ref, ...), custom_call_target="tpu_custom_call" | custom-call | flops 2147483648 | bytes 4194304 | tf_op jit(solution)/shard_map/attn_fwd/pallas_call | solution.py:48
  78.5 2.7 copy.55
  88.1 16.7 %copy.60 = bf16[2048,1024]{0,1:T(8,128)(2,1)} copy(bf16[2048,1024]{1,0:T(8,128)(2,1)} %param.21) | data formatting | bytes 8388608 | tf_op args[9]
  121.5 5.3 collective-permute-done.4
  127.8 17.8 %collective-permute-done.1 = bf16[1024,512]{0,1:T(8,128)(2,1)S(1)} collective-permute-done((bf16[1024,512]{0,1:T(8,128)(2,1)S(1)}, bf16[1024,512]{0,1:T(8,128)(2,1)S(1)}, u32[]{:S(2)}, u32[]{:S(2)}) %collective-permute-start.1) | collective-permute-done | bytes 1048608 | tf_op jit(solution)/shard_map/ppermute | solution.py:360
  148.6 7.8 %collective-permute-done.2 = bf16[512,512]{0,1:T(8,128)(2,1)S(1)} collective-permute-done((bf16[512,512]{0,1:T(8,128)(2,1)S(1)}, bf16[512,512]{0,1:T(8,128)(2,1)S(1)}, u32[]{:S(2)}, u32[]{:S(2)}) %collective-permute-start.2) | collective-permute-done | bytes 524320 | tf_op jit(solution)/shard_map/ppermute | solution.py:360
  170.9 17.4 %collective-permute-done.10 = bf16[256,2048]{0,1:T(8,128)(2,1)S(1)} collective-permute-done((bf16[256,2048]{0,1:T(8,128)(2,1)S(1)}, bf16[256,2048]{0,1:T(8,128)(2,1)S(1)}, u32[]{:S(2)}, u32[]{:S(2)}) %collective-permute-start.10) | collective-permute-done | bytes 1048608 | tf_op jit(solution)/shard_map/ppermute | solution.py:349
  191.0 2.7 multiply_convert_fusion.3
  193.7 6.6 %fusion.13 = bf16[512,1024]{1,0:T(8,128)(2,1)S(1)} fusion(f32[512,1024]{1,0:T(8,128)S(1)} %get-tuple-element.159, bf16[1024,2048]{1,0:T(8,128)(2,1)} %param.22, bf16[256,2048]{1,0:T(8,128)(2,1)} %collective-permute-done.16, bf16[256,2048]{1,0:T(8,128)(2,1)} %param.23), kind=kOutput, calls=%fused_computation.42 | convolution fusion | flops 2162163712 | bytes 9437184 | tf_op jit(solution)/shard_map/dot_general | solution.py:174
  202.4 4.0 multiply_convert_fusion.1
  206.4 8.3 %fusion.27 = bf16[512,1024]{1,0:T(8,128)(2,1)} fusion(f32[512,1024]{1,0:T(8,128)} %get-tuple-element.155, bf16[1024,2048]{1,0:T(8,128)(2,1)} %param.22, bf16[256,2048]{1,0:T(8,128)(2,1)S(1)} %collective-permute-done.20, bf16[256,2048]{1,0:T(8,128)(2,1)} %collective-permute-done.18), kind=kOutput, calls=%fused_computation.56 | convolution fusion | flops 2162163712 | bytes 9437184 | tf_op jit(solution)/shard_map/dot_general | solution.py:174
  214.8 2.7 multiply_convert_fusion.2
  217.5 6.3 %fusion.20 = bf16[512,1024]{1,0:T(8,128)(2,1)S(1)} fusion(f32[512,1024]{1,0:T(8,128)S(1)} %get-tuple-element.157, bf16[1024,2048]{1,0:T(8,128)(2,1)} %param.22, bf16[256,2048]{1,0:T(8,128)(2,1)S(1)} %collective-permute-done.19, bf16[256,2048]{1,0:T(8,128)(2,1)} %collective-permute-done.17), kind=kOutput, calls=%fused_computation.49 | convolution fusion | flops 2162163712 | bytes 9437184 | tf_op jit(solution)/shard_map/dot_general | solution.py:174
  223.9 2.8 multiply_convert_fusion
  226.7 6.2 %fusion.34 = bf16[512,1024]{1,0:T(8,128)(2,1)S(1)} fusion(f32[512,1024]{1,0:T(8,128)S(1)} %get-tuple-element.153, bf16[1024,2048]{1,0:T(8,128)(2,1)} %param.22, bf16[256,2048]{1,0:T(8,128)(2,1)S(1)} %collective-permute-done.23, bf16[128,2048]{1,0:T(8,128)(2,1)S(1)} %collective-permute-done.22, bf16[128,2048]{1,0:T(8,128)(2,1)S(1)} %collective-permute-done.21), kind=kOutput, calls=%fused_computation.63 | convolution fusion | flops 2164260864 | bytes 9437184 | tf_op jit(solution)/shard_map/dot_general | solution.py:174
  232.9 7.6 %convolution_convert_fusion.3 = bf16[2048,512]{0,1:T(8,128)(2,1)} fusion(bf16[2048,1024]{1,0:T(8,128)(2,1)S(1)} %copy-done.27, s32[]{:T(128)S(6)} %select_n.102, bf16[512,1024]{1,0:T(8,128)(2,1)S(1)} %fusion.34, bf16[512,1024]{1,0:T(8,128)(2,1)S(1)} %copy-done.66, bf16[512,1024]{1,0:T(8,128)(2,1)S(1)} %fusion.20, bf16[512,1024]{1,0:T(8,128)(2,1)S(1)} %fusion.13), kind=kOutput, calls=%fused_computation.22 | convolution fusion | flops 2165309440 | bytes 7340036 | tf_op jit(solution)/shard_map/dot_general | solution.py:174
  241.1 4.9 convolution_convert_fusion.4
  251.2 6.5 %fusion.164 = f32[2048,512]{0,1:T(8,128)S(1)} fusion(bf16[2048,1024]{1,0:T(8,128)(2,1)S(1)} %copy-done.27, s32[]{:T(128)S(6)} %select_n.99, bf16[512,1024]{1,0:T(8,128)(2,1)} %copy-done.71, bf16[512,1024]{1,0:T(8,128)(2,1)S(1)} %copy-done.68, bf16[512,1024]{1,0:T(8,128)(2,1)} %copy-done.69, bf16[512,1024]{1,0:T(8,128)(2,1)S(1)} %fusion.13), kind=kOutput, calls=%fused_computation.229 | convolution fusion | flops 2164260864 | bytes 9437188 | tf_op jit(solution)/shard_map/dot_general | solution.py:174
  264.5 11.4 %convolution_convert_fusion = bf16[1024,2048]{1,0:T(8,128)(2,1)} fusion(bf16[2048,2048]{1,0:T(8,128)(2,1)S(1)} %bitcast.44, bf16[512,1024]{1,0:T(8,128)(2,1)S(1)} %get-tuple-element.152, bf16[512,1024]{1,0:T(8,128)(2,1)S(1)} %get-tuple-element.154, bf16[512,1024]{1,0:T(8,128)(2,1)S(1)} %get-tuple-element.156, bf16[512,1024]{1,0:T(8,128)(2,1)S(1)} %get-tuple-element.158), kind=kOutput, calls=%fused_computation.4 | convolution fusion | flops 8608808960 | bytes 16777216 | tf_op jit(solution)/shard_map/dot_general | solution.py:170
  275.9 2.5 constant_dynamic-update-slice_fusion.8
  282.3 2.6 constant_dynamic-update-slice_fusion.6
  284.9 3.8 collective-permute-done.25
  293.6 5.6 collective-permute-done.26
  310.6 15.9 %fusion.212 = (bf16[2048,1024]{0,1:T(8,128)(2,1)}, f32[2048]{0:T(1024)S(1)}) fusion(bf16[2048,1024]{0,1:T(8,128)(2,1)} %copy.60, bf16[2048,2048]{0,1:T(8,128)(2,1)} %constant_dynamic-update-slice_fusion.3, bf16[512,1024]{1,0:T(8,128)(2,1)} %copy-done.71, bf16[512,1024]{1,0:T(8,128)(2,1)} %fusion.27, bf16[512,1024]{1,0:T(8,128)(2,1)} %copy-done.69, ...), kind=kOutput, calls=%fused_computation.326 | convolution fusion | flops 8615098368 | bytes 20979712 | tf_op jit(solution)/shard_map/dot_general | solution.py:170
  326.6 7.8 %collective-permute-done.34 = bf16[256,2048]{0,1:T(8,128)(2,1)S(1)} collective-permute-done((bf16[256,2048]{0,1:T(8,128)(2,1)}, bf16[256,2048]{0,1:T(8,128)(2,1)S(1)}, u32[]{:S(2)}, u32[]{:S(2)}) %collective-permute-start.34) | collective-permute-done | bytes 1048608 | tf_op jit(solution)/shard_map/ppermute | solution.py:349
  334.4 3.7 pad_maximum_fusion
  364.0 19.7 %attn_bwd.1 = (bf16[2048,256]{1,0:T(8,128)(2,1)S(1)}, bf16[2048,256]{1,0:T(8,128)(2,1)S(1)}, bf16[2048,256]{1,0:T(8,128)(2,1)S(1)}) custom-call(s32[8]{0:T(128)S(1)} %broadcast_select_fusion.order_ref, bf16[2048,768]{1,0:T(8,128)(2,1)} %get-tuple-element.22.q_ref.k_ref.v_ref, bf16[2048,768]{1,0:T(8,128)(2,1)} %get-tuple-element.22.q_ref.k_ref.v_ref, ...), custom_call_target="tpu_custom_call" | custom-call | flops 5368709120 | bytes 8388608 | tf_op jit(solution)/shard_map/attn_bwd/pallas_call | solution.py:124
  384.0 5.3 convolution_convert_fusion.7
  390.6 5.1 convolution_convert_fusion.1
  395.7 3.4 convolution_convert_fusion.9
  399.0 11.8 %fusion.213 = (bf16[2048,768]{0,1:T(8,128)(2,1)}, f32[2048]{0:T(1024)S(1)}) fusion(bf16[2048,256]{0,1:T(8,128)(2,1)} %copy.57, bf16[2048,256]{0,1:T(8,128)(2,1)} %copy.56, bf16[2048,256]{0,1:T(8,128)(2,1)S(1)} %copy-done.31, bf16[2048,2048]{1,0:T(8,128)(2,1)} %get-tuple-element.30, bf16[2048,768]{1,0:T(8,128)(2,1)} %copy-done.55), kind=kOutput, calls=%fused_computation.327 | convolution fusion | flops 6456604672 | bytes 17833984 | tf_op jit(solution)/shard_map/dot_general | solution.py:170
  411.4 6.3 %convolution_convert_fusion.2 = bf16[2048,512]{0,1:T(8,128)(2,1)} fusion(bf16[2048,1024]{1,0:T(8,128)(2,1)} %pad_maximum_fusion, bf16[1024,2048]{1,0:T(8,128)(2,1)} %param.22, s32[]{:T(128)S(6)} %select_n.100), kind=kOutput, calls=%fused_computation.21 | convolution fusion | flops 2148532224 | bytes 7340036 | tf_op jit(solution)/shard_map/dot_general | solution.py:166
  417.7 4.5 convolution_convert_fusion.8
  422.5 4.5 fusion.158
  427.3 4.5 fusion.155
  432.1 4.2 fusion.167
  436.4 3.2 fusion.170
  451.6 4.9 collective-permute-done.52
  457.9 15.4 %collective-permute-done.49 = bf16[1024,512]{0,1:T(8,128)(2,1)S(1)} collective-permute-done((bf16[1024,512]{0,1:T(8,128)(2,1)S(1)}, bf16[1024,512]{0,1:T(8,128)(2,1)S(1)}, u32[]{:S(2)}, u32[]{:S(2)}) %collective-permute-start.49) | collective-permute-done | bytes 1048608 | tf_op jit(solution)/shard_map/ppermute | solution.py:360
  474.8 15.4 %collective-permute-done.41 = bf16[1024,512]{0,1:T(8,128)(2,1)S(1)} collective-permute-done((bf16[1024,512]{0,1:T(8,128)(2,1)S(1)}, bf16[1024,512]{0,1:T(8,128)(2,1)S(1)}, u32[]{:S(2)}, u32[]{:S(2)}) %collective-permute-start.41) | collective-permute-done | bytes 1048608 | tf_op jit(solution)/shard_map/ppermute | solution.py:360
  491.6 15.4 %collective-permute-done.44 = bf16[1024,512]{0,1:T(8,128)(2,1)S(1)} collective-permute-done((bf16[1024,512]{0,1:T(8,128)(2,1)S(1)}, bf16[1024,512]{0,1:T(8,128)(2,1)S(1)}, u32[]{:S(2)}, u32[]{:S(2)}) %collective-permute-start.44) | collective-permute-done | bytes 1048608 | tf_op jit(solution)/shard_map/ppermute | solution.py:360
  511.6 5.0 collective-permute-done.45
  519.8 2.9 convert_select_fusion.1
  530.2 2.8 convert_element_type.422
  533.0 2.6 copy.66
  545.2 2.6 collective-permute-start.60
  547.8 3.9 fusion.6
  (416 shorter events, 172.1 us)
Async XLA Ops:
  7.2 523.0 %reduce-scatter.11.cloned.1.call-start = ((), (), s32[]{:S(2)}) async-start(), calls=%async_computation.7 | async-start | bytes 5242880 | tf_op jit(solution)/shard_map/reduce_scatter | solution.py:458
  71.4 34.9 %collective-permute-start.3 = (bf16[2048,512]{0,1:T(8,128)(2,1)}, bf16[2048,512]{0,1:T(8,128)(2,1)}, u32[]{:S(2)}, u32[]{:S(2)}) collective-permute-start(bf16[2048,512]{0,1:T(8,128)(2,1)} %convolution_convert_fusion.5), channel_id=1, source_target_pairs={{0,1},{1,0},{2,3},{3,2},{4,5},{5,4},{6,7},{7,6},{8,9},{9,8},{10,11... | collective-permute-start | bytes 6291464 | tf_op jit(solution)/shard_map/ppermute | solution.py:360
  75.0 34.8 %collective-permute-start = (bf16[2048,512]{0,1:T(8,128)(2,1)}, bf16[2048,512]{0,1:T(8,128)(2,1)}, u32[]{:S(2)}, u32[]{:S(2)}) collective-permute-start(bf16[2048,512]{0,1:T(8,128)(2,1)} %convolution_convert_fusion.6), channel_id=1, source_target_pairs={{0,1},{1,0},{2,3},{3,2},{4,5},{5,4},{6,7},{7,6},{8,9},{9,8},{10,11... | collective-permute-start | bytes 6291464 | tf_op jit(solution)/shard_map/ppermute | solution.py:360
  75.0 40.8 %collective-permute-start.18 = (bf16[256,2048]{1,0:T(8,128)(2,1)}, bf16[256,2048]{1,0:T(8,128)(2,1)}, u32[]{:S(2)}, u32[]{:S(2)}) collective-permute-start(bf16[256,2048]{1,0:T(8,128)(2,1)} %param.23), channel_id=1, source_target_pairs={{0,4},{1,3},{2,6},{3,1},{4,0},{5,7},{6,2},{7,5},{8,12},{9,11},{10,... | collective-permute-start | bytes 3145736 | tf_op jit(solution)/shard_map/ppermute | solution.py:349
  75.8 42.0 %collective-permute-start.17 = (bf16[256,2048]{1,0:T(8,128)(2,1)}, bf16[256,2048]{1,0:T(8,128)(2,1)}, u32[]{:S(2)}, u32[]{:S(2)}) collective-permute-start(bf16[256,2048]{1,0:T(8,128)(2,1)} %param.23), channel_id=1, source_target_pairs={{0,2},{1,5},{2,0},{3,7},{4,6},{5,1},{6,4},{7,3},{8,10},{9,13},{10,... | collective-permute-start | bytes 3145736 | tf_op jit(solution)/shard_map/ppermute | solution.py:349
  77.1 43.1 %collective-permute-start.16 = (bf16[256,2048]{1,0:T(8,128)(2,1)}, bf16[256,2048]{1,0:T(8,128)(2,1)}, u32[]{:S(2)}, u32[]{:S(2)}) collective-permute-start(bf16[256,2048]{1,0:T(8,128)(2,1)} %param.23), channel_id=1, source_target_pairs={{0,1},{1,0},{2,3},{3,2},{4,5},{5,4},{6,7},{7,6},{8,9},{9,8},{10,11... | collective-permute-start | bytes 3145736 | tf_op jit(solution)/shard_map/ppermute | solution.py:349
  108.3 18.5 %collective-permute-start.4 = (bf16[1024,512]{0,1:T(8,128)(2,1)S(1)}, bf16[1024,512]{0,1:T(8,128)(2,1)S(1)}, u32[]{:S(2)}, u32[]{:S(2)}) collective-permute-start(bf16[1024,512]{0,1:T(8,128)(2,1)S(1)} %fusion.45), channel_id=1, source_target_pairs={{0,4},{1,3},{2,6},{3,1},{4,0},{5,7},{6,2},{7,5},{8,12},{9,11},{10,... | collective-permute-start | bytes 3145736 | tf_op jit(solution)/shard_map/ppermute | solution.py:360
  111.9 33.7 %collective-permute-start.1 = (bf16[1024,512]{0,1:T(8,128)(2,1)S(1)}, bf16[1024,512]{0,1:T(8,128)(2,1)S(1)}, u32[]{:S(2)}, u32[]{:S(2)}) collective-permute-start(bf16[1024,512]{0,1:T(8,128)(2,1)S(1)} %fusion.46), channel_id=1, source_target_pairs={{0,4},{1,3},{2,6},{3,1},{4,0},{5,7},{6,2},{7,5},{8,12},{9,11},{10,... | collective-permute-start | bytes 3145736 | tf_op jit(solution)/shard_map/ppermute | solution.py:360
  116.9 40.1 %collective-permute-start.22 = (bf16[128,2048]{1,0:T(8,128)(2,1)S(1)}, bf16[128,2048]{1,0:T(8,128)(2,1)S(1)}, u32[]{:S(2)}, u32[]{:S(2)}) collective-permute-start(bf16[128,2048]{1,0:T(8,128)(2,1)S(1)} %slice.629), channel_id=1, source_target_pairs={{0,2},{1,5},{2,0},{3,7},{4,6},{5,1},{6,4},{7,3},{8,10},{9,13},{10,... | collective-permute-start | bytes 1572872 | tf_op jit(solution)/shard_map/ppermute | solution.py:349
  118.8 38.5 %collective-permute-start.21 = (bf16[128,2048]{1,0:T(8,128)(2,1)S(1)}, bf16[128,2048]{1,0:T(8,128)(2,1)S(1)}, u32[]{:S(2)}, u32[]{:S(2)}) collective-permute-start(bf16[128,2048]{1,0:T(8,128)(2,1)S(1)} %slice.628), channel_id=1, source_target_pairs={{0,4},{1,3},{2,6},{3,1},{4,0},{5,7},{6,2},{7,5},{8,12},{9,11},{10,... | collective-permute-start | bytes 1572872 | tf_op jit(solution)/shard_map/ppermute | solution.py:349
  120.2 37.6 %collective-permute-start.19 = (bf16[256,2048]{1,0:T(8,128)(2,1)}, bf16[256,2048]{1,0:T(8,128)(2,1)S(1)}, u32[]{:S(2)}, u32[]{:S(2)}) collective-permute-start(bf16[256,2048]{1,0:T(8,128)(2,1)} %collective-permute-done.18), channel_id=1, source_target_pairs={{0,1},{1,0},{2,3},{3,2},{4,5},{5,4},{6,7},{7,6},{8,9},{9,8},{10,11... | collective-permute-start | bytes 3145736 | tf_op jit(solution)/shard_map/ppermute | solution.py:349
  127.0 21.1 %collective-permute-start.5 = (bf16[512,512]{0,1:T(8,128)(2,1)S(1)}, bf16[512,512]{0,1:T(8,128)(2,1)S(1)}, u32[]{:S(2)}, u32[]{:S(2)}) collective-permute-start(bf16[512,512]{0,1:T(8,128)(2,1)S(1)} %fusion.147), channel_id=1, source_target_pairs={{0,2},{1,5},{2,0},{3,7},{4,6},{5,1},{6,4},{7,3},{8,10},{9,13},{10,... | collective-permute-start | bytes 1572872 | tf_op jit(solution)/shard_map/ppermute | solution.py:360
  148.1 18.9 %collective-permute-start.20 = (bf16[256,2048]{1,0:T(8,128)(2,1)}, bf16[256,2048]{1,0:T(8,128)(2,1)S(1)}, u32[]{:S(2)}, u32[]{:S(2)}) collective-permute-start(bf16[256,2048]{1,0:T(8,128)(2,1)} %collective-permute-done.17), channel_id=1, source_target_pairs={{0,1},{1,0},{2,3},{3,2},{4,5},{5,4},{6,7},{7,6},{8,9},{9,8},{10,11... | collective-permute-start | bytes 3145736 | tf_op jit(solution)/shard_map/ppermute | solution.py:349
  157.4 12.4 %collective-permute-start.23 = (bf16[256,2048]{1,0:T(8,128)(2,1)S(1)}, bf16[256,2048]{1,0:T(8,128)(2,1)S(1)}, u32[]{:S(2)}, u32[]{:S(2)}) collective-permute-start(bf16[256,2048]{1,0:T(8,128)(2,1)S(1)} %pad_maximum_fusion.7), channel_id=1, source_target_pairs={{0,1},{1,0},{2,3},{3,2},{4,5},{5,4},{6,7},{7,6},{8,9},{9,8},{10,11... | collective-permute-start | bytes 3145736 | tf_op jit(solution)/shard_map/ppermute | solution.py:349
  162.6 25.8 %collective-permute-start.10 = (bf16[256,2048]{0,1:T(8,128)(2,1)S(1)}, bf16[256,2048]{0,1:T(8,128)(2,1)S(1)}, u32[]{:S(2)}, u32[]{:S(2)}) collective-permute-start(bf16[256,2048]{0,1:T(8,128)(2,1)S(1)} %get-tuple-element.63), channel_id=1, source_target_pairs={{0,4},{1,3},{2,6},{3,1},{4,0},{5,7},{6,2},{7,5},{8,12},{9,11},{10,... | collective-permute-start | bytes 3145736 | tf_op jit(solution)/shard_map/ppermute | solution.py:349
  164.1 25.2 %collective-permute-start.9 = (bf16[256,2048]{0,1:T(8,128)(2,1)S(1)}, bf16[256,2048]{0,1:T(8,128)(2,1)S(1)}, u32[]{:S(2)}, u32[]{:S(2)}) collective-permute-start(bf16[256,2048]{0,1:T(8,128)(2,1)S(1)} %get-tuple-element.63), channel_id=1, source_target_pairs={{0,2},{1,5},{2,0},{3,7},{4,6},{5,1},{6,4},{7,3},{8,10},{9,13},{10,... | collective-permute-start | bytes 3145736 | tf_op jit(solution)/shard_map/ppermute | solution.py:349
  164.6 26.4 %collective-permute-start.8 = (bf16[256,2048]{0,1:T(8,128)(2,1)S(1)}, bf16[256,2048]{0,1:T(8,128)(2,1)S(1)}, u32[]{:S(2)}, u32[]{:S(2)}) collective-permute-start(bf16[256,2048]{0,1:T(8,128)(2,1)S(1)} %get-tuple-element.63), channel_id=1, source_target_pairs={{0,1},{1,0},{2,3},{3,2},{4,5},{5,4},{6,7},{7,6},{8,9},{9,8},{10,11... | collective-permute-start | bytes 3145736 | tf_op jit(solution)/shard_map/ppermute | solution.py:349
  188.4 13.8 %collective-permute-start.14 = (bf16[128,2048]{0,1:T(8,128)(2,1)S(1)}, bf16[128,2048]{0,1:T(8,128)(2,1)S(1)}, u32[]{:S(2)}, u32[]{:S(2)}) collective-permute-start(bf16[128,2048]{0,1:T(8,128)(2,1)S(1)} %slice.627), channel_id=1, source_target_pairs={{0,2},{1,5},{2,0},{3,7},{4,6},{5,1},{6,4},{7,3},{8,10},{9,13},{10,... | collective-permute-start | bytes 1572872 | tf_op jit(solution)/shard_map/ppermute | solution.py:349
  189.3 12.9 %collective-permute-start.13 = (bf16[128,2048]{0,1:T(8,128)(2,1)S(1)}, bf16[128,2048]{0,1:T(8,128)(2,1)S(1)}, u32[]{:S(2)}, u32[]{:S(2)}) collective-permute-start(bf16[128,2048]{0,1:T(8,128)(2,1)S(1)} %slice.626), channel_id=1, source_target_pairs={{0,4},{1,3},{2,6},{3,1},{4,0},{5,7},{6,2},{7,5},{8,12},{9,11},{10,... | collective-permute-start | bytes 1572872 | tf_op jit(solution)/shard_map/ppermute | solution.py:349
  190.5 24.3 %collective-permute-start.11 = (bf16[256,2048]{0,1:T(8,128)(2,1)S(1)}, bf16[256,2048]{0,1:T(8,128)(2,1)S(1)}, u32[]{:S(2)}, u32[]{:S(2)}) collective-permute-start(bf16[256,2048]{0,1:T(8,128)(2,1)S(1)} %collective-permute-done.10), channel_id=1, source_target_pairs={{0,1},{1,0},{2,3},{3,2},{4,5},{5,4},{6,7},{7,6},{8,9},{9,8},{10,11... | collective-permute-start | bytes 3145736 | tf_op jit(solution)/shard_map/ppermute | solution.py:349
  190.5 11.9 %collective-permute-start.12 = (bf16[256,2048]{0,1:T(8,128)(2,1)S(1)}, bf16[256,2048]{0,1:T(8,128)(2,1)S(1)}, u32[]{:S(2)}, u32[]{:S(2)}) collective-permute-start(bf16[256,2048]{0,1:T(8,128)(2,1)S(1)} %collective-permute-done.9), channel_id=1, source_target_pairs={{0,1},{1,0},{2,3},{3,2},{4,5},{5,4},{6,7},{7,6},{8,9},{9,8},{10,11... | collective-permute-start | bytes 3145736 | tf_op jit(solution)/shard_map/ppermute | solution.py:349
  202.3 21.6 %collective-permute-start.15 = (bf16[256,2048]{0,1:T(8,128)(2,1)S(1)}, bf16[256,2048]{0,1:T(8,128)(2,1)S(1)}, u32[]{:S(2)}, u32[]{:S(2)}) collective-permute-start(bf16[256,2048]{0,1:T(8,128)(2,1)S(1)} %pad_maximum_fusion.6), channel_id=1, source_target_pairs={{0,1},{1,0},{2,3},{3,2},{4,5},{5,4},{6,7},{7,6},{8,9},{9,8},{10,11... | collective-permute-start | bytes 3145736 | tf_op jit(solution)/shard_map/ppermute | solution.py:349
  240.6 17.2 %collective-permute-start.27 = (bf16[2048,512]{0,1:T(8,128)(2,1)}, bf16[2048,512]{0,1:T(8,128)(2,1)S(1)}, u32[]{:S(2)}, u32[]{:S(2)}) collective-permute-start(bf16[2048,512]{0,1:T(8,128)(2,1)} %convolution_convert_fusion.3), channel_id=1, source_target_pairs={{0,1},{1,0},{2,3},{3,2},{4,5},{5,4},{6,7},{7,6},{8,9},{9,8},{10,11... | collective-permute-start | bytes 6291464 | tf_op jit(solution)/shard_map/ppermute | solution.py:360
  246.0 15.1 %collective-permute-start.24 = (bf16[2048,512]{0,1:T(8,128)(2,1)}, bf16[2048,512]{0,1:T(8,128)(2,1)S(1)}, u32[]{:S(2)}, u32[]{:S(2)}) collective-permute-start(bf16[2048,512]{0,1:T(8,128)(2,1)} %convolution_convert_fusion.4), channel_id=1, source_target_pairs={{0,1},{1,0},{2,3},{3,2},{4,5},{5,4},{6,7},{7,6},{8,9},{9,8},{10,11... | collective-permute-start | bytes 6291464 | tf_op jit(solution)/shard_map/ppermute | solution.py:360
  260.0 19.5 %collective-permute-start.28 = (bf16[1024,512]{0,1:T(8,128)(2,1)}, bf16[1024,512]{0,1:T(8,128)(2,1)}, u32[]{:S(2)}, u32[]{:S(2)}) collective-permute-start(bf16[1024,512]{0,1:T(8,128)(2,1)} %fusion.43), channel_id=1, source_target_pairs={{0,4},{1,3},{2,6},{3,1},{4,0},{5,7},{6,2},{7,5},{8,12},{9,11},{10,... | collective-permute-start | bytes 3145736 | tf_op jit(solution)/shard_map/ppermute | solution.py:360
  263.5 25.1 %collective-permute-start.25 = (bf16[1024,512]{0,1:T(8,128)(2,1)}, bf16[1024,512]{0,1:T(8,128)(2,1)}, u32[]{:S(2)}, u32[]{:S(2)}) collective-permute-start(bf16[1024,512]{0,1:T(8,128)(2,1)} %fusion.44), channel_id=1, source_target_pairs={{0,4},{1,3},{2,6},{3,1},{4,0},{5,7},{6,2},{7,5},{8,12},{9,11},{10,... | collective-permute-start | bytes 3145736 | tf_op jit(solution)/shard_map/ppermute | solution.py:360
  275.9 257.1 %reduce-scatter.9.cloned.1.call-start = ((), (), s32[]{:S(2)}) async-start(), calls=%async_computation.6 | async-start | bytes 5242880 | tf_op jit(solution)/shard_map/reduce_scatter | solution.py:461
  281.2 10.8 %collective-permute-start.29 = (bf16[512,512]{0,1:T(8,128)(2,1)S(1)}, bf16[512,512]{0,1:T(8,128)(2,1)S(1)}, u32[]{:S(2)}, u32[]{:S(2)}) collective-permute-start(bf16[512,512]{0,1:T(8,128)(2,1)S(1)} %fusion.139), channel_id=1, source_target_pairs={{0,2},{1,5},{2,0},{3,7},{4,6},{5,1},{6,4},{7,3},{8,10},{9,13},{10,... | collective-permute-start | bytes 1572872 | tf_op jit(solution)/shard_map/ppermute | solution.py:360
  308.4 26.0 %collective-permute-start.34 = (bf16[256,2048]{0,1:T(8,128)(2,1)}, bf16[256,2048]{0,1:T(8,128)(2,1)S(1)}, u32[]{:S(2)}, u32[]{:S(2)}) collective-permute-start(bf16[256,2048]{0,1:T(8,128)(2,1)} %get-tuple-element.61), channel_id=1, source_target_pairs={{0,4},{1,3},{2,6},{3,1},{4,0},{5,7},{6,2},{7,5},{8,12},{9,11},{10,... | collective-permute-start | bytes 3145736 | tf_op jit(solution)/shard_map/ppermute | solution.py:349
  309.5 29.9 %collective-permute-start.33 = (bf16[256,2048]{0,1:T(8,128)(2,1)}, bf16[256,2048]{0,1:T(8,128)(2,1)}, u32[]{:S(2)}, u32[]{:S(2)}) collective-permute-start(bf16[256,2048]{0,1:T(8,128)(2,1)} %get-tuple-element.61), channel_id=1, source_target_pairs={{0,2},{1,5},{2,0},{3,7},{4,6},{5,1},{6,4},{7,3},{8,10},{9,13},{10,... | collective-permute-start | bytes 3145736 | tf_op jit(solution)/shard_map/ppermute | solution.py:349
  310.6 31.2 %collective-permute-start.32 = (bf16[256,2048]{0,1:T(8,128)(2,1)}, bf16[256,2048]{0,1:T(8,128)(2,1)}, u32[]{:S(2)}, u32[]{:S(2)}) collective-permute-start(bf16[256,2048]{0,1:T(8,128)(2,1)} %get-tuple-element.61), channel_id=1, source_target_pairs={{0,1},{1,0},{2,3},{3,2},{4,5},{5,4},{6,7},{7,6},{8,9},{9,8},{10,11... | collective-permute-start | bytes 3145736 | tf_op jit(solution)/shard_map/ppermute | solution.py:349
  334.4 18.7 %collective-permute-start.35 = (bf16[256,2048]{0,1:T(8,128)(2,1)S(1)}, bf16[256,2048]{0,1:T(8,128)(2,1)}, u32[]{:S(2)}, u32[]{:S(2)}) collective-permute-start(bf16[256,2048]{0,1:T(8,128)(2,1)S(1)} %collective-permute-done.34), channel_id=1, source_target_pairs={{0,1},{1,0},{2,3},{3,2},{4,5},{5,4},{6,7},{7,6},{8,9},{9,8},{10,11... | collective-permute-start | bytes 3145736 | tf_op jit(solution)/shard_map/ppermute | solution.py:349
  338.1 197.5 %reduce-scatter.7.cloned.1.call-start = ((), (), s32[]{:S(2)}) async-start(), calls=%async_computation.5 | async-start | bytes 1310720 | tf_op jit(solution)/shard_map/reduce_scatter | solution.py:468
  338.2 13.3 %collective-permute-start.38 = (bf16[128,2048]{0,1:T(8,128)(2,1)S(1)}, bf16[128,2048]{0,1:T(8,128)(2,1)S(1)}, u32[]{:S(2)}, u32[]{:S(2)}) collective-permute-start(bf16[128,2048]{0,1:T(8,128)(2,1)S(1)} %slice.661), channel_id=1, source_target_pairs={{0,2},{1,5},{2,0},{3,7},{4,6},{5,1},{6,4},{7,3},{8,10},{9,13},{10,... | collective-permute-start | bytes 1572872 | tf_op jit(solution)/shard_map/ppermute | solution.py:349
  340.5 12.1 %collective-permute-start.37 = (bf16[128,2048]{0,1:T(8,128)(2,1)S(1)}, bf16[128,2048]{0,1:T(8,128)(2,1)S(1)}, u32[]{:S(2)}, u32[]{:S(2)}) collective-permute-start(bf16[128,2048]{0,1:T(8,128)(2,1)S(1)} %slice.660), channel_id=1, source_target_pairs={{0,4},{1,3},{2,6},{3,1},{4,0},{5,7},{6,2},{7,5},{8,12},{9,11},{10,... | collective-permute-start | bytes 1572872 | tf_op jit(solution)/shard_map/ppermute | solution.py:349
  341.9 14.7 %collective-permute-start.36 = (bf16[256,2048]{0,1:T(8,128)(2,1)}, bf16[256,2048]{0,1:T(8,128)(2,1)S(1)}, u32[]{:S(2)}, u32[]{:S(2)}) collective-permute-start(bf16[256,2048]{0,1:T(8,128)(2,1)} %collective-permute-done.33), channel_id=1, source_target_pairs={{0,1},{1,0},{2,3},{3,2},{4,5},{5,4},{6,7},{7,6},{8,9},{9,8},{10,11... | collective-permute-start | bytes 3145736 | tf_op jit(solution)/shard_map/ppermute | solution.py:349
  389.3 50.3 %collective-permute-start.51 = (bf16[2048,512]{0,1:T(8,128)(2,1)}, bf16[2048,512]{0,1:T(8,128)(2,1)}, u32[]{:S(2)}, u32[]{:S(2)}) collective-permute-start(bf16[2048,512]{0,1:T(8,128)(2,1)} %convolution_convert_fusion.7), channel_id=1, source_target_pairs={{0,1},{1,0},{2,3},{3,2},{4,5},{5,4},{6,7},{7,6},{8,9},{9,8},{10,11... | collective-permute-start | bytes 6291464 | tf_op jit(solution)/shard_map/ppermute | solution.py:360
  410.9 146.4 %reduce-scatter.5.cloned.1.call-start = ((), (), s32[]{:S(2)}) async-start(), calls=%async_computation.4 | async-start | bytes 3932160 | tf_op jit(solution)/shard_map/reduce_scatter | solution.py:480
  422.2 20.6 %collective-permute-start.48 = (bf16[2048,512]{0,1:T(8,128)(2,1)}, bf16[2048,512]{0,1:T(8,128)(2,1)}, u32[]{:S(2)}, u32[]{:S(2)}) collective-permute-start(bf16[2048,512]{0,1:T(8,128)(2,1)} %convolution_convert_fusion.8), channel_id=1, source_target_pairs={{0,1},{1,0},{2,3},{3,2},{4,5},{5,4},{6,7},{7,6},{8,9},{9,8},{10,11... | collective-permute-start | bytes 6291464 | tf_op jit(solution)/shard_map/ppermute | solution.py:360
  427.1 18.8 %collective-permute-start.40 = (bf16[2048,512]{0,1:T(8,128)(2,1)}, bf16[2048,512]{0,1:T(8,128)(2,1)}, u32[]{:S(2)}, u32[]{:S(2)}) collective-permute-start(bf16[2048,512]{0,1:T(8,128)(2,1)} %convolution_convert_fusion.2), channel_id=1, source_target_pairs={{0,1},{1,0},{2,3},{3,2},{4,5},{5,4},{6,7},{7,6},{8,9},{9,8},{10,11... | collective-permute-start | bytes 6291464 | tf_op jit(solution)/shard_map/ppermute | solution.py:360
  431.8 17.3 %collective-permute-start.43 = (bf16[2048,512]{0,1:T(8,128)(2,1)}, bf16[2048,512]{0,1:T(8,128)(2,1)S(1)}, u32[]{:S(2)}, u32[]{:S(2)}) collective-permute-start(bf16[2048,512]{0,1:T(8,128)(2,1)} %convolution_convert_fusion.1), channel_id=1, source_target_pairs={{0,1},{1,0},{2,3},{3,2},{4,5},{5,4},{6,7},{7,6},{8,9},{9,8},{10,11... | collective-permute-start | bytes 6291464 | tf_op jit(solution)/shard_map/ppermute | solution.py:360
  441.6 14.9 %collective-permute-start.52 = (bf16[1024,512]{0,1:T(8,128)(2,1)S(1)}, bf16[1024,512]{0,1:T(8,128)(2,1)S(1)}, u32[]{:S(2)}, u32[]{:S(2)}) collective-permute-start(bf16[1024,512]{0,1:T(8,128)(2,1)S(1)} %fusion.39), channel_id=1, source_target_pairs={{0,4},{1,3},{2,6},{3,1},{4,0},{5,7},{6,2},{7,5},{8,12},{9,11},{10,... | collective-permute-start | bytes 3145736 | tf_op jit(solution)/shard_map/ppermute | solution.py:360
  444.8 28.5 %collective-permute-start.49 = (bf16[1024,512]{0,1:T(8,128)(2,1)S(1)}, bf16[1024,512]{0,1:T(8,128)(2,1)S(1)}, u32[]{:S(2)}, u32[]{:S(2)}) collective-permute-start(bf16[1024,512]{0,1:T(8,128)(2,1)S(1)} %fusion.40), channel_id=1, source_target_pairs={{0,4},{1,3},{2,6},{3,1},{4,0},{5,7},{6,2},{7,5},{8,12},{9,11},{10,... | collective-permute-start | bytes 3145736 | tf_op jit(solution)/shard_map/ppermute | solution.py:360
  448.1 42.1 %collective-permute-start.41 = (bf16[1024,512]{0,1:T(8,128)(2,1)S(1)}, bf16[1024,512]{0,1:T(8,128)(2,1)S(1)}, u32[]{:S(2)}, u32[]{:S(2)}) collective-permute-start(bf16[1024,512]{0,1:T(8,128)(2,1)S(1)} %fusion.42), channel_id=1, source_target_pairs={{0,4},{1,3},{2,6},{3,1},{4,0},{5,7},{6,2},{7,5},{8,12},{9,11},{10,... | collective-permute-start | bytes 3145736 | tf_op jit(solution)/shard_map/ppermute | solution.py:360
  450.6 56.4 %collective-permute-start.44 = (bf16[1024,512]{0,1:T(8,128)(2,1)S(1)}, bf16[1024,512]{0,1:T(8,128)(2,1)S(1)}, u32[]{:S(2)}, u32[]{:S(2)}) collective-permute-start(bf16[1024,512]{0,1:T(8,128)(2,1)S(1)} %fusion.41), channel_id=1, source_target_pairs={{0,4},{1,3},{2,6},{3,1},{4,0},{5,7},{6,2},{7,5},{8,12},{9,11},{10,... | collective-permute-start | bytes 3145736 | tf_op jit(solution)/shard_map/ppermute | solution.py:360
  456.7 51.8 %collective-permute-start.53 = (bf16[512,512]{0,1:T(8,128)(2,1)S(1)}, bf16[512,512]{0,1:T(8,128)(2,1)S(1)}, u32[]{:S(2)}, u32[]{:S(2)}) collective-permute-start(bf16[512,512]{0,1:T(8,128)(2,1)S(1)} %fusion.123), channel_id=1, source_target_pairs={{0,2},{1,5},{2,0},{3,7},{4,6},{5,1},{6,4},{7,3},{8,10},{9,13},{10,... | collective-permute-start | bytes 1572872 | tf_op jit(solution)/shard_map/ppermute | solution.py:360
  473.6 35.4 %collective-permute-start.50 = (bf16[512,512]{0,1:T(8,128)(2,1)S(1)}, bf16[512,512]{0,1:T(8,128)(2,1)S(1)}, u32[]{:S(2)}, u32[]{:S(2)}) collective-permute-start(bf16[512,512]{0,1:T(8,128)(2,1)S(1)} %fusion.127), channel_id=1, source_target_pairs={{0,2},{1,5},{2,0},{3,7},{4,6},{5,1},{6,4},{7,3},{8,10},{9,13},{10,... | collective-permute-start | bytes 1572872 | tf_op jit(solution)/shard_map/ppermute | solution.py:360
  490.4 20.1 %collective-permute-start.42 = (bf16[512,512]{0,1:T(8,128)(2,1)S(1)}, bf16[512,512]{0,1:T(8,128)(2,1)S(1)}, u32[]{:S(2)}, u32[]{:S(2)}) collective-permute-start(bf16[512,512]{0,1:T(8,128)(2,1)S(1)} %fusion.135), channel_id=1, source_target_pairs={{0,2},{1,5},{2,0},{3,7},{4,6},{5,1},{6,4},{7,3},{8,10},{9,13},{10,... | collective-permute-start | bytes 1572872 | tf_op jit(solution)/shard_map/ppermute | solution.py:360
  (98 other events, 981.8 us)
Sparse Core Ops, SparseCore 0:
  276.0 77.2 reduce-scatter.10
  355.7 77.2 reduce-scatter.8
  435.3 27.6 reduce-scatter.6
  465.2 58.9 reduce-scatter.4

commit v3 on v2

v3 whole, which is shorter than its diff:
```python
import functools

import jax
import jax.numpy as jnp
from jax import lax
from jax.experimental import pallas as pl
from jax.experimental.pallas import tpu as pltpu
from jax.sharding import PartitionSpec as P

HD = 128
NEGATIVE = -1e30
LOG2E = 1.4426950408889634
EPSILON = 1e-05
BF = jnp.bfloat16
F32 = jnp.float32
MIB = 2**20


def dot_nn(a, b):
    return jnp.dot(a, b, preferred_element_type=F32)


def dot_tn(a, b):
    return lax.dot_general(a, b, (((0,), (0,)), ((), ())), preferred_element_type=F32)


def dot_nt(a, b):
    return lax.dot_general(a, b, (((1,), (1,)), ((), ())), preferred_element_type=F32)


def diagonal(blk):
    rows = lax.broadcasted_iota(jnp.int32, (blk, blk), 0)
    cols = lax.broadcasted_iota(jnp.int32, (blk, blk), 1)
    return cols < rows, cols == rows


def attend_head(blk, count, place, queries, keys, values, rk_ref, ck_ref, put_mixed, put_lse, ks, vs):
    c = HD ** -0.5 * LOG2E
    for a in range(count):
        ks[a * blk:(a + 1) * blk, :] = keys(place(a))
        vs[a * blk:(a + 1) * blk, :] = values(place(a))
    earlier, itself = diagonal(blk)
    for a in range(count):
        end = (a + 1) * blk
        low = end - blk
        s = dot_nt(queries(place(a)), ks[:end, :])
        ok = rk_ref[low:end, :] == ck_ref[:, :end]
        sd = jnp.where((ok[:, low:] & earlier) | itself, s[:, low:], NEGATIVE)
        m = jnp.max(sd, axis=1, keepdims=True)
        if a:
            so = jnp.where(ok[:, :low], s[:, :low], NEGATIVE)
            m = jnp.maximum(m, jnp.max(so, axis=1, keepdims=True))
        pd = jnp.exp2((sd - m) * c)
        total = jnp.sum(pd, axis=1, keepdims=True)
        o = dot_nn(pd.astype(BF), vs[low:end, :])
        if a:
            po = jnp.exp2((so - m) * c)
            total += jnp.sum(po, axis=1, keepdims=True)
            o += dot_nn(po.astype(BF), vs[:low, :])
        put_mixed(place(a), (o / total).astype(BF))
        put_lse(a, m * c + jnp.log2(total))


def attn_fwd_body(blk, count, order_ref, q_ref, k_ref, v_ref, rk_ref, ck_ref, mix_ref, lse_ref, ks, vs):
    def place(a):
        return pl.multiple_of(order_ref[a] * blk, blk)

    def put_mixed(at, value):
        mix_ref[pl.ds(at, blk), :] = value

    def put_lse(a, value):
        lse_ref[0, a * blk:(a + 1) * blk, :] = value

    attend_head(
        blk, count, place, lambda at: q_ref[pl.ds(at, blk), :], lambda at: k_ref[pl.ds(at, blk), :],
        lambda at: v_ref[pl.ds(at, blk), :], rk_ref, ck_ref, put_mixed, put_lse, ks, vs,
    )


def attn_fwd(qkv, order, rowkey, colkey, heads, blk):
    seq = qkv.shape[0]
    part = lambda off: pl.BlockSpec((seq, HD), lambda h, o: (0, off * heads + h))
    return pl.pallas_call(
        functools.partial(attn_fwd_body, blk, seq // blk), name="attn_fwd",
        grid_spec=pltpu.PrefetchScalarGridSpec(
            num_scalar_prefetch=1, grid=(heads,),
            in_specs=[part(0), part(1), part(2), pl.BlockSpec((seq, 1), lambda h, o: (0, 0)),
                      pl.BlockSpec((1, seq), lambda h, o: (0, 0))],
            out_specs=[part(0), pl.BlockSpec((1, seq, 1), lambda h, o: (h, 0, 0))],
            scratch_shapes=[pltpu.VMEM((seq, HD), BF)] * 2),
        out_shape=[jax.ShapeDtypeStruct((seq, heads * HD), BF), jax.ShapeDtypeStruct((heads, seq, 1), F32)],
        compiler_params=pltpu.CompilerParams(vmem_limit_bytes=48 * MIB),
        cost_estimate=pl.CostEstimate(
            flops=2 * seq * seq * HD * heads, bytes_accessed=8 * seq * HD * heads, transcendentals=seq * seq * heads // 2),
    )(order, qkv, qkv, qkv, rowkey, colkey)


def unattend_head(blk, count, place, queries, keys, values, grads, mixes, lses, rk_ref, ck_ref, put_q, put_k, put_v, ks, vs, dks, dvs,
                  between=None):
    scale = HD ** -0.5
    c = scale * LOG2E
    for a in range(count):
        ks[a * blk:(a + 1) * blk, :] = keys(place(a))
        vs[a * blk:(a + 1) * blk, :] = values(place(a))
    earlier, itself = diagonal(blk)

    def add(ref, lo, hi, value, fresh):
        if fresh:
            ref[lo:hi, :] = value
        else:
            ref[lo:hi, :] += value

    for a in reversed(range(count)):
        end = (a + 1) * blk
        low = end - blk
        fresh = a == count - 1
        at = place(a)
        q, do = queries(at), grads(at)
        delta = jnp.sum(do.astype(F32) * mixes(at).astype(F32), axis=1, keepdims=True)
        p = jnp.exp2(dot_nt(q, ks[:end, :]) * c - lses(a))
        dp = dot_nt(do, vs[:end, :])
        ok = rk_ref[low:end, :] == ck_ref[:, :end]
        pd = jnp.where((ok[:, low:] & earlier) | itself, p[:, low:], 0.0)
        dsd = (pd * (dp[:, low:] - delta)).astype(BF)
        dq = dot_nn(dsd, ks[low:end, :])
        add(dks, low, end, dot_tn(dsd, q), fresh)
        add(dvs, low, end, dot_tn(pd.astype(BF), do), fresh)
        if a:
            po = jnp.where(ok[:, :low], p[:, :low], 0.0)
            dso = (po * (dp[:, :low] - delta)).astype(BF)
            dq += dot_nn(dso, ks[:low, :])
            add(dks, 0, low, dot_tn(dso, q), fresh)
            add(dvs, 0, low, dot_tn(po.astype(BF), do), fresh)
        put_q(at, (dq * scale).astype(BF))
        if between is not None:
            between(a)
    for a in range(count):
        put_k(place(a), (dks[a * blk:(a + 1) * blk, :] * scale).astype(BF))
        put_v(place(a), dvs[a * blk:(a + 1) * blk, :].astype(BF))


def attn_bwd_body(blk, count, order_ref, q_ref, k_ref, v_ref, do_ref, mix_ref, lse_ref, rk_ref, ck_ref, dq_ref, dk_ref, dv_ref,
                  ks, vs, dks, dvs):
    def place(a):
        return pl.multiple_of(order_ref[a] * blk, blk)

    def load(ref):
        return lambda at: ref[pl.ds(at, blk), :]

    def save(ref):
        def put(at, value):
            ref[pl.ds(at, blk), :] = value
        return put

    unattend_head(
        blk, count, place, load(q_ref), load(k_ref), load(v_ref), load(do_ref), load(mix_ref),
        lambda a: lse_ref[0, a * blk:(a + 1) * blk, :], rk_ref, ck_ref, save(dq_ref), save(dk_ref), save(dv_ref), ks, vs, dks, dvs,
    )


def attn_bwd(qkv, do, mixed, lse, order, rowkey, colkey, heads, blk):
    seq = qkv.shape[0]
    part = lambda off: pl.BlockSpec((seq, HD), lambda h, o: (0, off * heads + h))
    return pl.pallas_call(
        functools.partial(attn_bwd_body, blk, seq // blk), name="attn_bwd",
        grid_spec=pltpu.PrefetchScalarGridSpec(
            num_scalar_prefetch=1, grid=(heads,),
            in_specs=[part(0), part(1), part(2), part(0), part(0), pl.BlockSpec((1, seq, 1), lambda h, o: (h, 0, 0)),
                      pl.BlockSpec((seq, 1), lambda h, o: (0, 0)), pl.BlockSpec((1, seq), lambda h, o: (0, 0))],
            out_specs=[part(0), part(0), part(0)],
            scratch_shapes=[pltpu.VMEM((seq, HD), BF)] * 2 + [pltpu.VMEM((seq, HD), F32)] * 2),
        out_shape=[jax.ShapeDtypeStruct((seq, heads * HD), BF)] * 3,
        compiler_params=pltpu.CompilerParams(vmem_limit_bytes=56 * MIB),
        cost_estimate=pl.CostEstimate(
            flops=5 * seq * seq * HD * heads, bytes_accessed=16 * seq * HD * heads, transcendentals=seq * seq * heads // 2),
    )(order, qkv, qkv, qkv, do, mixed, lse, rowkey, colkey)


def row_scale(values):
    return lax.rsqrt(jnp.mean(values * values, axis=-1, keepdims=True) + EPSILON)


def norm_rows(values, norm_gain):
    return values * row_scale(values) * norm_gain


def norm_back(values, norm_gain, grad_norm):
    scale = row_scale(values)
    normal = values * scale
    grad_hat = grad_norm * norm_gain
    inner = jnp.mean(grad_hat * normal, axis=-1, keepdims=True)
    return scale * (grad_hat - normal * inner)


def gelu_fn(values):
    return jax.nn.gelu(values, approximate=True)


MESH = pl.DeviceIdType.MESH
HBM_SPACE = pl.ANY
VMEM_SPACE = pltpu.VMEM


def neighbours():
    dp, me = lax.axis_index("dp"), lax.axis_index("mp")
    core, along_x, along_y = me % 2, (me // 2) % 2, me // 4
    by_x, by_y = me + 2 - 4 * along_x, me + 4 - 8 * along_y
    first = (1 - core) * by_y + core * by_x
    second = (1 - core) * by_x + core * by_y
    return core, (dp, me + 1 - 2 * core), (dp, first), (dp, second)


def greet(*others):
    barrier = pltpu.get_barrier_semaphore()
    for other in others:
        pl.semaphore_signal(barrier, inc=1, device_id=other, device_id_type=MESH)
    pl.semaphore_wait(barrier, len(others))


class Gather:
    COPIES = 11

    def __init__(self, buf, sends, recvs, sib, first, second):
        rows = buf.shape[1]
        low, high, whole = pl.ds(0, rows // 2), pl.ds(rows // 2, rows // 2), pl.ds(0, rows)

        def copy(i, source, target, part, device):
            return pltpu.make_async_remote_copy(
                src_ref=buf.at[source, part], dst_ref=buf.at[target, part],
                send_sem=sends.at[i], recv_sem=recvs.at[i], device_id=device, device_id_type=MESH,
            )

        self.copies = [
            copy(0, 0, 4, high, first), copy(1, 0, 4, low, first),
            copy(2, 0, 2, low, second), copy(3, 0, 2, high, second),
            copy(4, 0, 1, whole, sib),
            copy(5, 2, 6, low, first), copy(6, 4, 6, high, second),
            copy(7, 4, 3, whole, sib), copy(8, 2, 5, whole, sib),
            copy(9, 6, 7, low, sib), copy(10, 6, 7, high, sib),
        ]

    def start(self):
        for i in (0, 2, 1, 3, 4):
            self.copies[i].start()

    def pair(self):
        self.copies[4].wait_recv()

    def forward(self):
        for arrived, onward in ((2, 5), (0, 6)):
            self.copies[arrived].wait_recv()
            self.copies[onward].start()
        for arrived, onward in ((1, 7), (3, 8)):
            self.copies[arrived].wait_recv()
            self.copies[onward].start()

    def middle(self):
        self.copies[7].wait_recv()
        self.copies[8].wait_recv()

    def finish(self):
        for arrived, onward in ((5, 9), (6, 10)):
            self.copies[arrived].wait_recv()
            self.copies[onward].start()
        self.copies[9].wait_recv()
        self.copies[10].wait_recv()

    def drain(self):
        for one in self.copies:
            one.wait_send()


def norm_store(rows_ref, gain_ref, store, step=32):
    def some(i, carry):
        part = pl.ds(pl.multiple_of(i * step, step), step)
        store(part, norm_rows(rows_ref[part, :].astype(F32), gain_ref[...]).astype(BF))
        return carry

    lax.fori_loop(0, rows_ref.shape[0] // step, some, 0)


def project_body(tok_hbm, gain_ref, wq_hbm, wk_hbm, wv_hbm, qkv_hbm, normed_hbm, tok_ref, w_ref, qkv_ref, buf, sends, recvs, locals_):
    core, sib, first, second = neighbours()
    rows = tok_ref.shape[0]
    width = wq_hbm.shape[1]
    fetch = [pltpu.make_async_copy(tok_hbm, tok_ref, locals_.at[16])]
    for k, w_hbm in enumerate((wq_hbm, wk_hbm, wv_hbm)):
        fetch.append(pltpu.make_async_copy(w_hbm, w_ref.at[:, pl.ds(k * width, width)], locals_.at[17 + k]))
    for one in fetch:
        one.start()
    greet(sib, first, second)
    fetch[0].wait()

    def keep(part, value):
        buf[0, part, :] = value

    norm_store(tok_ref, gain_ref, keep)
    ring = Gather(buf, sends, recvs, sib, first, second)
    ring.start()
    for one in fetch[1:]:
        one.wait()

    def moved(s):
        at = pl.ds(pl.multiple_of(s * rows, rows), rows)
        return (
            pltpu.make_async_copy(buf.at[s], normed_hbm.at[at], locals_.at[s]),
            pltpu.make_async_copy(qkv_ref.at[at], qkv_hbm.at[at], locals_.at[8 + s]),
        )

    def slot(s, carry):
        at = pl.ds(pl.multiple_of(s * rows, rows), rows)
        normed_out, qkv_out = moved(s)
        normed_out.start()
        qkv_ref[at, :] = dot_nn(buf[s], w_ref[...]).astype(BF)
        qkv_out.start()
        return carry

    ring.pair()
    lax.fori_loop(0, 2, slot, 0)
    ring.forward()
    ring.middle()
    lax.fori_loop(2, 6, slot, 0)
    ring.finish()
    lax.fori_loop(6, 8, slot, 0)
    for s in range(8):
        for one in moved(s):
            one.wait()
    ring.drain()


def project(tokens, gain, w_query, w_key, w_value):
    rows, width = tokens.shape
    cols = w_query.shape[1]
    hbm = pl.BlockSpec(memory_space=HBM_SPACE)
    return pl.pallas_call(
        project_body, name="gather_project",
        in_specs=[hbm, pl.BlockSpec(memory_space=VMEM_SPACE), hbm, hbm, hbm],
        out_specs=[hbm, hbm],
        out_shape=[jax.ShapeDtypeStruct((8 * rows, 3 * cols), BF), jax.ShapeDtypeStruct((8 * rows, width), BF)],
        scratch_shapes=[
            pltpu.VMEM((rows, width), BF), pltpu.VMEM((width, 3 * cols), BF), pltpu.VMEM((8 * rows, 3 * cols), BF),
            pltpu.VMEM((8, rows, width), BF), pltpu.SemaphoreType.DMA((11,)), pltpu.SemaphoreType.DMA((11,)),
            pltpu.SemaphoreType.DMA((20,)),
        ],
        compiler_params=pltpu.CompilerParams(collective_id=1, has_side_effects=True, vmem_limit_bytes=58 * 2**20),
        cost_estimate=pl.CostEstimate(flops=2 * 8 * rows * width * 3 * cols, bytes_accessed=60 * 2**20, transcendentals=0),
    )(tokens, gain[None, :], w_query, w_key, w_value)

class Scatter:
    def __init__(self, product, own_ref, bufs, sems, core, sib, first, second):
        self.product, self.own_ref, self.core = product, own_ref, core
        self.away_ref, self.r0, self.s1, self.r1, self.s2, self.r2, self.s3, self.r3 = bufs
        self.chunks, _, self.rows, self.step = self.away_ref.shape
        self.half = self.chunks * self.step
        sends, recvs = sems

        def copy(source, target, j, k, device):
            return pltpu.make_async_remote_copy(
                src_ref=source.at[j], dst_ref=target.at[j], send_sem=sends.at[j, k], recv_sem=recvs.at[j, k],
                device_id=device, device_id_type=MESH,
            )

        self.copies = [
            [copy(self.away_ref, self.r0, j, 0, sib), copy(self.s1, self.r1, j, 1, first),
             copy(self.s2, self.r2, j, 2, second), copy(self.s3, self.r3, j, 3, sib)]
            for j in range(self.chunks)
        ]

    def column(self, j, core):
        return pl.multiple_of(core * self.half + j * self.step, self.step)

    def away(self, j):
        col = self.column(j, 1 - self.core)

        def some(p, carry):
            self.away_ref[j, p] = self.product(p, col).astype(BF)
            return carry

        lax.fori_loop(0, 8, some, 0)
        self.copies[j][0].start()

    def kept(self, j, p):
        came = 4 * ((p // 2) % 2) + 2 * (p // 4) + 1 - p % 2
        return self.product(p, self.column(j, self.core)) + self.r0[j, came].astype(F32)

    def one(self, j):
        self.copies[j][0].wait_recv()

        def some(p, carry):
            self.s1[j, p - 4] = self.kept(j, p).astype(BF)
            return carry

        lax.fori_loop(4, 8, some, 0)
        self.copies[j][1].start()

    def two(self, j):
        self.copies[j][1].wait_recv()

        def some(p, carry):
            self.s2[j, p - 2] = (self.kept(j, p) + self.r1[j, p].astype(F32)).astype(BF)
            return carry

        lax.fori_loop(2, 4, some, 0)
        self.copies[j][2].start()

    def three(self, j):
        self.copies[j][2].wait_recv()

        def last(p):
            return self.kept(j, p) + self.r1[j, p].astype(F32) + self.r2[j, p].astype(F32)

        self.s3[j] = last(1).astype(BF)
        self.copies[j][3].start()
        self.own_ref[:, pl.ds(self.column(j, self.core), self.step)] = last(0)

    def four(self, j):
        self.copies[j][3].wait_recv()
        self.own_ref[:, pl.ds(self.column(j, 1 - self.core), self.step)] = self.r3[j].astype(F32)

    def each(self, stage):
        for j in range(self.chunks):
            stage(j)

    def drain(self):
        for copies in self.copies:
            for one in copies:
                one.wait_send()


def scatter_scratch(rows, width, chunks):
    step = width // 2 // chunks
    sizes = [(8, rows, step)] * 2 + [(4, rows, step)] * 2 + [(2, rows, step)] * 2 + [(rows, step)] * 2
    return [pltpu.VMEM((chunks,) + size, BF) for size in sizes] + [pltpu.SemaphoreType.DMA((chunks, 4))] * 2


def gather_scratch(rows, width):
    return [pltpu.VMEM((8, rows, width), BF), pltpu.SemaphoreType.DMA((11,)), pltpu.SemaphoreType.DMA((11,))]


def rows_loop(rows, step, body):
    def some(i, carry):
        body(pl.ds(pl.multiple_of(i * step, step), step))
        return carry

    lax.fori_loop(0, rows // step, some, 0)


def block_place(a, rows):
    me = lax.axis_index("mp")
    core = me % 2
    by_c = (a % 2 + core) % 2
    by_x = (a // 2 + me // 2) % 2
    by_y = (a // 4 + me // 4) % 2
    position = 4 * (by_y + core * (by_x - by_y)) + 2 * (by_x + core * (by_y - by_x)) + by_c
    return pl.multiple_of(position * rows, rows)


def forward_body(
    heads, qkv_hbm, grad_hbm, tok_hbm, w_out_hbm, w_up_hbm, gain_ref, rk_ref, ck_ref,
    mixed_hbm, lse_ref, attn_hbm, normed_hbm, hidden_hbm, rows_hbm,
    qkv, tok, w_out, w_up, mixed, own, hidden, ks, vs, loads, stores,
    nbuf, nsend, nrecv, gbuf, gsend, grecv, *scatter,
):
    core, sib, first, second = neighbours()
    rows, width = tok.shape
    local = pltpu.make_async_copy
    fetch = [
        local(grad_hbm, gbuf.at[0], loads.at[0]), local(qkv_hbm, qkv, loads.at[1]), local(w_out_hbm, w_out, loads.at[2]),
        local(tok_hbm, tok, loads.at[3]), local(w_up_hbm, w_up, loads.at[4]),
    ]
    for one in fetch:
        one.start()
    greet(sib, first, second)
    fetch[0].wait()
    grads = Gather(gbuf, gsend, grecv, sib, first, second)
    grads.start()
    fetch[1].wait()

    def head(h, carry):
        def part(k):
            return lambda at: qkv[pl.ds(at, rows), pl.ds(pl.multiple_of((k * heads + h) * HD, HD), HD)]

        def put_mixed(at, value):
            mixed[pl.ds(at, rows), pl.ds(pl.multiple_of(h * HD, HD), HD)] = value

        def put_lse(a, value):
            lse_ref[h, a * rows:(a + 1) * rows, :] = value

        attend_head(rows, 8, lambda a: block_place(a, rows), part(0), part(1), part(2), rk_ref, ck_ref, put_mixed, put_lse, ks, vs)
        return carry

    lax.fori_loop(0, heads, head, 0)
    mixed_out = local(mixed, mixed_hbm, stores.at[0])
    mixed_out.start()

    def product(p, col):
        return dot_nn(mixed[pl.ds(pl.multiple_of(p * rows, rows), rows), :], w_out[:, pl.ds(col, net.step)])

    fetch[2].wait()
    net = Scatter(product, own, scatter[:8], scatter[8:], core, sib, first, second)
    for stage in (net.away, net.one, net.two, net.three, net.four):
        net.each(stage)
    attn_out = local(own, attn_hbm, stores.at[1])
    attn_out.start()

    fetch[3].wait()

    def norm(part):
        residual = tok[part, :].astype(F32) + own[part, :]
        nbuf[0, part, :] = norm_rows(residual, gain_ref[...]).astype(BF)

    rows_loop(rows, 32, norm)
    ring = Gather(nbuf, nsend, nrecv, sib, first, second)
    ring.start()
    fetch[4].wait()
    cols = hidden.shape[1]
    tile = min(512, cols)

    def moved(s):
        at = pl.ds(pl.multiple_of(s * rows, rows), rows)
        return (
            local(nbuf.at[s], normed_hbm.at[at], stores.at[2 + s]),
            local(hidden.at[at], hidden_hbm.at[at], stores.at[10 + s]),
        )

    def slot(s, carry):
        at = pl.ds(pl.multiple_of(s * rows, rows), rows)
        normed_out, hidden_out = moved(s)
        normed_out.start()

        def some(t, inner):
            col = pl.ds(pl.multiple_of(t * tile, tile), tile)
            hidden[at, col] = gelu_fn(dot_nn(nbuf[s], w_up[:, col])).astype(BF)
            return inner

        lax.fori_loop(0, cols // tile, some, 0)
        hidden_out.start()
        return carry

    ring.pair()
    lax.fori_loop(0, 2, slot, 0)
    ring.forward()
    grads.pair()
    grads.forward()
    ring.middle()
    lax.fori_loop(2, 6, slot, 0)
    ring.finish()
    lax.fori_loop(6, 8, slot, 0)
    grads.middle()
    grads.finish()
    copies = [local(gbuf.at[s], rows_hbm.at[pl.ds(s * rows, rows)], stores.at[18 + s]) for s in range(8)]
    for one in copies:
        one.start()
    for s in range(8):
        copies.extend(moved(s))
    for one in copies + [mixed_out, attn_out]:
        one.wait()
    ring.drain()
    grads.drain()
    net.drain()


def forward(qkv, grad_out, tokens, w_out, w_up, gain, row_key, col_key, heads):
    rows, width = tokens.shape
    seq, hidden = 8 * rows, w_up.shape[1]
    hbm, vmem = pl.BlockSpec(memory_space=HBM_SPACE), pl.BlockSpec(memory_space=VMEM_SPACE)
    shape = jax.ShapeDtypeStruct
    return pl.pallas_call(
        functools.partial(forward_body, heads), name="forward_layer",
        in_specs=[hbm] * 5 + [vmem] * 3,
        out_specs=[hbm, vmem, hbm, hbm, hbm, hbm],
        out_shape=[
            shape((seq, heads * HD), BF), shape((heads, seq, 1), F32), shape((rows, width), F32), shape((seq, width), BF),
            shape((seq, hidden), BF), shape((seq, width), BF),
        ],
        scratch_shapes=[
            pltpu.VMEM((seq, 3 * heads * HD), BF), pltpu.VMEM((rows, width), BF), pltpu.VMEM((heads * HD, width), BF),
            pltpu.VMEM((width, hidden), BF), pltpu.VMEM((seq, heads * HD), BF), pltpu.VMEM((rows, width), F32),
            pltpu.VMEM((seq, hidden), BF), pltpu.VMEM((seq, HD), BF), pltpu.VMEM((seq, HD), BF),
            pltpu.SemaphoreType.DMA((5,)), pltpu.SemaphoreType.DMA((26,)),
        ] + gather_scratch(rows, width) * 2 + scatter_scratch(rows, width, 2),
        compiler_params=pltpu.CompilerParams(collective_id=2, has_side_effects=True, vmem_limit_bytes=62 * MIB),
        cost_estimate=pl.CostEstimate(flops=40 * 10**9, bytes_accessed=250 * MIB, transcendentals=0),
    )(qkv, grad_out, tokens, w_out, w_up, gain[None, :], row_key, col_key)

def gelu_slope(x):
    c = 0.7978845608028654
    square = x * x
    t = jnp.tanh(c * (x + 0.044715 * (x * square)))
    return 0.5 * (1.0 + t) + 0.5 * x * (1.0 - t * t) * (c * (1.0 + 3 * 0.044715 * square))


def row_sums(product):
    ones = jnp.ones((8, product.shape[1]), F32)
    return lax.dot_general(
        ones, product, (((1,), (1,)), ((), ())), preferred_element_type=F32, precision=lax.Precision.HIGHEST
    )[0:1]


def middle_body(
    hidden_hbm, w_down_hbm, w_up_hbm, normed_hbm, grads_hbm,
    mlp_hbm, dnorm_hbm, up_hbm, gain_ref,
    hidden, w_down, w_up, pre, normed, grads, tiles, ups, mlp, dnorm, loads, stores, *scatter,
):
    core, sib, first, second = neighbours()
    rows, width = mlp.shape
    inner = hidden.shape[1]
    local = pltpu.make_async_copy
    fetch = [
        local(source, target, loads.at[i])
        for i, (source, target) in enumerate(((hidden_hbm, hidden), (w_down_hbm, w_down), (w_up_hbm, w_up)))
    ]

    def at(p):
        return pl.ds(pl.multiple_of(p * rows, rows), rows)

    def block(s):
        return (
            local(normed_hbm.at[at(s)], normed.at[s % 2], loads.at[3 + s % 2]),
            local(grads_hbm.at[at(s)], grads.at[s % 2], loads.at[5 + s % 2]),
        )

    for one in fetch:
        one.start()
    for one in block(0):
        one.start()
    greet(sib, first, second)

    def down(p, col):
        return dot_nn(hidden[at(p), :], w_down[:, pl.ds(col, net.step)])

    def up_back(p, col):
        return dot_nt(pre[at(p), :], w_up[pl.ds(col, net.step), :])

    net = Scatter(down, mlp, scatter[:8], scatter[8:10], core, sib, first, second)
    back = Scatter(up_back, dnorm, scatter[10:18], scatter[18:], core, sib, first, second)
    fetch[0].wait()
    fetch[1].wait()
    net.each(net.away)
    net.each(net.one)
    fetch[2].wait()
    part = min(512, inner)

    def slopes(s, carry):
        for one in block(s):
            one.wait()

        @pl.when(s < 7)
        def _():
            for one in block(s + 1):
                one.start()

        def some(t, more):
            col = pl.ds(pl.multiple_of(t * part, part), part)
            slope = gelu_slope(dot_nn(normed[s % 2], w_up[:, col]))
            pre[at(s), col] = (slope * dot_nt(grads[s % 2], w_down[col, :])).astype(BF)
            return more

        lax.fori_loop(0, inner // part, some, 0)
        return carry

    lax.fori_loop(0, 8, slopes, 0)
    tile = tiles.shape[2]

    def load_tile(t):
        return local(normed_hbm.at[:, pl.ds(pl.multiple_of(t * tile, tile), tile)], tiles.at[t % 2], loads.at[7 + t % 2])

    def save_tile(t):
        return local(ups.at[t % 2], up_hbm.at[pl.ds(pl.multiple_of(t * tile, tile), tile)], stores.at[2 + t % 2])

    load_tile(0).start()
    net.each(net.two)
    back.each(back.away)
    back.each(back.one)
    net.each(net.three)

    def weight(t, carry):
        load_tile(t).wait()

        @pl.when(t < width // tile - 1)
        def _():
            load_tile(t + 1).start()

        @pl.when(t >= 2)
        def _():
            save_tile(t - 2).wait()

        value = dot_tn(tiles[t % 2], pre[...])
        ups[t % 2] = value.astype(BF)
        save_tile(t).start()
        gain_ref[:, pl.ds(pl.multiple_of(t * tile, tile), tile)] = row_sums(
            value * w_up[pl.ds(pl.multiple_of(t * tile, tile), tile), :].astype(F32)
        )
        return carry

    lax.fori_loop(0, width // tile, weight, 0)
    net.each(net.four)
    outs = [local(mlp, mlp_hbm, stores.at[0])]
    outs[0].start()
    for name in ("two", "three", "four"):
        back.each(getattr(back, name))
    outs.append(local(dnorm, dnorm_hbm, stores.at[1]))
    outs[1].start()
    for one in outs:
        one.wait()
    save_tile(width // tile - 2).wait()
    save_tile(width // tile - 1).wait()
    net.drain()
    back.drain()


def middle(hidden, w_down, w_up, normed, grads):
    seq, inner = hidden.shape
    width = w_down.shape[1]
    rows = seq // 8
    tile = 256
    hbm, vmem = pl.BlockSpec(memory_space=HBM_SPACE), pl.BlockSpec(memory_space=VMEM_SPACE)
    shape = jax.ShapeDtypeStruct
    return pl.pallas_call(
        middle_body, name="middle_layer",
        in_specs=[hbm] * 5,
        out_specs=[hbm] * 3 + [vmem],
        out_shape=[shape((rows, width), F32), shape((rows, width), F32), shape((width, inner), BF), shape((1, width), F32)],
        scratch_shapes=[
            pltpu.VMEM((seq, inner), BF), pltpu.VMEM((inner, width), BF), pltpu.VMEM((width, inner), BF),
            pltpu.VMEM((seq, inner), BF), pltpu.VMEM((2, rows, width), BF), pltpu.VMEM((2, rows, width), BF),
            pltpu.VMEM((2, seq, tile), BF), pltpu.VMEM((2, tile, inner), BF), pltpu.VMEM((rows, width), F32),
            pltpu.VMEM((rows, width), F32), pltpu.SemaphoreType.DMA((9,)), pltpu.SemaphoreType.DMA((4,)),
        ] + scatter_scratch(rows, width, 2) * 2,
        compiler_params=pltpu.CompilerParams(collective_id=5, has_side_effects=True, vmem_limit_bytes=63 * MIB),
        cost_estimate=pl.CostEstimate(flops=45 * 10**9, bytes_accessed=200 * MIB, transcendentals=0),
    )(hidden, w_down, w_up, normed, grads)


def turn_body(
    heads, dnorm_hbm, attn_hbm, tok_hbm, grad_hbm, w_out_hbm, qkv_hbm, mixed_hbm, gain_ref, lse_ref, rk_ref, ck_ref,
    branch_hbm, dqkv_hbm, residual_hbm,
    own, attn, tok, grad, w_out, qkv, mixed, dmixed, dqkv, ks, vs, dks, dvs, loads, stores, bbuf, bsend, brecv,
):
    core, sib, first, second = neighbours()
    rows, width = tok.shape
    local = pltpu.make_async_copy
    fetch = [
        local(source, target, loads.at[i])
        for i, (source, target) in enumerate((
            (dnorm_hbm, own), (attn_hbm, attn), (tok_hbm, tok), (grad_hbm, grad), (w_out_hbm, w_out), (qkv_hbm, qkv),
            (mixed_hbm, mixed),
        ))
    ]
    for one in fetch:
        one.start()
    greet(sib, first, second)
    for one in fetch[:4]:
        one.wait()

    def norm(part):
        residual = tok[part, :].astype(F32) + attn[part, :]
        total = grad[part, :].astype(F32) + norm_back(residual, gain_ref[...], own[part, :])
        own[part, :] = total
        bbuf[0, part, :] = total.astype(BF)

    rows_loop(rows, 32, norm)
    ring = Gather(bbuf, bsend, brecv, sib, first, second)
    ring.start()
    residual_out = local(own, residual_hbm, stores.at[0])
    residual_out.start()
    fetch[4].wait()

    def moved(s):
        return local(bbuf.at[s], branch_hbm.at[pl.ds(pl.multiple_of(s * rows, rows), rows)], stores.at[2 + s])

    def slot(s, carry):
        moved(s).start()
        dmixed[pl.ds(pl.multiple_of(s * rows, rows), rows), :] = dot_nt(bbuf[s], w_out[...]).astype(BF)
        return carry

    ring.pair()
    lax.fori_loop(0, 2, slot, 0)
    ring.forward()
    ring.middle()
    lax.fori_loop(2, 6, slot, 0)
    ring.finish()
    lax.fori_loop(6, 8, slot, 0)
    fetch[5].wait()
    fetch[6].wait()

    def head(h, carry):
        def load(ref, k):
            return lambda at: ref[pl.ds(at, rows), pl.ds(pl.multiple_of((k * heads + h) * HD, HD), HD)]

        def save(k):
            def put(at, value):
                dqkv[pl.ds(at, rows), pl.ds(pl.multiple_of((k * heads + h) * HD, HD), HD)] = value
            return put

        unattend_head(
            rows, 8, lambda a: block_place(a, rows), load(qkv, 0), load(qkv, 1), load(qkv, 2), load(dmixed, 0), load(mixed, 0),
            lambda a: lse_ref[h, a * rows:(a + 1) * rows, :], rk_ref, ck_ref, save(0), save(1), save(2), ks, vs, dks, dvs,
        )
        return carry

    lax.fori_loop(0, heads, head, 0)
    dqkv_out = local(dqkv, dqkv_hbm, stores.at[1])
    dqkv_out.start()
    for s in range(8):
        moved(s).wait()
    residual_out.wait()
    dqkv_out.wait()
    ring.drain()


def turn(dnorm, attn_own, tokens, grad_out, w_out, qkv, mixed, gain, lse, row_key, col_key, heads):
    rows, width = tokens.shape
    seq = 8 * rows
    hbm, vmem = pl.BlockSpec(memory_space=HBM_SPACE), pl.BlockSpec(memory_space=VMEM_SPACE)
    shape = jax.ShapeDtypeStruct
    cols = heads * HD
    return pl.pallas_call(
        functools.partial(turn_body, heads), name="turn_layer",
        in_specs=[hbm] * 7 + [vmem] * 4,
        out_specs=[hbm] * 3,
        out_shape=[shape((seq, width), BF), shape((seq, 3 * cols), BF), shape((rows, width), F32)],
        scratch_shapes=[
            pltpu.VMEM((rows, width), F32), pltpu.VMEM((rows, width), F32), pltpu.VMEM((rows, width), BF),
            pltpu.VMEM((rows, width), BF), pltpu.VMEM((cols, width), BF), pltpu.VMEM((seq, 3 * cols), BF),
            pltpu.VMEM((seq, cols), BF), pltpu.VMEM((seq, cols), BF), pltpu.VMEM((seq, 3 * cols), BF),
            pltpu.VMEM((seq, HD), BF), pltpu.VMEM((seq, HD), BF), pltpu.VMEM((seq, HD), F32), pltpu.VMEM((seq, HD), F32),
            pltpu.SemaphoreType.DMA((7,)), pltpu.SemaphoreType.DMA((10,)),
        ] + gather_scratch(rows, width),
        compiler_params=pltpu.CompilerParams(collective_id=3, has_side_effects=True, vmem_limit_bytes=60 * MIB),
        cost_estimate=pl.CostEstimate(flops=45 * 10**9, bytes_accessed=200 * MIB, transcendentals=0),
    )(dnorm, attn_own, tokens, grad_out, w_out, qkv, mixed, gain[None, :], lse, row_key, col_key)


def weights_body(normed_ref, branch_ref, dqkv_ref, mixed_ref, wq_ref, wk_ref, wv_ref, out_ref, gain_ref):
    cols = wq_ref.shape[1]
    value = dot_tn(normed_ref[...], dqkv_ref[...])
    out_ref[:, :3 * cols] = value.astype(BF)
    out_ref[:, 3 * cols:] = dot_tn(branch_ref[...], mixed_ref[...]).astype(BF)
    gain_ref[...] = sum(
        row_sums(value[:, k * cols:(k + 1) * cols] * w_ref[...].astype(F32))
        for k, w_ref in enumerate((wq_ref, wk_ref, wv_ref))
    )


def weights(normed, branch, dqkv, mixed, w_query, w_key, w_value):
    seq, width = normed.shape
    cols = w_query.shape[1]
    tile = 256
    full = lambda c: pl.BlockSpec((seq, c), lambda t: (0, 0))
    strip = pl.BlockSpec((seq, tile), lambda t: (0, t))
    rows = pl.BlockSpec((tile, cols), lambda t: (t, 0))
    return pl.pallas_call(
        weights_body, name="weight_gradients", grid=(width // tile,),
        in_specs=[strip, strip, full(3 * cols), full(cols), rows, rows, rows],
        out_specs=[pl.BlockSpec((tile, 4 * cols), lambda t: (t, 0)), pl.BlockSpec((1, tile), lambda t: (0, t))],
        out_shape=[jax.ShapeDtypeStruct((width, 4 * cols), BF), jax.ShapeDtypeStruct((1, width), F32)],
        compiler_params=pltpu.CompilerParams(vmem_limit_bytes=48 * MIB),
        cost_estimate=pl.CostEstimate(flops=2 * seq * width * 4 * cols, bytes_accessed=30 * MIB, transcendentals=0),
    )(normed, branch, dqkv, mixed, w_query, w_key, w_value)


def finish_body(dqkv_hbm, wq_hbm, wk_hbm, wv_hbm, dnorm_hbm, dqkv, w_qkv, dnorm, loads, stores, *scatter):
    core, sib, first, second = neighbours()
    rows = dnorm.shape[0]
    cols = wq_hbm.shape[1]
    local = pltpu.make_async_copy
    pairs = [(dqkv_hbm, dqkv)]
    pairs += [(w, w_qkv.at[:, pl.ds(k * cols, cols)]) for k, w in enumerate((wq_hbm, wk_hbm, wv_hbm))]
    fetch = [local(source, target, loads.at[i]) for i, (source, target) in enumerate(pairs)]
    for one in fetch:
        one.start()
    greet(sib, first, second)

    def project_back(p, col):
        return dot_nt(dqkv[pl.ds(pl.multiple_of(p * rows, rows), rows), :], w_qkv[pl.ds(col, net.step), :])

    net = Scatter(project_back, dnorm, scatter[:8], scatter[8:], core, sib, first, second)
    for one in fetch:
        one.wait()
    for stage in (net.away, net.one, net.two, net.three, net.four):
        net.each(stage)
    out = local(dnorm, dnorm_hbm, stores.at[0])
    out.start()
    out.wait()
    net.drain()


def finish(dqkv, w_query, w_key, w_value):
    seq = dqkv.shape[0]
    width, cols = w_query.shape
    rows = seq // 8
    hbm = pl.BlockSpec(memory_space=HBM_SPACE)
    return pl.pallas_call(
        finish_body, name="last_scatter",
        in_specs=[hbm] * 4,
        out_specs=hbm,
        out_shape=jax.ShapeDtypeStruct((rows, width), F32),
        scratch_shapes=[
            pltpu.VMEM((seq, 3 * cols), BF), pltpu.VMEM((width, 3 * cols), BF), pltpu.VMEM((rows, width), F32),
            pltpu.SemaphoreType.DMA((4,)), pltpu.SemaphoreType.DMA((1,)),
        ] + scatter_scratch(rows, width, 2),
        compiler_params=pltpu.CompilerParams(collective_id=4, has_side_effects=True, vmem_limit_bytes=48 * MIB),
        cost_estimate=pl.CostEstimate(flops=20 * 10**9, bytes_accessed=100 * MIB, transcendentals=0),
    )(dqkv, w_query, w_key, w_value)


def after(value, *others):
    return lax.optimization_barrier((value,) + others)[0]


def over_mp(value):
    return lax.all_gather(value, "mp", axis=0, tiled=True)


def sum_mp(value):
    return lax.psum_scatter(value.astype(BF), "mp", scatter_dimension=0, tiled=True).astype(F32)


def sum_dp(value, axis):
    return lax.psum_scatter(value.astype(BF), "dp", scatter_dimension=axis, tiled=True).astype(F32)


def small_total(vector, n_dp):
    for axis, count in (("mp", 8), ("dp", n_dp)):
        bit = 1
        while bit < count:
            vector = vector + lax.ppermute(vector, axis, [(i, i ^ bit) for i in range(count)])
            bit *= 2
    return vector


def on_device(tokens, segment, valid, gain_attn, w_query, w_key, w_value, w_out, gain_mlp, w_up, w_down, grad_out):
    own_rows, width = tokens.shape
    seq_rows = segment.shape[0]
    heads = w_query.shape[1] // HD
    n_dp, n_mp = lax.axis_size("dp"), lax.axis_size("mp")
    dp, me = lax.axis_index("dp"), lax.axis_index("mp")
    cube = n_mp == 8 and n_dp & (n_dp - 1) == 0
    order = jnp.arange(seq_rows // own_rows, dtype=jnp.int32)
    valid_group = lax.dynamic_slice_in_dim(valid, dp * seq_rows, seq_rows)
    valid_own = lax.dynamic_slice_in_dim(valid_group, me * own_rows, own_rows)
    row_key = segment[:, None]
    col_key = jnp.where(valid_group > 0, segment, -1)[None, :]
    tokens32 = tokens.astype(F32)

    if cube:
        qkv, normed = project(tokens, gain_attn, w_query, w_key, w_value)
        mixed, lse, attn_own, normed_mlp, hidden, grad_rows = forward(
            qkv, grad_out, tokens, w_out, w_up, gain_mlp, row_key, col_key, heads
        )
    else:
        normed = over_mp(norm_rows(tokens32, gain_attn).astype(BF))
        qkv = jnp.concatenate([dot_nn(normed, w).astype(BF) for w in (w_query, w_key, w_value)], 1)
        mixed, lse = attn_fwd(qkv, order, row_key, col_key, heads, own_rows)
        grad_rows = over_mp(after(grad_out, qkv))
        attn_own = sum_mp(dot_nn(mixed, w_out))
        normed_mlp = over_mp(norm_rows(tokens32 + attn_own, gain_mlp).astype(BF))
        hidden = gelu_fn(dot_nn(normed_mlp, w_up)).astype(BF)
    residual = tokens32 + attn_own

    part_down = dot_tn(hidden, grad_rows).astype(BF)
    grad_down = sum_dp(part_down, 1)
    if cube:
        mlp_own, grad_normed, part_up, gain_mlp_part = middle(
            hidden, w_down, w_up, normed_mlp, after(grad_rows, part_down)
        )
        grad_normed, grad_down = lax.optimization_barrier((grad_normed, grad_down))
        gain_mlp_part = gain_mlp_part[0]
        grad_up = sum_dp(part_up, 0)
        grad_branch, grads_qkv, grad_residual = turn(
            grad_normed, attn_own, tokens, grad_out, w_out, qkv, mixed, gain_mlp, lse, row_key, col_key, heads
        )
        part_last, gain_attn_part = weights(normed, grad_branch, grads_qkv, mixed, w_query, w_key, w_value)
        gain_attn_part = gain_attn_part[0]
        part_last, grads_qkv, grad_up = lax.optimization_barrier((part_last, grads_qkv, grad_up))
        grad_last = sum_dp(part_last, 0)
        grad_qkv, grad_out_proj = grad_last[:, :3 * heads * HD], grad_last[:, 3 * heads * HD:].T
        grad_normed_attn = finish(grads_qkv, w_query, w_key, w_value)
    else:
        grad_hidden = dot_nt(grad_rows, w_down)
        grad_pre = (gelu_slope(dot_nn(normed_mlp, w_up)) * grad_hidden).astype(BF)
        part_up = dot_tn(normed_mlp, grad_pre)
        grad_up = sum_dp(part_up, 0)
        gain_mlp_part = jnp.sum(part_up * w_up.astype(F32), axis=1)
        grad_residual = grad_out.astype(F32) + norm_back(residual, gain_mlp, sum_mp(dot_nt(grad_pre, w_up)))
        grad_branch = over_mp(grad_residual.astype(BF))
        grad_mixed = dot_nt(grad_branch, w_out).astype(BF)
        grads_qkv = jnp.concatenate(attn_bwd(qkv, grad_mixed, mixed, lse, order, row_key, col_key, heads, own_rows), 1)
        grad_out_proj = sum_dp(dot_tn(mixed, grad_branch), 1)
        part_qkv = dot_tn(normed, grads_qkv)
        grad_qkv = sum_dp(part_qkv, 0)
        w_qkv = jnp.concatenate([w_query, w_key, w_value], 1)
        gain_attn_part = jnp.sum(part_qkv * w_qkv.astype(F32), axis=1)
        mlp_own = sum_mp(dot_nn(hidden, w_down))
        grad_normed_attn = sum_mp(dot_nt(grads_qkv, w_qkv))
    stream = residual + mlp_own
    mask_own = valid_own.astype(F32)[:, None]
    grad_tokens = (grad_residual + norm_back(tokens32, gain_attn, grad_normed_attn)).astype(BF)

    squares = jnp.stack([jnp.sum(mask_own * part * part) for part in (stream, attn_own, mlp_own)])
    small = jnp.concatenate([gain_attn_part / gain_attn, gain_mlp_part / gain_mlp, squares])
    summed = small_total(small, n_dp) if cube else lax.psum(small, ("dp", "mp"))
    counted = jnp.maximum(jnp.sum(valid).astype(F32) * width, 1.0)
    gain_rows = width // (n_dp * n_mp)
    place = (dp * n_mp + me) * gain_rows
    rms = jnp.sqrt(summed[2 * width:] / counted)
    shard = heads * HD
    return (
        stream.astype(BF),
        grad_tokens,
        lax.dynamic_slice_in_dim(summed[:width], place, gain_rows),
        grad_qkv[:, :shard],
        grad_qkv[:, shard:2 * shard],
        grad_qkv[:, 2 * shard:],
        grad_out_proj,
        lax.dynamic_slice_in_dim(summed[width:2 * width], place, gain_rows),
        grad_up,
        grad_down,
        rms[0],
        rms[1],
        rms[2],
    )


def solution(mesh):
    tokens_spec = P(("dp", "mp"), None)
    cols, rows = P(None, "mp"), P("mp", None)
    return jax.shard_map(
        on_device,
        mesh=mesh,
        in_specs=(tokens_spec, P("dp"), P(), P(), cols, cols, cols, rows, P(), cols, rows, tokens_spec),
        out_specs=(
            tokens_spec,
            tokens_spec,
            P(("dp", "mp")),
            P("dp", "mp"),
            P("dp", "mp"),
            P("dp", "mp"),
            P("mp", "dp"),
            P(("dp", "mp")),
            P("dp", "mp"),
            P("mp", "dp"),
            P(),
            P(),
            P(),
        ),
        check_vma=False,
    )
```

time: 573 us -> 476 us (0.83)
  Pallas kernels: 76.5 us -> 397 us
  matrix products: 153 us -> 14.4 us
  waiting for transfers between devices: 132 us -> 8.07 us
  local copies, waits for them, and re-layouts: 105 us -> 10.1 us
  starting transfers between devices: 43.9 us -> 6.42 us
  other arithmetic: 41.9 us -> 16.5 us
    pallas_call x2 -> x5, Pallas kernels: 31.9 us -> 352 us  [the longest x1 122 us: forward(): pl.pallas_call(functools.partial(forward_body, heads), name='forward_laye...]
    ppermute x61 -> x5, waiting for transfers between devices: 132 us -> 7.98 us  [small_total(): lax.ppermute(vector, axis, [(i, i ^ bit) for i in range(count)])]
    dot_general x28 -> x0, matrix products: 111 us -> none  [the longest x16 72.4 us: dot_nt(): lax.dot_general(a, b, (((1,), (1,)), ((), ())), preferred_element_type=F32)]
    unnamed x190 -> x23, local copies, waits for them, and re-layouts: 79.2 us -> 2.99 us
    ppermute x61 -> x5, starting transfers between devices: 43.4 us -> 6.3 us  [small_total(): lax.ppermute(vector, axis, [(i, i ^ bit) for i in range(count)])]
    dot_general x4 -> x1, matrix products: 42.5 us -> 14.4 us  [dot_tn(): lax.dot_general(a, b, (((0,), (0,)), ((), ())), preferred_element_type=F32)]
    slice x34 -> x0, local copies, waits for them, and re-layouts: 16.8 us -> none  [the longest x8 10.7 us: scatter(): came[k * rows:(k + 1) * rows]]
    convert_element_type x18 -> x3, other arithmetic: 13.6 us -> 7.17 us  [sum_dp(): lax.psum_scatter(value.astype(BF), 'dp', scatter_dimension=axis, tiled=True)]
  transfers between devices with their start and end apart: 65 -> 8, of which waited for: 19 -> 3; matrix products, arithmetic and copies ran while one was open for 46% -> 3% of each run, Pallas kernels for 3% -> 49%
where the time goes in v3:
time: 476 us; the launch traced here: 467 us
  Pallas kernels  397 us (83%)
  other arithmetic  16.5 us (3%)
  between operations  14.9 us (3%)
  matrix products  14.4 us (3%)
  local copies, waits for them, and re-layouts  10.1 us (2%)
  waiting for transfers between devices  8.07 us (2%)
  starting transfers between devices  6.42 us (1%)
    pallas_call x1, Pallas kernels, forward(): pl.pallas_call(functools.partial(forward_body, heads), name='forward_laye...  122 us
    pallas_call x1, Pallas kernels, middle(): pl.pallas_call(middle_body, name='middle_layer', in_specs=[hbm] * 5, out_...  93.2 us
    pallas_call x1, Pallas kernels, turn(): pl.pallas_call(functools.partial(turn_body, heads), name='turn_layer', in...  65 us
    pallas_call x1, Pallas kernels, finish(): pl.pallas_call(finish_body, name='last_scatter', in_specs=[hbm] * 4, out_...  51.8 us
    pallas_call x1, Pallas kernels, project(): pl.pallas_call(project_body, name='gather_project', in_specs=[hbm, pl.Blo...  44.5 us
    pallas_call x1, Pallas kernels, weights(): pl.pallas_call(weights_body, name='weight_gradients', grid=(width // tile...  20.4 us
    dot_general x1, matrix products, dot_tn(): lax.dot_general(a, b, (((0,), (0,)), ((), ())), preferred_element_type=F32)  14.4 us
  transfers between devices with their start and end apart: 8, of which 3 were waited for; matrix products, arithmetic and copies ran while one was open for 3% of the time, Pallas kernels for 49%

profile of v3, /device:TPU:0, one launch (start us, length us, event | category | flops | bytes accessed | tf_op | source)
XLA Modules:
  0.0 466.9 jit_solution(9146109496778269053)
XLA Ops:
  7.2 0.0 reduce-scatter.4.cloned.1.call-start
  7.2 2.0 copy.26.rk_ref
  9.3 1.3 fusion.13
  10.6 44.5 %gather_project.1 = (bf16[2048,768]{1,0:T(8,128)(2,1)}, bf16[2048,2048]{1,0:T(8,128)(2,1)}) custom-call(bf16[256,2048]{1,0:T(8,128)(2,1)} %tok_hbm.5, f32[1,2048]{1,0:T(1,128)} %bitcast.17, bf16[2048,256]{1,0:T(8,128)(2,1)} %wq_hbm.3, bf16[2048,256]{1,0:T(8,128)(2,1)} %wk_hbm.3, bf16[2048,256]{1,0:T(8,128)(2,1)} %wv_hbm.3), custom_call_target="tpu_custom_call" | custom-call | flops 6442450944 | bytes 62914560 | tf_op jit(solution)/shard_map/gather_project/pallas_call | solution.py:335
  55.1 121.7 %forward_layer.1 = (bf16[2048,256]{1,0:T(8,128)(2,1)}, f32[2,2048,1]{2,1,0:T(8,128)}, f32[256,2048]{1,0:T(8,128)}, bf16[2048,2048]{1,0:T(8,128)(2,1)}, bf16[2048...) custom-call(bf16[2048,768]{1,0:T(8,128)(2,1)} %get-tuple-element.36.qkv_hbm, bf16[256,2048]{1,0:T(8,128)(2,1)} %grad_hbm.3, ...), custom_call_target="tpu_custom_call" | custom-call | flops 40000000000 | bytes 262144000 | tf_op jit(solution)/shard_map/forward_layer/pallas_call | solution.py:568
  176.8 14.4 %convolution_convert_fusion = bf16[1024,2048]{1,0:T(8,128)(2,1)} fusion(bf16[2048,1024]{1,0:T(8,128)(2,1)} %get-tuple-element.38.hidden_hbm, bf16[2048,2048]{1,0:T(8,128)(2,1)} %get-tuple-element.41.grads_hbm), kind=kOutput, calls=%fused_computation | convolution fusion | flops 8592031744 | bytes 16777216 | tf_op jit(solution)/shard_map/dot_general | solution.py:24
  191.2 0.0 reduce-scatter.4.cloned.1.call-update
  191.3 0.0 reduce-scatter.6.cloned.1.call-start
  191.3 93.2 %middle_layer.1 = (f32[256,2048]{1,0:T(8,128)}, f32[256,2048]{1,0:T(8,128)}, bf16[2048,1024]{1,0:T(8,128)(2,1)}, f32[1,2048]{1,0:T(1,128)}) custom-call(bf16[2048,1024]{1,0:T(8,128)(2,1)} %get-tuple-element.38.hidden_hbm, bf16[1024,2048]{1,0:T(8,128)(2,1)} %w_down_hbm.1, bf16[2048,1024]{1,0:T(8,128)(2,1)} %w_up_hbm.3, ...), custom_call_target="tpu_custom_call" | custom-call | flops 44999999488 | bytes 209715200 | tf_op jit(solution)/shard_map/middle_layer/pallas_call | solution.py:719
  284.5 0.0 reduce-scatter.6.cloned.1.call-update
  284.6 0.0 reduce-scatter.8.cloned.1.call-start
  284.6 0.0 reduce-scatter.4.cloned.1.call-done
  284.6 2.8 convert_element_type.30
  287.5 65.0 %turn_layer.1 = (bf16[2048,2048]{1,0:T(8,128)(2,1)}, bf16[2048,768]{1,0:T(8,128)(2,1)}, f32[256,2048]{1,0:T(8,128)}) custom-call(f32[256,2048]{1,0:T(8,128)} %get-tuple-element.44.dnorm_hbm, f32[256,2048]{1,0:T(8,128)} %get-tuple-element.37.attn_hbm, bf16[256,2048]{1,0:T(8,128)(2,1)} %tok_hbm.5, bf16[256,2048]{1,0:T(8,128)(2,1)} %grad_hbm.3, ...), custom_call_target="tpu_custom_call" | custom-call | flops 44999999488 | bytes 209715200 | tf_op jit(solution)/shard_map/turn_layer/pallas_call | solution.py:818
  352.5 1.2 copy-done.3
  353.7 20.4 %weight_gradients.1 = (bf16[2048,1024]{1,0:T(8,128)(2,1)}, f32[1,2048]{1,0:T(1,128)S(1)}) custom-call(bf16[2048,2048]{1,0:T(8,128)(2,1)} %get-tuple-element.48.normed_ref, bf16[2048,2048]{1,0:T(8,128)(2,1)} %get-tuple-element.49.branch_ref, bf16[2048,768]{1,0:T(8,128)(2,1)} %get-tuple-element.53.dqkv_ref.dqkv_hbm, bf16[2048,256]{1,0:T(8,128)(2,1)S(1)} %copy-done.3, ...), custom_call_target="tpu_custom_call" | custom-call | flops 8589934592 | bytes 31457280 | tf_op jit(solution)/shard_map/weight_gradients/pallas_call | solution.py:853
  374.1 0.0 reduce-scatter.6.cloned.1.call-done
  374.2 2.8 convert_element_type.31
  377.0 0.0 reduce-scatter.8.cloned.1.call-update
  377.0 0.7 copy-done.9
  377.6 0.0 copy-done.10
  377.7 0.1 copy-done.8
  377.7 0.1 dynamic-slice_convert_fusion
  377.8 5.1 %fusion.11 = (f32[]{:T(128)}, f32[]{:T(128)}, f32[]{:T(128)}, f32[256]{0:T(256)S(1)}, bf16[256,2048]{1,0:T(8,128)(2,1)}) fusion(f32[256,2048]{1,0:T(8,128)} %get-tuple-element.42, f32[256]{0:T(256)S(1)} %dynamic-slice_convert_fusion, f32[256,2048]{1,0:T(8,128)} %get-tuple-element.37.attn_hbm, bf16[256,2048]{1,0:T(8,128)(2,1)} %tok_hbm.5), kind=kLoop, calls=%fused_computation.18 | loop fusion | flops 7864061 | bytes 6293516 | tf_op jit(solution)/shard_map/reduce_sum | solution.py:1001
  383.0 2.0 concatenate.3
  385.0 0.0 collective-permute-start
  385.0 0.6 reduce_sum.59
  386.3 0.0 collective-permute-done
  386.4 0.0 copy-start.4
  386.4 1.7 collective-permute-start.1
  388.1 51.8 %last_scatter.1 = f32[256,2048]{1,0:T(8,128)S(1)} custom-call(bf16[2048,768]{1,0:T(8,128)(2,1)} %get-tuple-element.53.dqkv_ref.dqkv_hbm, bf16[2048,256]{1,0:T(8,128)(2,1)S(1)} %copy-done, bf16[2048,256]{1,0:T(8,128)(2,1)S(1)} %copy-done.1, bf16[2048,256]{1,0:T(8,128)(2,1)S(1)} %copy-done.2), custom_call_target="tpu_custom_call" | custom-call | flops 20000000000 | bytes 104857600 | tf_op jit(solution)/shard_map/last_scatter/pallas_call | solution.py:894
  439.9 0.0 collective-permute-done.1
  439.9 0.7 collective-permute-start.2
  440.6 0.5 fusion.2
  441.1 2.6 collective-permute-done.2
  443.8 1.4 collective-permute-start.3
  445.2 3.0 collective-permute-done.3
  448.2 2.5 collective-permute-start.4
  450.6 0.0 copy-done.6
  450.6 1.6 fusion.6
  452.2 2.3 collective-permute-done.4
  454.6 0.6 dynamic_slice.18
  455.2 0.6 dynamic_slice.17
  455.8 0.6 fusion.17
  456.4 1.5 convert_element_type.34
  458.0 1.0 copy.28
  459.0 0.0 copy-done.5
  459.0 1.2 fusion.15
  (28 shorter events, 0.1 us)
Async XLA Ops:
  7.2 277.5 %reduce-scatter.4.cloned.1.call-start = ((), (), s32[]{:S(2)}) async-start(), calls=%async_computation.3 | async-start | bytes 5242880 | tf_op jit(solution)/shard_map/reduce_scatter | solution.py:921
  191.3 182.9 %reduce-scatter.6.cloned.1.call-start = ((), (), s32[]{:S(2)}) async-start(), calls=%async_computation.4 | async-start | bytes 5242880 | tf_op jit(solution)/shard_map/reduce_scatter | solution.py:921
  284.6 171.8 %reduce-scatter.8.cloned.1.call-start = ((), (), s32[]{:S(2)}) async-start(), calls=%async_computation.5 | async-start | bytes 5242880 | tf_op jit(solution)/shard_map/reduce_scatter | solution.py:921
  287.5 65.0 %copy-start = (bf16[2048,256]{1,0:T(8,128)(2,1)S(1)}, bf16[2048,256]{1,0:T(8,128)(2,1)}, u32[]{:S(2)}) copy-start(bf16[2048,256]{1,0:T(8,128)(2,1)} %wq_hbm.3) | copy-start | bytes 3145732
  287.5 65.0 %copy-start.1 = (bf16[2048,256]{1,0:T(8,128)(2,1)S(1)}, bf16[2048,256]{1,0:T(8,128)(2,1)}, u32[]{:S(2)}) copy-start(bf16[2048,256]{1,0:T(8,128)(2,1)} %wk_hbm.3) | copy-start | bytes 3145732
  287.5 65.0 %copy-start.2 = (bf16[2048,256]{1,0:T(8,128)(2,1)S(1)}, bf16[2048,256]{1,0:T(8,128)(2,1)}, u32[]{:S(2)}) copy-start(bf16[2048,256]{1,0:T(8,128)(2,1)} %wv_hbm.3) | copy-start | bytes 3145732
  352.5 1.2 copy-start.3
  376.9 0.7 copy-start.9
  377.0 0.7 copy-start.10
  377.0 0.8 copy-start.8
  377.8 5.1 %copy-start.7 = (f32[2048]{0:T(1024)S(1)}, f32[2048]{0:T(1024)}, u32[]{:S(2)}) copy-start(f32[2048]{0:T(1024)} %param.15) | copy-start | bytes 24580
  385.0 1.3 collective-permute-start
  386.4 54.2 %copy-start.4 = (bf16[256,2048]{1,0:T(8,128)(2,1)S(1)}, bf16[256,2048]{1,0:T(8,128)(2,1)}, u32[]{:S(2)}) copy-start(bf16[256,2048]{1,0:T(8,128)(2,1)} %tok_hbm.5) | copy-start | bytes 3145732
  386.4 53.5 %collective-permute-start.1 = (f32[4099]{0:T(1024)S(1)}, f32[4099]{0:T(1024)S(1)}, u32[]{:S(2)}, u32[]{:S(2)}) collective-permute-start(f32[4099]{0:T(1024)S(1)} %add.62), channel_id=1, source_target_pairs={{0,2},{1,3},{2,0},{3,1},{4,6},{5,7},{6,4},{7,5},{8,10},{9,11},{10,... | collective-permute-start | bytes 49196 | tf_op jit(solution)/shard_map/ppermute | solution.py:928
  439.9 10.8 %copy-start.6 = (f32[256,2048]{1,0:T(8,128)S(1)}, f32[256,2048]{1,0:T(8,128)}, u32[]{:S(2)}) copy-start(f32[256,2048]{1,0:T(8,128)} %get-tuple-element.47) | copy-start | bytes 6291460
  439.9 3.8 collective-permute-start.2
  443.8 4.4 collective-permute-start.3
  448.2 6.4 %collective-permute-start.4 = (f32[4099]{0:T(1024)S(1)}, f32[4099]{0:T(1024)S(1)}, u32[]{:S(2)}, u32[]{:S(2)}) collective-permute-start(f32[4099]{0:T(1024)S(1)} %add.65), channel_id=1, source_target_pairs={{0,16},{8,24},{16,0},{24,8},{1,17},{9,25},{17,1},{25,9},{2,18},{10... | collective-permute-start | bytes 49196 | tf_op jit(solution)/shard_map/ppermute | solution.py:928
  456.4 2.6 copy-start.5
Sparse Core Ops, SparseCore 0:
  191.4 77.1 reduce-scatter.3
  284.7 77.4 reduce-scatter.5
  377.1 77.9 reduce-scatter.7

commit v4 on v3

--- a/solution.py
+++ b/solution.py
@@ -44,7 +44,7 @@
         end = (a + 1) * blk
         low = end - blk
         s = dot_nt(queries(place(a)), ks[:end, :])
-        ok = rk_ref[low:end, :] == ck_ref[:, :end]
+        ok = rk_ref[low:end, 0:1] == ck_ref[:, :end]
         sd = jnp.where((ok[:, low:] & earlier) | itself, s[:, low:], NEGATIVE)
         m = jnp.max(sd, axis=1, keepdims=True)
         if a:
@@ -119,7 +119,7 @@
         delta = jnp.sum(do.astype(F32) * mixes(at).astype(F32), axis=1, keepdims=True)
         p = jnp.exp2(dot_nt(q, ks[:end, :]) * c - lses(a))
         dp = dot_nt(do, vs[:end, :])
-        ok = rk_ref[low:end, :] == ck_ref[:, :end]
+        ok = rk_ref[low:end, 0:1] == ck_ref[:, :end]
         pd = jnp.where((ok[:, low:] & earlier) | itself, p[:, low:], 0.0)
         dsd = (pd * (dp[:, low:] - delta)).astype(BF)
         dq = dot_nn(dsd, ks[low:end, :])
@@ -246,13 +246,18 @@
     def pair(self):
         self.copies[4].wait_recv()
 
-    def forward(self):
+    def forward(self, both=True):
         for arrived, onward in ((2, 5), (0, 6)):
             self.copies[arrived].wait_recv()
-            self.copies[onward].start()
+            if both:
+                self.copies[onward].start()
         for arrived, onward in ((1, 7), (3, 8)):
             self.copies[arrived].wait_recv()
             self.copies[onward].start()
+
+    def onward(self):
+        self.copies[5].start()
+        self.copies[6].start()
 
     def middle(self):
         self.copies[7].wait_recv()
@@ -349,6 +354,7 @@
 class Scatter:
     def __init__(self, product, own_ref, bufs, sems, core, sib, first, second):
         self.product, self.own_ref, self.core = product, own_ref, core
+        self.sent = 0
         self.away_ref, self.r0, self.s1, self.r1, self.s2, self.r2, self.s3, self.r3 = bufs
         self.chunks, _, self.rows, self.step = self.away_ref.shape
         self.half = self.chunks * self.step
@@ -421,9 +427,13 @@
         for j in range(self.chunks):
             stage(j)
 
+    def release(self, j):
+        self.copies[j][0].wait_send()
+        self.sent = 1
+
     def drain(self):
         for copies in self.copies:
-            for one in copies:
+            for one in copies[self.sent:]:
                 one.wait_send()
 
 
@@ -455,18 +465,37 @@
     return pl.multiple_of(position * rows, rows)
 
 
+def gelu_pair(x):
+    c = 0.7978845608028654
+    square = x * x
+    t = jnp.tanh(c * (x + 0.044715 * (x * square)))
+    upper = 0.5 * (1.0 + t)
+    return x * upper, upper + 0.5 * x * (1.0 - t * t) * (c + (3 * 0.044715 * c) * square)
+
+
+def fill_keys(seg_ref, valid_ref, rk, ck):
+    seq = seg_ref.shape[1]
+    here = pl.ds(pl.multiple_of(lax.axis_index("dp") * seq, seq), seq)
+    numbers = seg_ref[...].astype(F32)
+    ck[...] = jnp.where(valid_ref[:, here] > 0, numbers, -1.0)
+    step = 256
+    for i in range(0, seq, step):
+        rk[i:i + step, :] = jnp.transpose(jnp.broadcast_to(numbers[:, i:i + step], (128, step)))
+
+
 def forward_body(
-    heads, qkv_hbm, grad_hbm, tok_hbm, w_out_hbm, w_up_hbm, gain_ref, rk_ref, ck_ref,
-    mixed_hbm, lse_ref, attn_hbm, normed_hbm, hidden_hbm, rows_hbm,
-    qkv, tok, w_out, w_up, mixed, own, hidden, ks, vs, loads, stores,
+    heads, qkv_hbm, grad_hbm, tok_hbm, w_out_hbm, w_up_hbm, w_down_hbm, gain_ref, seg_ref, valid_ref,
+    mixed_hbm, lse_ref, attn_hbm, normed_hbm, hidden_hbm, pre_hbm, rows_hbm,
+    qkv, w_out, w_up, w_down, mixed, own, hidden, pre, rk_ref, ck_ref, ks, vs, loads, stores,
     nbuf, nsend, nrecv, gbuf, gsend, grecv, *scatter,
 ):
     core, sib, first, second = neighbours()
-    rows, width = tok.shape
+    rows, width = own.shape
     local = pltpu.make_async_copy
     fetch = [
         local(grad_hbm, gbuf.at[0], loads.at[0]), local(qkv_hbm, qkv, loads.at[1]), local(w_out_hbm, w_out, loads.at[2]),
-        local(tok_hbm, tok, loads.at[3]), local(w_up_hbm, w_up, loads.at[4]),
+        local(tok_hbm, nbuf.at[0], loads.at[3]), local(w_up_hbm, w_up, loads.at[4]),
+        local(w_down_hbm, w_down, loads.at[5]),
     ]
     for one in fetch:
         one.start()
@@ -474,6 +503,7 @@
     fetch[0].wait()
     grads = Gather(gbuf, gsend, grecv, sib, first, second)
     grads.start()
+    fill_keys(seg_ref, valid_ref, rk_ref, ck_ref)
     fetch[1].wait()
 
     def head(h, carry):
@@ -498,186 +528,164 @@
 
     fetch[2].wait()
     net = Scatter(product, own, scatter[:8], scatter[8:], core, sib, first, second)
-    for stage in (net.away, net.one, net.two, net.three, net.four):
-        net.each(stage)
+    net.each(net.away)
+    net.each(net.one)
+    grads.pair()
+    fetch[5].wait()
+    net.each(net.release)
+    slopes = net.away_ref
+    tile = net.step
+
+    def back(s, carry):
+        for t in range(net.chunks):
+            slopes[t, s] = dot_nt(gbuf[s], w_down[t * tile:(t + 1) * tile, :]).astype(BF)
+        return carry
+
+    lax.fori_loop(0, 2, back, 0)
+    grads.forward(False)
+    grads.middle()
+    lax.fori_loop(2, 6, back, 0)
+    net.each(net.two)
+    net.each(net.three)
+    grads.onward()
+    net.each(net.four)
     attn_out = local(own, attn_hbm, stores.at[1])
     attn_out.start()
 
     fetch[3].wait()
 
+    def at(s):
+        return pl.ds(pl.multiple_of(s * rows, rows), rows)
+
     def norm(part):
-        residual = tok[part, :].astype(F32) + own[part, :]
+        residual = nbuf[0, part, :].astype(F32) + own[part, :]
         nbuf[0, part, :] = norm_rows(residual, gain_ref[...]).astype(BF)
 
     rows_loop(rows, 32, norm)
     ring = Gather(nbuf, nsend, nrecv, sib, first, second)
     ring.start()
     fetch[4].wait()
-    cols = hidden.shape[1]
-    tile = min(512, cols)
+    rows_out = [local(gbuf.at[s], rows_hbm.at[pl.ds(s * rows, rows)], stores.at[6 + s]) for s in range(8)]
+    for one in rows_out[:6]:
+        one.start()
+    def normed_copy(s):
+        return local(nbuf.at[s], normed_hbm.at[at(s)], stores.at[14 + s])
 
     def moved(s):
-        at = pl.ds(pl.multiple_of(s * rows, rows), rows)
         return (
-            local(nbuf.at[s], normed_hbm.at[at], stores.at[2 + s]),
-            local(hidden.at[at], hidden_hbm.at[at], stores.at[10 + s]),
+            local(hidden.at[s % 2], hidden_hbm.at[at(s)], stores.at[2 + s % 2]),
+            local(pre.at[s % 2], pre_hbm.at[at(s)], stores.at[4 + s % 2]),
         )
 
     def slot(s, carry):
-        at = pl.ds(pl.multiple_of(s * rows, rows), rows)
-        normed_out, hidden_out = moved(s)
-        normed_out.start()
+        normed_copy(s).start()
+
+        @pl.when(s >= 2)
+        def _():
+            for one in moved(s - 2):
+                one.wait()
 
         def some(t, inner):
             col = pl.ds(pl.multiple_of(t * tile, tile), tile)
-            hidden[at, col] = gelu_fn(dot_nn(nbuf[s], w_up[:, col])).astype(BF)
+            value, slope = gelu_pair(dot_nn(nbuf[s], w_up[:, col]))
+            hidden[s % 2, :, col] = value.astype(BF)
+            pre[s % 2, :, col] = (slope * slopes[t, s].astype(F32)).astype(BF)
             return inner
 
-        lax.fori_loop(0, cols // tile, some, 0)
-        hidden_out.start()
+        lax.fori_loop(0, net.chunks, some, 0)
+        for one in moved(s):
+            one.start()
         return carry
 
     ring.pair()
     lax.fori_loop(0, 2, slot, 0)
+    grads.finish()
+    lax.fori_loop(6, 8, back, 0)
+    for one in rows_out[6:]:
+        one.start()
     ring.forward()
-    grads.pair()
-    grads.forward()
     ring.middle()
     lax.fori_loop(2, 6, slot, 0)
     ring.finish()
     lax.fori_loop(6, 8, slot, 0)
-    grads.middle()
-    grads.finish()
-    copies = [local(gbuf.at[s], rows_hbm.at[pl.ds(s * rows, rows)], stores.at[18 + s]) for s in range(8)]
-    for one in copies:
-        one.start()
     for s in range(8):
-        copies.extend(moved(s))
-    for one in copies + [mixed_out, attn_out]:
+        normed_copy(s).wait()
+    for one in [*moved(6), *moved(7), *rows_out, mixed_out, attn_out]:
         one.wait()
     ring.drain()
     grads.drain()
     net.drain()
 
 
-def forward(qkv, grad_out, tokens, w_out, w_up, gain, row_key, col_key, heads):
+def forward(qkv, grad_out, tokens, w_out, w_up, w_down, gain, segment, valid, heads):
     rows, width = tokens.shape
     seq, hidden = 8 * rows, w_up.shape[1]
     hbm, vmem = pl.BlockSpec(memory_space=HBM_SPACE), pl.BlockSpec(memory_space=VMEM_SPACE)
     shape = jax.ShapeDtypeStruct
     return pl.pallas_call(
         functools.partial(forward_body, heads), name="forward_layer",
-        in_specs=[hbm] * 5 + [vmem] * 3,
-        out_specs=[hbm, vmem, hbm, hbm, hbm, hbm],
+        in_specs=[hbm] * 6 + [vmem] * 3,
+        out_specs=[hbm, vmem, hbm, hbm, hbm, hbm, hbm],
         out_shape=[
             shape((seq, heads * HD), BF), shape((heads, seq, 1), F32), shape((rows, width), F32), shape((seq, width), BF),
-            shape((seq, hidden), BF), shape((seq, width), BF),
+            shape((seq, hidden), BF), shape((seq, hidden), BF), shape((seq, width), BF),
         ],
         scratch_shapes=[
-            pltpu.VMEM((seq, 3 * heads * HD), BF), pltpu.VMEM((rows, width), BF), pltpu.VMEM((heads * HD, width), BF),
-            pltpu.VMEM((width, hidden), BF), pltpu.VMEM((seq, heads * HD), BF), pltpu.VMEM((rows, width), F32),
-            pltpu.VMEM((seq, hidden), BF), pltpu.VMEM((seq, HD), BF), pltpu.VMEM((seq, HD), BF),
-            pltpu.SemaphoreType.DMA((5,)), pltpu.SemaphoreType.DMA((26,)),
+            pltpu.VMEM((seq, 3 * heads * HD), BF), pltpu.VMEM((heads * HD, width), BF),
+            pltpu.VMEM((width, hidden), BF), pltpu.VMEM((hidden, width), BF), pltpu.VMEM((seq, heads * HD), BF),
+            pltpu.VMEM((rows, width), F32), pltpu.VMEM((2, rows, hidden), BF), pltpu.VMEM((2, rows, hidden), BF),
+            pltpu.VMEM((seq, 128), F32), pltpu.VMEM((1, seq), F32),
+            pltpu.VMEM((seq, HD), BF), pltpu.VMEM((seq, HD), BF),
+            pltpu.SemaphoreType.DMA((6,)), pltpu.SemaphoreType.DMA((22,)),
         ] + gather_scratch(rows, width) * 2 + scatter_scratch(rows, width, 2),
         compiler_params=pltpu.CompilerParams(collective_id=2, has_side_effects=True, vmem_limit_bytes=62 * MIB),
         cost_estimate=pl.CostEstimate(flops=40 * 10**9, bytes_accessed=250 * MIB, transcendentals=0),
-    )(qkv, grad_out, tokens, w_out, w_up, gain[None, :], row_key, col_key)
-
-def gelu_slope(x):
-    c = 0.7978845608028654
-    square = x * x
-    t = jnp.tanh(c * (x + 0.044715 * (x * square)))
-    return 0.5 * (1.0 + t) + 0.5 * x * (1.0 - t * t) * (c * (1.0 + 3 * 0.044715 * square))
-
+    )(qkv, grad_out, tokens, w_out, w_up, w_down, gain[None, :], segment[None, :], valid[None, :])
 
 def row_sums(product):
-    ones = jnp.ones((8, product.shape[1]), F32)
+    part = sum(product[:, i:i + 128] for i in range(0, product.shape[1], 128))
     return lax.dot_general(
-        ones, product, (((1,), (1,)), ((), ())), preferred_element_type=F32, precision=lax.Precision.HIGHEST
+        jnp.ones((8, 128), F32), part, (((1,), (1,)), ((), ())), preferred_element_type=F32, precision=lax.Precision.HIGHEST
     )[0:1]
 
 
 def middle_body(
-    hidden_hbm, w_down_hbm, w_up_hbm, normed_hbm, grads_hbm,
-    mlp_hbm, dnorm_hbm, up_hbm, gain_ref,
-    hidden, w_down, w_up, pre, normed, grads, tiles, ups, mlp, dnorm, loads, stores, *scatter,
+    pre_hbm, w_up_hbm, normed_hbm, dnorm_hbm, up_hbm, gain_ref, pre, w_up, tiles, ups, dnorm, loads, stores, *scatter
 ):
     core, sib, first, second = neighbours()
-    rows, width = mlp.shape
-    inner = hidden.shape[1]
+    rows, width = dnorm.shape
     local = pltpu.make_async_copy
-    fetch = [
-        local(source, target, loads.at[i])
-        for i, (source, target) in enumerate(((hidden_hbm, hidden), (w_down_hbm, w_down), (w_up_hbm, w_up)))
-    ]
-
-    def at(p):
-        return pl.ds(pl.multiple_of(p * rows, rows), rows)
-
-    def block(s):
-        return (
-            local(normed_hbm.at[at(s)], normed.at[s % 2], loads.at[3 + s % 2]),
-            local(grads_hbm.at[at(s)], grads.at[s % 2], loads.at[5 + s % 2]),
-        )
+    tile = tiles.shape[2]
+    count = width // tile
+    fetch = [local(pre_hbm, pre, loads.at[0]), local(w_up_hbm, w_up, loads.at[1])]
+
+    def strip(t):
+        return pl.ds(pl.multiple_of(t * tile, tile), tile)
+
+    def load_tile(t):
+        return local(normed_hbm.at[:, strip(t)], tiles.at[t % 2], loads.at[2 + t % 2])
+
+    def save_tile(t):
+        return local(ups.at[t % 2], up_hbm.at[strip(t)], stores.at[1 + t % 2])
 
     for one in fetch:
         one.start()
-    for one in block(0):
-        one.start()
+    load_tile(0).start()
     greet(sib, first, second)
 
-    def down(p, col):
-        return dot_nn(hidden[at(p), :], w_down[:, pl.ds(col, net.step)])
-
     def up_back(p, col):
-        return dot_nt(pre[at(p), :], w_up[pl.ds(col, net.step), :])
-
-    net = Scatter(down, mlp, scatter[:8], scatter[8:10], core, sib, first, second)
-    back = Scatter(up_back, dnorm, scatter[10:18], scatter[18:], core, sib, first, second)
+        return dot_nt(pre[pl.ds(pl.multiple_of(p * rows, rows), rows), :], w_up[pl.ds(col, net.step), :])
+
+    net = Scatter(up_back, dnorm, scatter[:8], scatter[8:], core, sib, first, second)
     fetch[0].wait()
     fetch[1].wait()
     net.each(net.away)
     net.each(net.one)
-    fetch[2].wait()
-    part = min(512, inner)
-
-    def slopes(s, carry):
-        for one in block(s):
-            one.wait()
-
-        @pl.when(s < 7)
-        def _():
-            for one in block(s + 1):
-                one.start()
-
-        def some(t, more):
-            col = pl.ds(pl.multiple_of(t * part, part), part)
-            slope = gelu_slope(dot_nn(normed[s % 2], w_up[:, col]))
-            pre[at(s), col] = (slope * dot_nt(grads[s % 2], w_down[col, :])).astype(BF)
-            return more
-
-        lax.fori_loop(0, inner // part, some, 0)
-        return carry
-
-    lax.fori_loop(0, 8, slopes, 0)
-    tile = tiles.shape[2]
-
-    def load_tile(t):
-        return local(normed_hbm.at[:, pl.ds(pl.multiple_of(t * tile, tile), tile)], tiles.at[t % 2], loads.at[7 + t % 2])
-
-    def save_tile(t):
-        return local(ups.at[t % 2], up_hbm.at[pl.ds(pl.multiple_of(t * tile, tile), tile)], stores.at[2 + t % 2])
-
-    load_tile(0).start()
-    net.each(net.two)
-    back.each(back.away)
-    back.each(back.one)
-    net.each(net.three)
 
     def weight(t, carry):
         load_tile(t).wait()
 
-        @pl.when(t < width // tile - 1)
+        @pl.when(t < count - 1)
         def _():
             load_tile(t + 1).start()
 
@@ -688,54 +696,50 @@
         value = dot_tn(tiles[t % 2], pre[...])
         ups[t % 2] = value.astype(BF)
         save_tile(t).start()
-        gain_ref[:, pl.ds(pl.multiple_of(t * tile, tile), tile)] = row_sums(
-            value * w_up[pl.ds(pl.multiple_of(t * tile, tile), tile), :].astype(F32)
-        )
+        gain_ref[:, strip(t)] = row_sums(value * w_up[strip(t), :].astype(F32))
         return carry
 
-    lax.fori_loop(0, width // tile, weight, 0)
+    half = count // 2
+    lax.fori_loop(0, half, weight, 0)
+    net.two(0)
+    lax.fori_loop(half, count, weight, 0)
+    net.two(1)
+    net.each(net.three)
     net.each(net.four)
-    outs = [local(mlp, mlp_hbm, stores.at[0])]
-    outs[0].start()
-    for name in ("two", "three", "four"):
-        back.each(getattr(back, name))
-    outs.append(local(dnorm, dnorm_hbm, stores.at[1]))
-    outs[1].start()
-    for one in outs:
-        one.wait()
-    save_tile(width // tile - 2).wait()
-    save_tile(width // tile - 1).wait()
+    out = local(dnorm, dnorm_hbm, stores.at[0])
+    out.start()
+    out.wait()
+    save_tile(count - 2).wait()
+    save_tile(count - 1).wait()
     net.drain()
-    back.drain()
-
-
-def middle(hidden, w_down, w_up, normed, grads):
-    seq, inner = hidden.shape
-    width = w_down.shape[1]
+
+
+def middle(pre, w_up, normed):
+    seq, inner = pre.shape
+    width = w_up.shape[0]
     rows = seq // 8
     tile = 256
     hbm, vmem = pl.BlockSpec(memory_space=HBM_SPACE), pl.BlockSpec(memory_space=VMEM_SPACE)
     shape = jax.ShapeDtypeStruct
     return pl.pallas_call(
         middle_body, name="middle_layer",
-        in_specs=[hbm] * 5,
-        out_specs=[hbm] * 3 + [vmem],
-        out_shape=[shape((rows, width), F32), shape((rows, width), F32), shape((width, inner), BF), shape((1, width), F32)],
+        in_specs=[hbm] * 3,
+        out_specs=[hbm] * 2 + [vmem],
+        out_shape=[shape((rows, width), F32), shape((width, inner), BF), shape((1, width), F32)],
         scratch_shapes=[
-            pltpu.VMEM((seq, inner), BF), pltpu.VMEM((inner, width), BF), pltpu.VMEM((width, inner), BF),
-            pltpu.VMEM((seq, inner), BF), pltpu.VMEM((2, rows, width), BF), pltpu.VMEM((2, rows, width), BF),
+            pltpu.VMEM((seq, inner), BF), pltpu.VMEM((width, inner), BF),
             pltpu.VMEM((2, seq, tile), BF), pltpu.VMEM((2, tile, inner), BF), pltpu.VMEM((rows, width), F32),
-            pltpu.VMEM((rows, width), F32), pltpu.SemaphoreType.DMA((9,)), pltpu.SemaphoreType.DMA((4,)),
-        ] + scatter_scratch(rows, width, 2) * 2,
-        compiler_params=pltpu.CompilerParams(collective_id=5, has_side_effects=True, vmem_limit_bytes=63 * MIB),
+            pltpu.SemaphoreType.DMA((4,)), pltpu.SemaphoreType.DMA((3,)),
+        ] + scatter_scratch(rows, width, 2),
+        compiler_params=pltpu.CompilerParams(collective_id=5, has_side_effects=True, vmem_limit_bytes=56 * MIB),
         cost_estimate=pl.CostEstimate(flops=45 * 10**9, bytes_accessed=200 * MIB, transcendentals=0),
-    )(hidden, w_down, w_up, normed, grads)
+    )(pre, w_up, normed)
 
 
 def turn_body(
-    heads, dnorm_hbm, attn_hbm, tok_hbm, grad_hbm, w_out_hbm, qkv_hbm, mixed_hbm, gain_ref, lse_ref, rk_ref, ck_ref,
+    heads, dnorm_hbm, attn_hbm, tok_hbm, grad_hbm, w_out_hbm, qkv_hbm, mixed_hbm, gain_ref, lse_ref, seg_ref, valid_ref,
     branch_hbm, dqkv_hbm, residual_hbm,
-    own, attn, tok, grad, w_out, qkv, mixed, dmixed, dqkv, ks, vs, dks, dvs, loads, stores, bbuf, bsend, brecv,
+    own, attn, tok, grad, w_out, qkv, mixed, dmixed, dqkv, rk_ref, ck_ref, ks, vs, dks, dvs, loads, stores, bbuf, bsend, brecv,
 ):
     core, sib, first, second = neighbours()
     rows, width = tok.shape
@@ -764,6 +768,7 @@
     ring.start()
     residual_out = local(own, residual_hbm, stores.at[0])
     residual_out.start()
+    fill_keys(seg_ref, valid_ref, rk_ref, ck_ref)
     fetch[4].wait()
 
     def moved(s):
@@ -809,7 +814,7 @@
     ring.drain()
 
 
-def turn(dnorm, attn_own, tokens, grad_out, w_out, qkv, mixed, gain, lse, row_key, col_key, heads):
+def turn(dnorm, attn_own, tokens, grad_out, w_out, qkv, mixed, gain, lse, segment, valid, heads):
     rows, width = tokens.shape
     seq = 8 * rows
     hbm, vmem = pl.BlockSpec(memory_space=HBM_SPACE), pl.BlockSpec(memory_space=VMEM_SPACE)
@@ -824,29 +829,48 @@
             pltpu.VMEM((rows, width), F32), pltpu.VMEM((rows, width), F32), pltpu.VMEM((rows, width), BF),
             pltpu.VMEM((rows, width), BF), pltpu.VMEM((cols, width), BF), pltpu.VMEM((seq, 3 * cols), BF),
             pltpu.VMEM((seq, cols), BF), pltpu.VMEM((seq, cols), BF), pltpu.VMEM((seq, 3 * cols), BF),
+            pltpu.VMEM((seq, 128), F32), pltpu.VMEM((1, seq), F32),
             pltpu.VMEM((seq, HD), BF), pltpu.VMEM((seq, HD), BF), pltpu.VMEM((seq, HD), F32), pltpu.VMEM((seq, HD), F32),
             pltpu.SemaphoreType.DMA((7,)), pltpu.SemaphoreType.DMA((10,)),
         ] + gather_scratch(rows, width),
         compiler_params=pltpu.CompilerParams(collective_id=3, has_side_effects=True, vmem_limit_bytes=60 * MIB),
         cost_estimate=pl.CostEstimate(flops=45 * 10**9, bytes_accessed=200 * MIB, transcendentals=0),
-    )(dnorm, attn_own, tokens, grad_out, w_out, qkv, mixed, gain[None, :], lse, row_key, col_key)
+    )(dnorm, attn_own, tokens, grad_out, w_out, qkv, mixed, gain[None, :], lse, segment[None, :], valid[None, :])
 
 
 def weights_body(normed_ref, branch_ref, dqkv_ref, mixed_ref, wq_ref, wk_ref, wv_ref, out_ref, gain_ref):
     cols = wq_ref.shape[1]
     value = dot_tn(normed_ref[...], dqkv_ref[...])
     out_ref[:, :3 * cols] = value.astype(BF)
-    out_ref[:, 3 * cols:] = dot_tn(branch_ref[...], mixed_ref[...]).astype(BF)
+    out_ref[:, 3 * cols:] = dot_tn(mixed_ref[...], branch_ref[...]).astype(BF)
     gain_ref[...] = sum(
         row_sums(value[:, k * cols:(k + 1) * cols] * w_ref[...].astype(F32))
         for k, w_ref in enumerate((wq_ref, wk_ref, wv_ref))
     )
 
 
+def down_body(hidden_ref, grad_ref, out_ref):
+    out_ref[...] = dot_tn(hidden_ref[...], grad_ref[...]).astype(BF)
+
+
+def down_weights(hidden, grads):
+    seq, inner = hidden.shape
+    width = grads.shape[1]
+    tile = 512
+    return pl.pallas_call(
+        down_body, name="down_weights", grid=(width // tile,),
+        in_specs=[pl.BlockSpec((seq, inner), lambda t: (0, 0)), pl.BlockSpec((seq, tile), lambda t: (0, t))],
+        out_specs=pl.BlockSpec((inner, tile), lambda t: (0, t)),
+        out_shape=jax.ShapeDtypeStruct((inner, width), BF),
+        compiler_params=pltpu.CompilerParams(vmem_limit_bytes=63 * MIB),
+        cost_estimate=pl.CostEstimate(flops=2 * seq * width * inner, bytes_accessed=16 * MIB, transcendentals=0),
+    )(hidden, grads)
+
+
 def weights(normed, branch, dqkv, mixed, w_query, w_key, w_value):
     seq, width = normed.shape
     cols = w_query.shape[1]
-    tile = 256
+    tile = cols
     full = lambda c: pl.BlockSpec((seq, c), lambda t: (0, 0))
     strip = pl.BlockSpec((seq, tile), lambda t: (0, t))
     rows = pl.BlockSpec((tile, cols), lambda t: (t, 0))
@@ -855,54 +879,133 @@
         in_specs=[strip, strip, full(3 * cols), full(cols), rows, rows, rows],
         out_specs=[pl.BlockSpec((tile, 4 * cols), lambda t: (t, 0)), pl.BlockSpec((1, tile), lambda t: (0, t))],
         out_shape=[jax.ShapeDtypeStruct((width, 4 * cols), BF), jax.ShapeDtypeStruct((1, width), F32)],
-        compiler_params=pltpu.CompilerParams(vmem_limit_bytes=48 * MIB),
+        compiler_params=pltpu.CompilerParams(vmem_limit_bytes=63 * MIB),
         cost_estimate=pl.CostEstimate(flops=2 * seq * width * 4 * cols, bytes_accessed=30 * MIB, transcendentals=0),
     )(normed, branch, dqkv, mixed, w_query, w_key, w_value)
 
 
-def finish_body(dqkv_hbm, wq_hbm, wk_hbm, wv_hbm, dnorm_hbm, dqkv, w_qkv, dnorm, loads, stores, *scatter):
+class Total:
+    def __init__(self, vec, got, sends, recvs, sib, first, second):
+        self.vec, self.got = vec, got
+        self.partners = [sib, first, second]
+        self.copies = [
+            pltpu.make_async_remote_copy(
+                src_ref=vec, dst_ref=got.at[k], send_sem=sends.at[k], recv_sem=recvs.at[k], device_id=other, device_id_type=MESH,
+            )
+            for k, other in enumerate(self.partners)
+        ]
+
+    def start(self, k):
+        self.copies[k].start()
+
+    def add(self, k):
+        self.copies[k].wait()
+        self.vec[...] += self.got[k]
+        if k + 1 < len(self.copies):
+            self.copies[k + 1].start()
+
+
+def finish_body(
+    hidden_hbm, w_down_hbm, dqkv_hbm, wq_hbm, wk_hbm, wv_hbm, tok_hbm, attn_hbm, gres_hbm, gain_ref, part_attn_ref, part_mlp_ref,
+    valid_ref, tokens_hbm, grads_hbm, total_ref,
+    hidden, w_down, dqkv, w_qkv, tok, attn, gres, out, mlp, dnorm, vec, got, sends, recvs, loads, stores, *scatter,
+):
     core, sib, first, second = neighbours()
-    rows = dnorm.shape[0]
+    rows, width = mlp.shape
     cols = wq_hbm.shape[1]
     local = pltpu.make_async_copy
-    pairs = [(dqkv_hbm, dqkv)]
+    pairs = [(hidden_hbm, hidden), (w_down_hbm, w_down), (dqkv_hbm, dqkv)]
     pairs += [(w, w_qkv.at[:, pl.ds(k * cols, cols)]) for k, w in enumerate((wq_hbm, wk_hbm, wv_hbm))]
+    pairs += [(tok_hbm, tok), (attn_hbm, attn), (gres_hbm, gres)]
     fetch = [local(source, target, loads.at[i]) for i, (source, target) in enumerate(pairs)]
     for one in fetch:
         one.start()
-    greet(sib, first, second)
+    total = Total(vec, got, sends, recvs, sib, first, second)
+    greet(*total.partners)
+
+    def at(p):
+        return pl.ds(pl.multiple_of(p * rows, rows), rows)
+
+    def down(p, col):
+        return dot_nn(hidden[at(p), :], w_down[:, pl.ds(col, late.step)])
 
     def project_back(p, col):
-        return dot_nt(dqkv[pl.ds(pl.multiple_of(p * rows, rows), rows), :], w_qkv[pl.ds(col, net.step), :])
-
-    net = Scatter(project_back, dnorm, scatter[:8], scatter[8:], core, sib, first, second)
-    for one in fetch:
+        return dot_nt(dqkv[at(p), :], w_qkv[pl.ds(col, net.step), :])
+
+    late = Scatter(down, mlp, scatter[:8], scatter[8:10], core, sib, first, second)
+    net = Scatter(project_back, dnorm, scatter[10:18], scatter[18:], core, sib, first, second)
+    fetch[0].wait()
+    fetch[1].wait()
+    late.each(late.away)
+    late.each(late.one)
+    for one in fetch[2:]:
         one.wait()
-    for stage in (net.away, net.one, net.two, net.three, net.four):
-        net.each(stage)
-    out = local(dnorm, dnorm_hbm, stores.at[0])
-    out.start()
-    out.wait()
+    net.each(net.away)
+    net.each(net.one)
+    for stage in (late.two, late.three, late.four):
+        late.each(stage)
+
+    own = pl.ds(pl.multiple_of((lax.axis_index("dp") * 8 + lax.axis_index("mp")) * rows, rows), rows)
+    mask = jnp.transpose(jnp.broadcast_to(valid_ref[:, own].astype(F32), (128, rows)))
+    vec[...] = jnp.zeros_like(vec)
+    vec[0:1, :] = part_attn_ref[...]
+    vec[1:2, :] = part_mlp_ref[...]
+    step = 64
+    for i in range(0, rows, step):
+        part = slice(i, i + step)
+        attn_part, mlp_part = attn[part, :], mlp[part, :]
+        stream = tok[part, :].astype(F32) + attn_part + mlp_part
+        out[0, part, :] = stream.astype(BF)
+        for k, value in enumerate((stream, attn_part, mlp_part)):
+            vec[2 + k:3 + k, :] += jnp.sum(mask[part, 0:1] * value * value, axis=0, keepdims=True)
+    tokens_out = local(out.at[0], tokens_hbm, stores.at[0])
+    tokens_out.start()
+    total.start(0)
+    net.each(net.two)
+    total.add(0)
+    net.each(net.three)
+    total.add(1)
+    net.each(net.four)
+
+    def last(part):
+        back = norm_back(tok[part, :].astype(F32), gain_ref[...], dnorm[part, :])
+        out[1, part, :] = (gres[part, :] + back).astype(BF)
+
+    rows_loop(rows, 32, last)
+    grads_out = local(out.at[1], grads_hbm, stores.at[1])
+    grads_out.start()
+    total.add(2)
+    total_ref[...] = vec[...]
+    tokens_out.wait()
+    grads_out.wait()
     net.drain()
-
-
-def finish(dqkv, w_query, w_key, w_value):
-    seq = dqkv.shape[0]
-    width, cols = w_query.shape
-    rows = seq // 8
-    hbm = pl.BlockSpec(memory_space=HBM_SPACE)
+    late.drain()
+
+
+def finish(hidden, w_down, dqkv, w_query, w_key, w_value, tokens, attn_own, grad_residual, gain, part_attn, part_mlp, valid):
+    seq, inner = hidden.shape
+    rows, width = tokens.shape
+    cols = w_query.shape[1]
+    stages = 3
+    hbm, vmem = pl.BlockSpec(memory_space=HBM_SPACE), pl.BlockSpec(memory_space=VMEM_SPACE)
+    shape = jax.ShapeDtypeStruct
     return pl.pallas_call(
-        finish_body, name="last_scatter",
-        in_specs=[hbm] * 4,
-        out_specs=hbm,
-        out_shape=jax.ShapeDtypeStruct((rows, width), F32),
+        finish_body, name="last_scatters",
+        in_specs=[hbm] * 9 + [vmem] * 4,
+        out_specs=[hbm] * 2 + [vmem],
+        out_shape=[shape((rows, width), BF), shape((rows, width), BF), shape((8, width), F32)],
         scratch_shapes=[
-            pltpu.VMEM((seq, 3 * cols), BF), pltpu.VMEM((width, 3 * cols), BF), pltpu.VMEM((rows, width), F32),
-            pltpu.SemaphoreType.DMA((4,)), pltpu.SemaphoreType.DMA((1,)),
-        ] + scatter_scratch(rows, width, 2),
-        compiler_params=pltpu.CompilerParams(collective_id=4, has_side_effects=True, vmem_limit_bytes=48 * MIB),
-        cost_estimate=pl.CostEstimate(flops=20 * 10**9, bytes_accessed=100 * MIB, transcendentals=0),
-    )(dqkv, w_query, w_key, w_value)
+            pltpu.VMEM((seq, inner), BF), pltpu.VMEM((inner, width), BF), pltpu.VMEM((seq, 3 * cols), BF),
+            pltpu.VMEM((width, 3 * cols), BF), pltpu.VMEM((rows, width), BF), pltpu.VMEM((rows, width), F32),
+            pltpu.VMEM((rows, width), F32), pltpu.VMEM((2, rows, width), BF), pltpu.VMEM((rows, width), F32),
+            pltpu.VMEM((rows, width), F32), pltpu.VMEM((8, width), F32), pltpu.VMEM((stages, 8, width), F32),
+            pltpu.SemaphoreType.DMA((stages,)), pltpu.SemaphoreType.DMA((stages,)),
+            pltpu.SemaphoreType.DMA((9,)), pltpu.SemaphoreType.DMA((2,)),
+        ] + scatter_scratch(rows, width, 2) * 2,
+        compiler_params=pltpu.CompilerParams(collective_id=4, has_side_effects=True, vmem_limit_bytes=63 * MIB),
+        cost_estimate=pl.CostEstimate(flops=30 * 10**9, bytes_accessed=200 * MIB, transcendentals=0),
+    )(hidden, w_down, dqkv, w_query, w_key, w_value, tokens, attn_own, grad_residual, gain[None, :], part_attn, part_mlp,
+      valid[None, :])
 
 
 def after(value, *others):
@@ -918,16 +1021,7 @@
 
 
 def sum_dp(value, axis):
-    return lax.psum_scatter(value.astype(BF), "dp", scatter_dimension=axis, tiled=True).astype(F32)
-
-
-def small_total(vector, n_dp):
-    for axis, count in (("mp", 8), ("dp", n_dp)):
-        bit = 1
-        while bit < count:
-            vector = vector + lax.ppermute(vector, axis, [(i, i ^ bit) for i in range(count)])
-            bit *= 2
-    return vector
+    return lax.psum_scatter(value.astype(BF), "dp", scatter_dimension=axis, tiled=True)
 
 
 def on_device(tokens, segment, valid, gain_attn, w_query, w_key, w_value, w_out, gain_mlp, w_up, w_down, grad_out):
@@ -940,16 +1034,16 @@
     order = jnp.arange(seq_rows // own_rows, dtype=jnp.int32)
     valid_group = lax.dynamic_slice_in_dim(valid, dp * seq_rows, seq_rows)
     valid_own = lax.dynamic_slice_in_dim(valid_group, me * own_rows, own_rows)
-    row_key = segment[:, None]
-    col_key = jnp.where(valid_group > 0, segment, -1)[None, :]
     tokens32 = tokens.astype(F32)
 
     if cube:
         qkv, normed = project(tokens, gain_attn, w_query, w_key, w_value)
-        mixed, lse, attn_own, normed_mlp, hidden, grad_rows = forward(
-            qkv, grad_out, tokens, w_out, w_up, gain_mlp, row_key, col_key, heads
+        mixed, lse, attn_own, normed_mlp, hidden, grad_pre, grad_rows = forward(
+            qkv, grad_out, tokens, w_out, w_up, w_down, gain_mlp, segment, valid, heads
         )
     else:
+        row_key = segment[:, None]
+        col_key = jnp.where(valid_group > 0, segment, -1)[None, :]
         normed = over_mp(norm_rows(tokens32, gain_attn).astype(BF))
         qkv = jnp.concatenate([dot_nn(normed, w).astype(BF) for w in (w_query, w_key, w_value)], 1)
         mixed, lse = attn_fwd(qkv, order, row_key, col_key, heads, own_rows)
@@ -959,62 +1053,76 @@
         hidden = gelu_fn(dot_nn(normed_mlp, w_up)).astype(BF)
     residual = tokens32 + attn_own
 
-    part_down = dot_tn(hidden, grad_rows).astype(BF)
-    grad_down = sum_dp(part_down, 1)
     if cube:
-        mlp_own, grad_normed, part_up, gain_mlp_part = middle(
-            hidden, w_down, w_up, normed_mlp, after(grad_rows, part_down)
+        part_down = down_weights(hidden, grad_rows)
+        sum_down = sum_dp(part_down, 1)
+        grad_normed, part_up, gain_mlp_part = middle(after(grad_pre, part_down), w_up, normed_mlp)
+        sum_up = sum_dp(part_up, 0)
+        grad_branch, grads_qkv, grad_residual = turn(
+            grad_normed, attn_own, tokens, grad_out, w_out, qkv, mixed, gain_mlp, lse, segment, valid, heads
         )
-        grad_normed, grad_down = lax.optimization_barrier((grad_normed, grad_down))
-        gain_mlp_part = gain_mlp_part[0]
-        grad_up = sum_dp(part_up, 0)
-        grad_branch, grads_qkv, grad_residual = turn(
-            grad_normed, attn_own, tokens, grad_out, w_out, qkv, mixed, gain_mlp, lse, row_key, col_key, heads
+        grads_qkv, sum_down = lax.optimization_barrier((grads_qkv, sum_down))
+        part_last, gain_attn_part = weights(normed, grad_branch, grads_qkv, mixed, w_query, w_key, w_value)
+        grad_down = after(sum_down, part_last).astype(F32)
+        grads_qkv = after(grads_qkv, part_last, grad_down)
+        grad_last = sum_dp(part_last, 0)
+        cols = heads * HD
+        grad_qkv = grad_last[:, :3 * cols].astype(F32)
+        grad_out_proj = jnp.concatenate(
+            [grad_last[i:i + cols, 3 * cols:] for i in range(0, grad_last.shape[0], cols)], 1
+        ).astype(F32)
+        out_tokens, grad_tokens, summed = finish(
+            hidden, w_down, grads_qkv, w_query, w_key, w_value, tokens, attn_own, grad_residual, gain_attn,
+            gain_attn_part, gain_mlp_part, valid
         )
-        part_last, gain_attn_part = weights(normed, grad_branch, grads_qkv, mixed, w_query, w_key, w_value)
-        gain_attn_part = gain_attn_part[0]
-        part_last, grads_qkv, grad_up = lax.optimization_barrier((part_last, grads_qkv, grad_up))
-        grad_last = sum_dp(part_last, 0)
-        grad_qkv, grad_out_proj = grad_last[:, :3 * heads * HD], grad_last[:, 3 * heads * HD:].T
-        grad_normed_attn = finish(grads_qkv, w_query, w_key, w_value)
+        grad_up = after(sum_up, out_tokens).astype(F32)
+        bit = 1
+        while bit < n_dp:
+            if bit == 2:
+                summed, grad_up = lax.optimization_barrier((summed, grad_up))
+            summed = summed + lax.ppermute(summed, "dp", [(i, i ^ bit) for i in range(n_dp)])
+            bit *= 2
     else:
-        grad_hidden = dot_nt(grad_rows, w_down)
-        grad_pre = (gelu_slope(dot_nn(normed_mlp, w_up)) * grad_hidden).astype(BF)
+        grad_down = sum_dp(dot_tn(hidden, grad_rows), 1).astype(F32)
+        grad_pre = (gelu_pair(dot_nn(normed_mlp, w_up))[1] * dot_nt(grad_rows, w_down)).astype(BF)
         part_up = dot_tn(normed_mlp, grad_pre)
-        grad_up = sum_dp(part_up, 0)
+        grad_up = sum_dp(part_up, 0).astype(F32)
         gain_mlp_part = jnp.sum(part_up * w_up.astype(F32), axis=1)
         grad_residual = grad_out.astype(F32) + norm_back(residual, gain_mlp, sum_mp(dot_nt(grad_pre, w_up)))
         grad_branch = over_mp(grad_residual.astype(BF))
         grad_mixed = dot_nt(grad_branch, w_out).astype(BF)
         grads_qkv = jnp.concatenate(attn_bwd(qkv, grad_mixed, mixed, lse, order, row_key, col_key, heads, own_rows), 1)
-        grad_out_proj = sum_dp(dot_tn(mixed, grad_branch), 1)
+        grad_out_proj = sum_dp(dot_tn(mixed, grad_branch), 1).astype(F32)
         part_qkv = dot_tn(normed, grads_qkv)
-        grad_qkv = sum_dp(part_qkv, 0)
+        grad_qkv = sum_dp(part_qkv, 0).astype(F32)
         w_qkv = jnp.concatenate([w_query, w_key, w_value], 1)
         gain_attn_part = jnp.sum(part_qkv * w_qkv.astype(F32), axis=1)
         mlp_own = sum_mp(dot_nn(hidden, w_down))
         grad_normed_attn = sum_mp(dot_nt(grads_qkv, w_qkv))
-    stream = residual + mlp_own
-    mask_own = valid_own.astype(F32)[:, None]
-    grad_tokens = (grad_residual + norm_back(tokens32, gain_attn, grad_normed_attn)).astype(BF)
-
-    squares = jnp.stack([jnp.sum(mask_own * part * part) for part in (stream, attn_own, mlp_own)])
-    small = jnp.concatenate([gain_attn_part / gain_attn, gain_mlp_part / gain_mlp, squares])
-    summed = small_total(small, n_dp) if cube else lax.psum(small, ("dp", "mp"))
+        stream = residual + mlp_own
+        out_tokens = stream.astype(BF)
+        grad_tokens = (grad_residual + norm_back(tokens32, gain_attn, grad_normed_attn)).astype(BF)
+        mask_own = valid_own.astype(F32)[:, None]
+        squares = [jnp.sum(mask_own * part * part, axis=0) for part in (stream, attn_own, mlp_own)]
+        summed = lax.psum(jnp.stack([gain_attn_part, gain_mlp_part, *squares]), ("dp", "mp"))
     counted = jnp.maximum(jnp.sum(valid).astype(F32) * width, 1.0)
     gain_rows = width // (n_dp * n_mp)
     place = (dp * n_mp + me) * gain_rows
-    rms = jnp.sqrt(summed[2 * width:] / counted)
+    rms = jnp.sqrt(jnp.sum(summed[2:5], axis=1) / counted)
+    gains = [
+        lax.dynamic_slice_in_dim(summed[k], place, gain_rows) / lax.dynamic_slice_in_dim(gain, place, gain_rows)
+        for k, gain in enumerate((gain_attn, gain_mlp))
+    ]
     shard = heads * HD
     return (
-        stream.astype(BF),
+        out_tokens,
         grad_tokens,
-        lax.dynamic_slice_in_dim(summed[:width], place, gain_rows),
+        gains[0],
         grad_qkv[:, :shard],
         grad_qkv[:, shard:2 * shard],
         grad_qkv[:, 2 * shard:],
         grad_out_proj,
-        lax.dynamic_slice_in_dim(summed[width:2 * width], place, gain_rows),
+        gains[1],
         grad_up,
         grad_down,
         rms[0],

time: 476 us -> 458 us (0.962)
  Pallas kernels: 397 us -> 412 us
  matrix products: 14.4 us -> 0 us
  other arithmetic: 16.5 us -> 9.63 us
  waiting for transfers between devices: 8.07 us -> 2.67 us
    pallas_call x2 -> x3, Pallas kernels: 145 us -> 162 us  [the longest x1 92.6 us: finish(): pl.pallas_call(finish_body, name='last_scatters', in_specs=[hbm] * 9 + [v...]
    dot_general x1 -> x0, matrix products: 14.4 us -> none  [dot_tn(): lax.dot_general(a, b, (((0,), (0,)), ((), ())), preferred_element_type=F32)]
    reduce_sum x2 -> x1, other arithmetic: 5.63 us -> 0.13 us  [on_device(): rms = jnp.sqrt(jnp.sum(summed[2:5], axis=1) / counted)]
    ppermute x5 -> x2, waiting for transfers between devices: 7.98 us -> 2.59 us  [on_device(): lax.ppermute(summed, 'dp', [(i, i ^ bit) for i in range(n_dp)])]
  transfers between devices with their start and end apart: 8 -> 5, of which waited for: 3 -> 2; matrix products, arithmetic and copies ran while one was open for 3% -> 2% of each run, Pallas kernels for 49% -> 51%
where the time goes in v4:
time: 458 us; the launch traced here: 449 us
  Pallas kernels  412 us (90%)
  between operations  14.9 us (3%)
  other arithmetic  9.63 us (2%)
  local copies, waits for them, and re-layouts  5.93 us (1%)
    pallas_call x1, Pallas kernels, forward(): pl.pallas_call(functools.partial(forward_body, heads), name='forward_laye...  123 us
    pallas_call x1, Pallas kernels, finish(): pl.pallas_call(finish_body, name='last_scatters', in_specs=[hbm] * 9 + [v...  92.6 us
    pallas_call x1, Pallas kernels, turn(): pl.pallas_call(functools.partial(turn_body, heads), name='turn_layer', in...  64.7 us
    pallas_call x1, Pallas kernels, middle(): pl.pallas_call(middle_body, name='middle_layer', in_specs=[hbm] * 3, out_...  55.6 us
    pallas_call x1, Pallas kernels, project(): pl.pallas_call(project_body, name='gather_project', in_specs=[hbm, pl.Blo...  44.5 us
    pallas_call x1, Pallas kernels, weights(): pl.pallas_call(weights_body, name='weight_gradients', grid=(width // tile...  17.8 us
    pallas_call x1, Pallas kernels, down_weights(): pl.pallas_call(down_body, name='down_weights', grid=(width // tile,), in_...  13.4 us
  transfers between devices with their start and end apart: 5, of which 2 were waited for; matrix products, arithmetic and copies ran while one was open for 2% of the time, Pallas kernels for 51%

profile of v4, /device:TPU:0, one launch (start us, length us, event | category | flops | bytes accessed | tf_op | source)
XLA Modules:
  0.0 449.1 jit_solution(4027598418598597877)
XLA Ops:
  7.2 0.0 reduce-scatter.4.cloned.1.call-start
  7.2 44.5 %gather_project.1 = (bf16[2048,768]{1,0:T(8,128)(2,1)}, bf16[2048,2048]{1,0:T(8,128)(2,1)}) custom-call(bf16[256,2048]{1,0:T(8,128)(2,1)} %tok_hbm.7, f32[1,2048]{1,0:T(1,128)} %bitcast.14, bf16[2048,256]{1,0:T(8,128)(2,1)} %wq_hbm.3, bf16[2048,256]{1,0:T(8,128)(2,1)} %wk_hbm.3, bf16[2048,256]{1,0:T(8,128)(2,1)} %wv_hbm.3), custom_call_target="tpu_custom_call" | custom-call | flops 6442450944 | bytes 62914560 | tf_op jit(solution)/shard_map/gather_project/pallas_call | solution.py:340
  51.8 122.9 %forward_layer.1 = (bf16[2048,256]{1,0:T(8,128)(2,1)}, f32[2,2048,1]{2,1,0:T(8,128)}, f32[256,2048]{1,0:T(8,128)}, bf16[2048,2048]{1,0:T(8,128)(2,1)}, bf16[2048...) custom-call(bf16[2048,768]{1,0:T(8,128)(2,1)} %get-tuple-element.41.qkv_hbm, ...), custom_call_target="tpu_custom_call" | custom-call | flops 40000000000 | bytes 262144000 | tf_op jit(solution)/shard_map/forward_layer/pallas_call | solution.py:625
  174.7 13.4 %down_weights.1 = bf16[1024,2048]{1,0:T(8,128)(2,1)} custom-call(bf16[2048,1024]{1,0:T(8,128)(2,1)} %get-tuple-element.42.hidden_ref.hidden_hbm, bf16[2048,2048]{1,0:T(8,128)(2,1)} %get-tuple-element.44.grad_ref), custom_call_target="tpu_custom_call" | custom-call | flops 8589934592 | bytes 16777216 | tf_op jit(solution)/shard_map/down_weights/pallas_call | solution.py:860
  188.1 0.0 reduce-scatter.4.cloned.1.call-update
  188.1 0.0 reduce-scatter.6.cloned.1.call-start
  188.2 55.6 %middle_layer.1 = (f32[256,2048]{1,0:T(8,128)}, bf16[2048,1024]{1,0:T(8,128)(2,1)}, f32[1,2048]{1,0:T(1,128)}) custom-call(bf16[2048,1024]{1,0:T(8,128)(2,1)} %get-tuple-element.45.pre_hbm, bf16[2048,1024]{1,0:T(8,128)(2,1)} %w_up_hbm.3, bf16[2048,2048]{1,0:T(8,128)(2,1)} %get-tuple-element.46.normed_hbm), custom_call_target="tpu_custom_call" | custom-call | flops 44999999488 | bytes 209715200 | tf_op jit(solution)/shard_map/middle_layer/pallas_call | solution.py:724
  243.7 0.0 reduce-scatter.6.cloned.1.call-update
  243.8 0.0 reduce-scatter.8.cloned.1.call-start
  243.8 64.7 %turn_layer.1 = (bf16[2048,2048]{1,0:T(8,128)(2,1)}, bf16[2048,768]{1,0:T(8,128)(2,1)}, f32[256,2048]{1,0:T(8,128)}) custom-call(f32[256,2048]{1,0:T(8,128)} %get-tuple-element.47.dnorm_hbm, f32[256,2048]{1,0:T(8,128)} %get-tuple-element.48.attn_hbm, bf16[256,2048]{1,0:T(8,128)(2,1)} %tok_hbm.7, bf16[256,2048]{1,0:T(8,128)(2,1)} %grad_hbm.3, ...), custom_call_target="tpu_custom_call" | custom-call | flops 44999999488 | bytes 209715200 | tf_op jit(solution)/shard_map/turn_layer/pallas_call | solution.py:823
  308.5 0.0 reduce-scatter.4.cloned.1.call-done
  308.5 17.8 %weight_gradients.1 = (bf16[2048,1024]{1,0:T(8,128)(2,1)}, f32[1,2048]{1,0:T(1,128)}) custom-call(bf16[2048,2048]{1,0:T(8,128)(2,1)} %get-tuple-element.53.normed_ref, bf16[2048,2048]{1,0:T(8,128)(2,1)} %get-tuple-element.54.branch_ref, bf16[2048,768]{1,0:T(8,128)(2,1)} %get-tuple-element.58.dqkv_ref.dqkv_hbm, ...), custom_call_target="tpu_custom_call" | custom-call | flops 8589934592 | bytes 31457280 | tf_op jit(solution)/shard_map/weight_gradients/pallas_call | solution.py:877
  326.3 0.0 copy-start
  326.3 0.0 reduce-scatter.8.cloned.1.call-update
  326.3 1.2 copy-done
  327.5 1.6 convert_element_type.15
  329.1 0.0 copy-start.3
  329.1 92.6 %last_scatters.1 = (bf16[256,2048]{1,0:T(8,128)(2,1)}, bf16[256,2048]{1,0:T(8,128)(2,1)}, f32[8,2048]{1,0:T(8,128)}) custom-call(bf16[2048,1024]{1,0:T(8,128)(2,1)} %get-tuple-element.42.hidden_ref.hidden_hbm, bf16[1024,2048]{1,0:T(8,128)(2,1)} %w_down_hbm.3, bf16[2048,768]{1,0:T(8,128)(2,1)} %get-tuple-element.58.dqkv_ref.dqkv_hbm, ...), custom_call_target="tpu_custom_call" | custom-call | flops 30000001024 | bytes 209715200 | tf_op jit(solution)/shard_map/last_scatters/pallas_call | solution.py:992
  421.8 1.6 collective-permute-start
  423.4 0.0 reduce-scatter.6.cloned.1.call-done
  423.4 2.8 convert_element_type.16
  426.2 0.0 copy-start.2
  426.2 0.1 collective-permute-done
  426.3 0.9 add.21
  427.3 2.7 collective-permute-start.1
  429.9 0.0 copy-done.3
  429.9 0.6 reduce_sum.19
  431.2 2.5 collective-permute-done.1
  433.7 1.3 bitcast_divide_fusion
  435.0 0.1 slice_reduce_fusion
  435.2 0.6 fusion.3
  435.8 0.0 copy-start.1
  435.8 0.0 reduce-scatter.8.cloned.1.call-done
  435.8 1.3 slice_convert_fusion
  437.1 1.2 fusion
  438.3 1.0 fusion.1
  439.3 0.9 maximum_convert_fusion
  440.1 0.0 copy-done.2
  440.1 1.0 copy.27
  441.1 0.0 copy-done.1
  441.1 1.0 copy.28
  (3 shorter events, 0.0 us)
Async XLA Ops:
  7.2 301.3 %reduce-scatter.4.cloned.1.call-start = ((), (), s32[]{:S(2)}) async-start(), calls=%async_computation.3 | async-start | bytes 5242880 | tf_op jit(solution)/shard_map/reduce_scatter | solution.py:1024
  188.1 235.3 %reduce-scatter.6.cloned.1.call-start = ((), (), s32[]{:S(2)}) async-start(), calls=%async_computation.4 | async-start | bytes 5242880 | tf_op jit(solution)/shard_map/reduce_scatter | solution.py:1024
  243.8 192.0 %reduce-scatter.8.cloned.1.call-start = ((), (), s32[]{:S(2)}) async-start(), calls=%async_computation.5 | async-start | bytes 5242880 | tf_op jit(solution)/shard_map/reduce_scatter | solution.py:1024
  326.3 1.2 copy-start
  329.1 100.8 %copy-start.3 = (s32[8192]{0:T(1024)S(1)}, s32[8192]{0:T(1024)}, u32[]{:S(2)}) copy-start(s32[8192]{0:T(1024)} %param.14) | copy-start | bytes 98308
  421.8 4.5 %collective-permute-start = (f32[8,2048]{1,0:T(8,128)}, f32[8,2048]{1,0:T(8,128)S(1)}, u32[]{:S(2)}, u32[]{:S(2)}) collective-permute-start(f32[8,2048]{1,0:T(8,128)} %get-tuple-element.64), channel_id=1, source_target_pairs={{0,8},{8,0},{16,24},{24,16},{1,9},{9,1},{17,25},{25,17},{2,10},{10... | collective-permute-start | bytes 196616 | tf_op jit(solution)/shard_map/ppermute | solution.py:1083
  426.2 13.9 %copy-start.2 = (bf16[256,2048]{1,0:T(8,128)(2,1)S(1)}, bf16[256,2048]{1,0:T(8,128)(2,1)}, u32[]{:S(2)}) copy-start(bf16[256,2048]{1,0:T(8,128)(2,1)} %get-tuple-element.94) | copy-start | bytes 3145732
  427.3 6.4 %collective-permute-start.1 = (f32[8,2048]{1,0:T(8,128)S(1)}, f32[8,2048]{1,0:T(8,128)S(1)}, u32[]{:S(2)}, u32[]{:S(2)}) collective-permute-start(f32[8,2048]{1,0:T(8,128)S(1)} %add.21), channel_id=1, source_target_pairs={{0,16},{8,24},{16,0},{24,8},{1,17},{9,25},{17,1},{25,9},{2,18},{10... | collective-permute-start | bytes 196616 | tf_op jit(solution)/shard_map/ppermute | solution.py:1083
  435.8 5.3 %copy-start.1 = (bf16[256,2048]{1,0:T(8,128)(2,1)S(1)}, bf16[256,2048]{1,0:T(8,128)(2,1)}, u32[]{:S(2)}) copy-start(bf16[256,2048]{1,0:T(8,128)(2,1)} %get-tuple-element.95) | copy-start | bytes 3145732
Sparse Core Ops, SparseCore 0:
  188.2 76.7 reduce-scatter.3
  267.4 77.2 reduce-scatter.5
  347.0 77.3 reduce-scatter.7
